TPU v7x, 128 devices: a whole 4x4x4 slice. The times are simulated.
128 devices in a mesh: wide: 16 (over z, x), narrow: 8 (over y, core).
Axes of the slice: x: 4, y: 4, z: 4, core: 2. Of those that a mesh axis runs over, the one named last changes fastest.
Arguments:
- design: float32 [262144, 128], P(('wide', 'narrow')), may hold values from 0.05 to 1
- filter_tiles: float32 [5, 128, 128], replicated
- filter_cols: int32 [262144, 5], P(('wide', 'narrow')), may hold values from -1 to 262143, as said below
- slot_block: int32 [262144], P(('wide', 'narrow')), may hold values from 0 to 262143, as said below
- holes: int32 [2048, 16384], P('wide', 'narrow'), may hold values 0 or 1
- squeeze_source: float32 [2048, 16384], P('wide', 'narrow'), may hold values from -6 to 6
- force_weight: float32 [2048, 16384], P('wide', 'narrow'), may hold values from 0.2 to 2
Outputs:
- pressure: float32 [2048, 16384], P('wide', 'narrow')
- sensitivity: float32 [262144, 128], P(('wide', 'narrow'))
Inputs may be any that keep to these rules, and one draw needn't show every extreme that they name: `slot_block`: film blocks are ordered along a curve that visits the tiles in order and, inside a tile of 16 x 128 blocks, the blocks in Morton order (column bit lowest); for one stagger h with 512 <= h <= 1536, design slot s controls the block at curve position (s + h) mod 262144. So the slots of owner d (slots d * 2048 to (d + 1) * 2048 - 1) lie in tiles d and d + 1, those of the last owner in its own tile and tile 0. filter_cols[r, 0] = r; entries 1 to 4 are the design slots of the film blocks above, below, left and right of the block of slot r inside the same tile, -1 where that neighbour lies outside the tile.
All inputs are finite; a program needn't handle non-finite values. No bound on the sum of `holes` on one device may be relied on, other than what follows from the above.
Results may differ from a plain program's by a relative error of at most 0.00025.
Values sent between devices are 32-bit elements; how exact they have to be, the bound alone decides.
No kernel may reach another device: no remote copies, remote signals or barrier semaphores. Data moves between devices by JAX's collectives and lax.ppermute only.
A program may use at most 192 MiB of HBM per device.

v0:
```python
import jax
import jax.numpy as jnp
from jax import lax
from jax.sharding import PartitionSpec as P

SWEEPS = 16


COND_FLOOR = 0.01
SQUEEZE_DAMPING = 0.25
FULL_PRECISION = lax.Precision.HIGHEST


def extended_2(x, sides, width, wrap):
    for axis, dim in sides:
        size, length = (lax.axis_size(axis), x.shape[dim])
        up = [(i, (i + 1) % size) for i in range(size if wrap else size - 1)]
        down = [(j, i) for i, j in up]
        last = lax.slice_in_dim(x, length - width, length, axis=dim)
        first = lax.slice_in_dim(x, 0, width, axis=dim)
        before = lax.ppermute(last, axis, up)
        after = lax.ppermute(first, axis, down)
        x = jnp.concatenate([before, x, after], axis=dim)
    return x


def passed_along(x, axis, by):
    length = lax.axis_size(axis)
    return lax.ppermute(x, axis, [(i, (i + by) % length) for i in range(length)])


def relax(fields, conduct, sources, solid_mask, rim_depth, outer_rim):
    offset = outer_rim - rim_depth + 1
    inner_rows = fields.shape[1] - 2
    inner_cols = fields.shape[2] - 2

    def window(values, row_step, col_step):
        return values[
            ...,
            offset + row_step : offset + row_step + inner_rows,
            offset + col_step : offset + col_step + inner_cols,
        ]

    k_here = window(conduct, 0, 0)
    face_north = 0.5 * (k_here + window(conduct, -1, 0))
    face_south = 0.5 * (k_here + window(conduct, 1, 0))
    face_west = 0.5 * (k_here + window(conduct, 0, -1))
    face_east = 0.5 * (k_here + window(conduct, 0, 1))
    coupled = face_north * fields[:, 0:inner_rows, 1 : inner_cols + 1]
    coupled = coupled + face_south * fields[:, 2 : inner_rows + 2, 1 : inner_cols + 1]
    coupled = coupled + face_west * fields[:, 1 : inner_rows + 1, 0:inner_cols]
    coupled = coupled + face_east * fields[:, 1 : inner_rows + 1, 2 : inner_cols + 2]
    diagonal = face_north + face_south + face_west + face_east + SQUEEZE_DAMPING
    return (window(sources, 0, 0) + coupled) / diagonal * window(solid_mask, 0, 0)


def film_gradient(padded, density):
    row_count = padded.shape[1] - 2
    col_count = padded.shape[2] - 2
    p_here = padded[0, 1 : row_count + 1, 1 : col_count + 1]
    a_here = padded[1, 1 : row_count + 1, 1 : col_count + 1]
    summed = jnp.zeros((row_count, col_count), jnp.float32)
    for row_start, col_start in ((0, 1), (2, 1), (1, 0), (1, 2)):
        nearby = padded[:, row_start : row_start + row_count, col_start : col_start + col_count]
        summed = summed + (a_here - nearby[1]) * (p_here - nearby[0])
    return -0.5 * summed * (3.0 * (1.0 - COND_FLOOR)) * density * density


def to_tile(blocks, row_count, col_count):
    shaped = blocks.reshape(row_count // 8, col_count // 16, 8, 16)
    return shaped.transpose(0, 2, 1, 3).reshape(row_count, col_count)


def to_blocks(tile):
    row_count, col_count = tile.shape
    shaped = tile.reshape(row_count // 8, 8, col_count // 16, 16)
    return shaped.transpose(0, 2, 1, 3).reshape(-1, 128)


def local(design, filter_tiles, filter_cols, slot_block, holes, squeeze_source, force_weight):
    owned = design.shape[0]
    owners = lax.axis_size(("wide", "narrow"))
    total_slots = owned * owners
    first_slot = lax.axis_index(("wide", "narrow")) * owned
    extended = extended_2(design, ((("wide", "narrow"), 0),), owned, True)
    present = filter_cols >= 0
    local_rows = jnp.where(present, jnp.mod(filter_cols - first_slot + owned, total_slots), 0)
    picked = jnp.where(present[:, :, None], extended[local_rows], 0.0)
    numer = jnp.einsum("rkj,kij->ri", picked, filter_tiles, precision=FULL_PRECISION)
    denom = jnp.dot(
        present.astype(jnp.float32), jnp.sum(filter_tiles, axis=2), precision=FULL_PRECISION
    )
    filtered = numer / denom
    relative = jnp.mod(slot_block - first_slot, total_slots)
    in_own = relative < owned
    own_index = jnp.where(in_own, relative, owned)
    next_index = jnp.where(in_own, owned, relative - owned)
    own_blocks = jnp.zeros((owned + 1, 128), jnp.float32).at[own_index].set(filtered)[:owned]
    next_blocks = jnp.zeros((owned + 1, 128), jnp.float32).at[next_index].set(filtered)[:owned]
    arrived = passed_along(next_blocks, ("wide", "narrow"), 1)
    row_count, col_count = holes.shape
    density = to_tile(own_blocks + arrived, row_count, col_count)
    conduct = COND_FLOOR + (1.0 - COND_FLOOR) * density * density * density
    solid_mask = jnp.where(holes > 0, 0.0, 1.0).astype(jnp.float32)
    statics = jnp.stack([conduct, squeeze_source, force_weight, solid_mask])
    initial = jnp.zeros((2, row_count, col_count), jnp.float32)
    grown_static = extended_2(statics, (("wide", 1), ("narrow", 2)), 1, False)

    def single_sweep(sweep_index, fields):
        grown = extended_2(fields, (("wide", 1), ("narrow", 2)), 1, False)
        return relax(grown, grown_static[0], grown_static[1:3], grown_static[3], 1, 1)

    fields = lax.fori_loop(0, SWEEPS, single_sweep, initial)
    padded_final = extended_2(fields, (("wide", 1), ("narrow", 2)), 1, False)
    film_sens = film_gradient(padded_final, density)
    tile_sens = to_blocks(film_sens)
    next_sens = passed_along(tile_sens, ("wide", "narrow"), -1)
    returned = jnp.concatenate([tile_sens, next_sens], axis=0)[relative]
    scaled = returned / denom
    spread = jnp.einsum("ri,kij->rkj", scaled, filter_tiles, precision=FULL_PRECISION)
    spread = jnp.where(present[:, :, None], spread, 0.0)
    collected = jnp.zeros((3 * owned, 128), jnp.float32).at[local_rows].add(spread)
    from_next = passed_along(collected[:owned], ("wide", "narrow"), -1)
    from_prev = passed_along(collected[2 * owned :], ("wide", "narrow"), 1)
    sensitivity = collected[owned : 2 * owned] + from_next + from_prev
    return (fields[0], sensitivity)


def solution(mesh):
    placed = (
        P(("wide", "narrow"), None),
        P(),
        P(("wide", "narrow"), None),
        P(("wide", "narrow")),
        P("wide", "narrow"),
        P("wide", "narrow"),
        P("wide", "narrow"),
    )
    return jax.shard_map(
        local,
        mesh=mesh,
        in_specs=placed,
        out_specs=(P("wide", "narrow"), P(("wide", "narrow"), None)),
        check_vma=False,
    )
```

profile of v0, /device:TPU:64, one launch (start us, length us, event | category | flops | bytes accessed | tf_op | source)
XLA Modules:
  0.0 792.5 jit_solution(1770991304085182190)
XLA Ops:
  0.7 5.9 collective-permute-start.5
  10.9 8.5 %collective-permute-done.4 = f32[2048,128]{1,0:T(8,128)S(1)} collective-permute-done((f32[2048,128]{1,0:T(8,128)}, f32[2048,128]{1,0:T(8,128)S(1)}, u32[]{:S(2)}, u32[]{:S(2)}) %collective-permute-start.4) | collective-permute-done | bytes 1048608 | tf_op jit(solution)/shard_map/ppermute | solution.py:21
  22.4 34.5 %gather_fusion = f32[10240,128]{1,0:T(8,128)} fusion(f32[6144,128]{1,0:T(8,128)S(1)} %pad_maximum_fusion.12, s32[10240]{0:T(1024)S(1)} %broadcast_clamp_fusion), kind=kCustom, calls=%fused_computation | custom fusion | bytes 10526720 | tf_op jit(solution)/shard_map/gather | solution.py:88
  56.9 7.4 reshape.83
  64.3 8.6 %fusion.14 = f32[2048,128]{1,0:T(8,128)} fusion(f32[2048,128]{1,0:T(8,128)S(1)} %copy-done.11, f32[5,128,128]{2,1,0:T(8,128)S(1)} %copy-done, f32[2048,5,128]{2,1,0:T(8,128)} %reshape.83, pred[2048,5]{0,1:T(8,128)(4,1)S(1)} %get-tuple-element.85), kind=kOutput, calls=%fused_computation.42 | convolution fusion | flops 2014838784 | bytes 7677952 | tf_op jit(solution)/shard_map/rkj,kij->ri/dot_general | solution.py:89
  72.9 6.3 scatter_custom_fusion.1
  80.4 6.2 scatter_custom_fusion
  86.6 12.4 %collective-permute-done.6 = f32[2048,128]{1,0:T(8,128)} collective-permute-done((f32[2048,128]{1,0:T(8,128)}, f32[2048,128]{1,0:T(8,128)}, u32[]{:S(2)}, u32[]{:S(2)}) %collective-permute-start.6) | collective-permute-done | bytes 1048608 | tf_op jit(solution)/shard_map/ppermute | solution.py:29
  100.9 4.7 copy.21
  105.5 7.9 reshape.77
  116.9 6.2 collective-permute-start.8
  133.3 6.7 concatenate.51
  144.5 468.9 %while.12 = (s32[]{:T(128)}, f32[2,128,2048]{2,1,0:T(8,128)}, f32[4,130,2050]{2,1,0:T(8,128)}, f32[128,2048]{1,0:T(8,128)}, f32[128,2048]{1,0:T(8,128)}, /*index...) while((s32[]{:T(128)}, f32[2,128,2048]{2,1,0:T(8,128)}, ...), condition=%wide.region_4.5_spmd.clone, body=%wide.region_3.4_spmd.clone.sunk | while | flops 12059667 | bytes 57981584 | solution.py:113
  144.7 6.3 collective-permute-start
  160.8 4.1 collective-permute-start.3
  169.2 6.6 fusion.53
  177.6 3.7 collective-permute-start
  191.1 4.2 collective-permute-start.3
  199.6 6.6 fusion.53
  207.9 3.7 collective-permute-start
  229.4 6.6 fusion.53
  258.5 6.6 fusion.53
  287.5 6.6 fusion.53
  316.5 6.6 fusion.53
  345.6 6.6 fusion.53
  374.6 6.6 fusion.53
  403.6 6.6 fusion.53
  432.6 6.6 fusion.53
  461.7 6.6 fusion.53
  490.7 6.6 fusion.53
  519.7 6.6 fusion.53
  548.8 6.6 fusion.53
  577.8 6.6 fusion.53
  606.8 6.6 fusion.53
  616.4 6.0 collective-permute-start.12
  631.5 4.3 fusion.22
  635.8 4.9 reshape.81
  640.7 6.1 copy.22
  649.8 5.9 collective-permute-start.15
  655.7 12.6 %collective-permute-done.15 = f32[2048,128]{1,0:T(8,128)S(1)} collective-permute-done((f32[2048,128]{1,0:T(8,128)}, f32[2048,128]{1,0:T(8,128)S(1)}, u32[]{:S(2)}, u32[]{:S(2)}) %collective-permute-start.15) | collective-permute-done | bytes 1048608 | tf_op jit(solution)/shard_map/ppermute | solution.py:29
  671.1 9.3 %gather_fusion.1 = f32[2048,128]{1,0:T(8,128)} fusion(f32[4096,128]{1,0:T(8,128)} %pad_maximum_fusion.13, s32[2048]{0:T(1024)S(1)} %get-tuple-element.109), kind=kCustom, calls=%fused_computation.1 | custom fusion | bytes 2105344 | tf_op jit(solution)/shard_map/gather | solution.py:118
  680.4 5.8 convolution_select_fusion
  686.3 12.9 %copy.25 = f32[2048,5,128]{2,1,0:T(8,128)} copy(f32[2048,5,128]{2,0,1:T(8,128)S(1)} %convolution_select_fusion) | data formatting | bytes 10485760 | tf_op jit(solution)/shard_map/jit(_where)/select_n | solution.py:121
  699.1 7.9 %reshape.118 = f32[10240,128]{1,0:T(8,128)} reshape(f32[2048,5,128]{2,1,0:T(8,128)} %copy.25) | data formatting | bytes 10485760 | tf_op jit(solution)/shard_map/jit(_where)/select_n | solution.py:121
  707.0 56.9 %scatter_custom_fusion.2 = f32[6144,128]{1,0:T(8,128)} fusion(s32[10240]{0:T(1024)} %copy-done.17, f32[10240,128]{1,0:T(8,128)} %reshape.118, f32[]{:T(128)} %constant.31.clone.1), kind=kCustom, calls=%fused_computation.44 | custom fusion | flops 1310720 | bytes 3146240 | tf_op jit(solution)/shard_map/scatter-add | solution.py:122
  765.6 6.1 collective-permute-start.16
  772.8 11.3 %collective-permute-done.16 = f32[2048,128]{1,0:T(8,128)S(1)} collective-permute-done((f32[2048,128]{1,0:T(8,128)S(1)}, f32[2048,128]{1,0:T(8,128)S(1)}, u32[]{:S(2)}, u32[]{:S(2)}) %collective-permute-start.16) | collective-permute-done | bytes 1048608 | tf_op jit(solution)/shard_map/ppermute | solution.py:29
  784.0 6.1 collective-permute-done.17
  (488 shorter events, 391.4 us)
Async XLA Ops:
  0.7 18.7 %collective-permute-start.4 = (f32[2048,128]{1,0:T(8,128)}, f32[2048,128]{1,0:T(8,128)S(1)}, u32[]{:S(2)}, u32[]{:S(2)}) collective-permute-start(f32[2048,128]{1,0:T(8,128)} %param.9), channel_id=1, source_target_pairs={{0,1},{1,2},{2,3},{3,4},{4,5},{5,6},{6,7},{7,8},{8,9},{9,10},{10,1... | collective-permute-start | bytes 3145736 | tf_op jit(solution)/shard_map/ppermute | solution.py:21
  0.7 19.6 %collective-permute-start.5 = (f32[2048,128]{1,0:T(8,128)}, f32[2048,128]{1,0:T(8,128)}, u32[]{:S(2)}, u32[]{:S(2)}) collective-permute-start(f32[2048,128]{1,0:T(8,128)} %param.9), channel_id=1, source_target_pairs={{1,0},{2,1},{3,2},{4,3},{5,4},{6,5},{7,6},{8,7},{9,8},{10,9},{11,1... | collective-permute-start | bytes 3145736 | tf_op jit(solution)/shard_map/ppermute | solution.py:22
  80.2 18.8 %collective-permute-start.6 = (f32[2048,128]{1,0:T(8,128)}, f32[2048,128]{1,0:T(8,128)}, u32[]{:S(2)}, u32[]{:S(2)}) collective-permute-start(f32[2048,128]{1,0:T(8,128)} %slice.214), channel_id=1, source_target_pairs={{0,1},{1,2},{2,3},{3,4},{4,5},{5,6},{6,7},{7,8},{8,9},{9,10},{10,1... | collective-permute-start | bytes 3145736 | tf_op jit(solution)/shard_map/ppermute | solution.py:29
  115.0 8.2 %collective-permute-start.7 = (f32[4,1,2048]{2,1,0:T(1,128)S(1)}, f32[4,1,2048]{2,1,0:T(1,128)S(1)}, u32[]{:S(2)}, u32[]{:S(2)}) collective-permute-start(f32[4,1,2048]{2,1,0:T(1,128)S(1)} %get-tuple-element.97), channel_id=1, source_target_pairs={{0,8},{8,16},{16,24},{24,32},{32,40},{40,48},{48,56},{56,64},{64,7... | collective-permute-start | bytes 98312 | tf_op jit(solution)/shard_map/ppermute | solution.py:21
  144.7 10.9 %collective-permute-start = (f32[2,1,2048]{2,1,0:T(1,128)S(1)}, f32[2,1,2048]{2,1,0:T(1,128)S(1)}, u32[]{:S(2)}, u32[]{:S(2)}) collective-permute-start(f32[2,1,2048]{2,1,0:T(1,128)S(1)} %get-tuple-element.164), channel_id=1, source_target_pairs={{8,0},{16,8},{24,16},{32,24},{40,32},{48,40},{56,48},{64,56},{72,6... | collective-permute-start | bytes 49160 | tf_op jit(solution)/shard_map/while/body/eval_jaxpr/ppermute | solution.py:22
  159.5 9.5 %collective-permute-start.2 = (f32[2,130,1]{2,1,0:T(8,128)}, f32[2,130,1]{2,1,0:T(8,128)}, u32[]{:S(2)}, u32[]{:S(2)}) collective-permute-start(f32[2,130,1]{2,1,0:T(8,128)} %get-tuple-element.166), channel_id=1, source_target_pairs={{1,0},{2,1},{3,2},{4,3},{5,4},{6,5},{7,6},{9,8},{10,9},{11,10},{12... | collective-permute-start | bytes 3128 | tf_op jit(solution)/shard_map/while/body/eval_jaxpr/ppermute | solution.py:22
  160.8 8.3 %collective-permute-start.3 = (f32[2,130,1]{2,1,0:T(8,128)}, f32[2,130,1]{2,1,0:T(8,128)}, u32[]{:S(2)}, u32[]{:S(2)}) collective-permute-start(f32[2,130,1]{2,1,0:T(8,128)} %get-tuple-element.167), channel_id=1, source_target_pairs={{0,1},{1,2},{2,3},{3,4},{4,5},{5,6},{6,7},{8,9},{9,10},{10,11},{11... | collective-permute-start | bytes 3128 | tf_op jit(solution)/shard_map/while/body/eval_jaxpr/ppermute | solution.py:21
  177.6 8.5 %collective-permute-start = (f32[2,1,2048]{2,1,0:T(1,128)S(1)}, f32[2,1,2048]{2,1,0:T(1,128)S(1)}, u32[]{:S(2)}, u32[]{:S(2)}) collective-permute-start(f32[2,1,2048]{2,1,0:T(1,128)S(1)} %get-tuple-element.164), channel_id=1, source_target_pairs={{8,0},{16,8},{24,16},{32,24},{40,32},{48,40},{56,48},{64,56},{72,6... | collective-permute-start | bytes 49160 | tf_op jit(solution)/shard_map/while/body/eval_jaxpr/ppermute | solution.py:22
  189.8 9.6 %collective-permute-start.2 = (f32[2,130,1]{2,1,0:T(8,128)}, f32[2,130,1]{2,1,0:T(8,128)}, u32[]{:S(2)}, u32[]{:S(2)}) collective-permute-start(f32[2,130,1]{2,1,0:T(8,128)} %get-tuple-element.166), channel_id=1, source_target_pairs={{1,0},{2,1},{3,2},{4,3},{5,4},{6,5},{7,6},{9,8},{10,9},{11,10},{12... | collective-permute-start | bytes 3128 | tf_op jit(solution)/shard_map/while/body/eval_jaxpr/ppermute | solution.py:22
  191.1 8.4 %collective-permute-start.3 = (f32[2,130,1]{2,1,0:T(8,128)}, f32[2,130,1]{2,1,0:T(8,128)}, u32[]{:S(2)}, u32[]{:S(2)}) collective-permute-start(f32[2,130,1]{2,1,0:T(8,128)} %get-tuple-element.167), channel_id=1, source_target_pairs={{0,1},{1,2},{2,3},{3,4},{4,5},{5,6},{6,7},{8,9},{9,10},{10,11},{11... | collective-permute-start | bytes 3128 | tf_op jit(solution)/shard_map/while/body/eval_jaxpr/ppermute | solution.py:21
  207.9 8.5 %collective-permute-start = (f32[2,1,2048]{2,1,0:T(1,128)S(1)}, f32[2,1,2048]{2,1,0:T(1,128)S(1)}, u32[]{:S(2)}, u32[]{:S(2)}) collective-permute-start(f32[2,1,2048]{2,1,0:T(1,128)S(1)} %get-tuple-element.164), channel_id=1, source_target_pairs={{8,0},{16,8},{24,16},{32,24},{40,32},{48,40},{56,48},{64,56},{72,6... | collective-permute-start | bytes 49160 | tf_op jit(solution)/shard_map/while/body/eval_jaxpr/ppermute | solution.py:22
  220.2 9.2 %collective-permute-start.2 = (f32[2,130,1]{2,1,0:T(8,128)}, f32[2,130,1]{2,1,0:T(8,128)}, u32[]{:S(2)}, u32[]{:S(2)}) collective-permute-start(f32[2,130,1]{2,1,0:T(8,128)} %get-tuple-element.166), channel_id=1, source_target_pairs={{1,0},{2,1},{3,2},{4,3},{5,4},{6,5},{7,6},{9,8},{10,9},{11,10},{12... | collective-permute-start | bytes 3128 | tf_op jit(solution)/shard_map/while/body/eval_jaxpr/ppermute | solution.py:22
  221.4 7.9 collective-permute-start.3
  237.8 8.5 %collective-permute-start = (f32[2,1,2048]{2,1,0:T(1,128)S(1)}, f32[2,1,2048]{2,1,0:T(1,128)S(1)}, u32[]{:S(2)}, u32[]{:S(2)}) collective-permute-start(f32[2,1,2048]{2,1,0:T(1,128)S(1)} %get-tuple-element.164), channel_id=1, source_target_pairs={{8,0},{16,8},{24,16},{32,24},{40,32},{48,40},{56,48},{64,56},{72,6... | collective-permute-start | bytes 49160 | tf_op jit(solution)/shard_map/while/body/eval_jaxpr/ppermute | solution.py:22
  249.2 9.2 %collective-permute-start.2 = (f32[2,130,1]{2,1,0:T(8,128)}, f32[2,130,1]{2,1,0:T(8,128)}, u32[]{:S(2)}, u32[]{:S(2)}) collective-permute-start(f32[2,130,1]{2,1,0:T(8,128)} %get-tuple-element.166), channel_id=1, source_target_pairs={{1,0},{2,1},{3,2},{4,3},{5,4},{6,5},{7,6},{9,8},{10,9},{11,10},{12... | collective-permute-start | bytes 3128 | tf_op jit(solution)/shard_map/while/body/eval_jaxpr/ppermute | solution.py:22
  250.5 7.9 collective-permute-start.3
  266.8 8.5 %collective-permute-start = (f32[2,1,2048]{2,1,0:T(1,128)S(1)}, f32[2,1,2048]{2,1,0:T(1,128)S(1)}, u32[]{:S(2)}, u32[]{:S(2)}) collective-permute-start(f32[2,1,2048]{2,1,0:T(1,128)S(1)} %get-tuple-element.164), channel_id=1, source_target_pairs={{8,0},{16,8},{24,16},{32,24},{40,32},{48,40},{56,48},{64,56},{72,6... | collective-permute-start | bytes 49160 | tf_op jit(solution)/shard_map/while/body/eval_jaxpr/ppermute | solution.py:22
  278.2 9.2 %collective-permute-start.2 = (f32[2,130,1]{2,1,0:T(8,128)}, f32[2,130,1]{2,1,0:T(8,128)}, u32[]{:S(2)}, u32[]{:S(2)}) collective-permute-start(f32[2,130,1]{2,1,0:T(8,128)} %get-tuple-element.166), channel_id=1, source_target_pairs={{1,0},{2,1},{3,2},{4,3},{5,4},{6,5},{7,6},{9,8},{10,9},{11,10},{12... | collective-permute-start | bytes 3128 | tf_op jit(solution)/shard_map/while/body/eval_jaxpr/ppermute | solution.py:22
  279.5 7.9 collective-permute-start.3
  295.8 8.5 %collective-permute-start = (f32[2,1,2048]{2,1,0:T(1,128)S(1)}, f32[2,1,2048]{2,1,0:T(1,128)S(1)}, u32[]{:S(2)}, u32[]{:S(2)}) collective-permute-start(f32[2,1,2048]{2,1,0:T(1,128)S(1)} %get-tuple-element.164), channel_id=1, source_target_pairs={{8,0},{16,8},{24,16},{32,24},{40,32},{48,40},{56,48},{64,56},{72,6... | collective-permute-start | bytes 49160 | tf_op jit(solution)/shard_map/while/body/eval_jaxpr/ppermute | solution.py:22
  307.2 9.2 %collective-permute-start.2 = (f32[2,130,1]{2,1,0:T(8,128)}, f32[2,130,1]{2,1,0:T(8,128)}, u32[]{:S(2)}, u32[]{:S(2)}) collective-permute-start(f32[2,130,1]{2,1,0:T(8,128)} %get-tuple-element.166), channel_id=1, source_target_pairs={{1,0},{2,1},{3,2},{4,3},{5,4},{6,5},{7,6},{9,8},{10,9},{11,10},{12... | collective-permute-start | bytes 3128 | tf_op jit(solution)/shard_map/while/body/eval_jaxpr/ppermute | solution.py:22
  324.9 8.5 %collective-permute-start = (f32[2,1,2048]{2,1,0:T(1,128)S(1)}, f32[2,1,2048]{2,1,0:T(1,128)S(1)}, u32[]{:S(2)}, u32[]{:S(2)}) collective-permute-start(f32[2,1,2048]{2,1,0:T(1,128)S(1)} %get-tuple-element.164), channel_id=1, source_target_pairs={{8,0},{16,8},{24,16},{32,24},{40,32},{48,40},{56,48},{64,56},{72,6... | collective-permute-start | bytes 49160 | tf_op jit(solution)/shard_map/while/body/eval_jaxpr/ppermute | solution.py:22
  336.3 9.2 %collective-permute-start.2 = (f32[2,130,1]{2,1,0:T(8,128)}, f32[2,130,1]{2,1,0:T(8,128)}, u32[]{:S(2)}, u32[]{:S(2)}) collective-permute-start(f32[2,130,1]{2,1,0:T(8,128)} %get-tuple-element.166), channel_id=1, source_target_pairs={{1,0},{2,1},{3,2},{4,3},{5,4},{6,5},{7,6},{9,8},{10,9},{11,10},{12... | collective-permute-start | bytes 3128 | tf_op jit(solution)/shard_map/while/body/eval_jaxpr/ppermute | solution.py:22
  353.9 8.5 %collective-permute-start = (f32[2,1,2048]{2,1,0:T(1,128)S(1)}, f32[2,1,2048]{2,1,0:T(1,128)S(1)}, u32[]{:S(2)}, u32[]{:S(2)}) collective-permute-start(f32[2,1,2048]{2,1,0:T(1,128)S(1)} %get-tuple-element.164), channel_id=1, source_target_pairs={{8,0},{16,8},{24,16},{32,24},{40,32},{48,40},{56,48},{64,56},{72,6... | collective-permute-start | bytes 49160 | tf_op jit(solution)/shard_map/while/body/eval_jaxpr/ppermute | solution.py:22
  365.3 9.2 %collective-permute-start.2 = (f32[2,130,1]{2,1,0:T(8,128)}, f32[2,130,1]{2,1,0:T(8,128)}, u32[]{:S(2)}, u32[]{:S(2)}) collective-permute-start(f32[2,130,1]{2,1,0:T(8,128)} %get-tuple-element.166), channel_id=1, source_target_pairs={{1,0},{2,1},{3,2},{4,3},{5,4},{6,5},{7,6},{9,8},{10,9},{11,10},{12... | collective-permute-start | bytes 3128 | tf_op jit(solution)/shard_map/while/body/eval_jaxpr/ppermute | solution.py:22
  382.9 8.5 %collective-permute-start = (f32[2,1,2048]{2,1,0:T(1,128)S(1)}, f32[2,1,2048]{2,1,0:T(1,128)S(1)}, u32[]{:S(2)}, u32[]{:S(2)}) collective-permute-start(f32[2,1,2048]{2,1,0:T(1,128)S(1)} %get-tuple-element.164), channel_id=1, source_target_pairs={{8,0},{16,8},{24,16},{32,24},{40,32},{48,40},{56,48},{64,56},{72,6... | collective-permute-start | bytes 49160 | tf_op jit(solution)/shard_map/while/body/eval_jaxpr/ppermute | solution.py:22
  394.3 9.2 %collective-permute-start.2 = (f32[2,130,1]{2,1,0:T(8,128)}, f32[2,130,1]{2,1,0:T(8,128)}, u32[]{:S(2)}, u32[]{:S(2)}) collective-permute-start(f32[2,130,1]{2,1,0:T(8,128)} %get-tuple-element.166), channel_id=1, source_target_pairs={{1,0},{2,1},{3,2},{4,3},{5,4},{6,5},{7,6},{9,8},{10,9},{11,10},{12... | collective-permute-start | bytes 3128 | tf_op jit(solution)/shard_map/while/body/eval_jaxpr/ppermute | solution.py:22
  411.9 8.5 %collective-permute-start = (f32[2,1,2048]{2,1,0:T(1,128)S(1)}, f32[2,1,2048]{2,1,0:T(1,128)S(1)}, u32[]{:S(2)}, u32[]{:S(2)}) collective-permute-start(f32[2,1,2048]{2,1,0:T(1,128)S(1)} %get-tuple-element.164), channel_id=1, source_target_pairs={{8,0},{16,8},{24,16},{32,24},{40,32},{48,40},{56,48},{64,56},{72,6... | collective-permute-start | bytes 49160 | tf_op jit(solution)/shard_map/while/body/eval_jaxpr/ppermute | solution.py:22
  423.4 9.2 %collective-permute-start.2 = (f32[2,130,1]{2,1,0:T(8,128)}, f32[2,130,1]{2,1,0:T(8,128)}, u32[]{:S(2)}, u32[]{:S(2)}) collective-permute-start(f32[2,130,1]{2,1,0:T(8,128)} %get-tuple-element.166), channel_id=1, source_target_pairs={{1,0},{2,1},{3,2},{4,3},{5,4},{6,5},{7,6},{9,8},{10,9},{11,10},{12... | collective-permute-start | bytes 3128 | tf_op jit(solution)/shard_map/while/body/eval_jaxpr/ppermute | solution.py:22
  424.6 7.9 collective-permute-start.3
  441.0 8.5 %collective-permute-start = (f32[2,1,2048]{2,1,0:T(1,128)S(1)}, f32[2,1,2048]{2,1,0:T(1,128)S(1)}, u32[]{:S(2)}, u32[]{:S(2)}) collective-permute-start(f32[2,1,2048]{2,1,0:T(1,128)S(1)} %get-tuple-element.164), channel_id=1, source_target_pairs={{8,0},{16,8},{24,16},{32,24},{40,32},{48,40},{56,48},{64,56},{72,6... | collective-permute-start | bytes 49160 | tf_op jit(solution)/shard_map/while/body/eval_jaxpr/ppermute | solution.py:22
  452.4 9.2 %collective-permute-start.2 = (f32[2,130,1]{2,1,0:T(8,128)}, f32[2,130,1]{2,1,0:T(8,128)}, u32[]{:S(2)}, u32[]{:S(2)}) collective-permute-start(f32[2,130,1]{2,1,0:T(8,128)} %get-tuple-element.166), channel_id=1, source_target_pairs={{1,0},{2,1},{3,2},{4,3},{5,4},{6,5},{7,6},{9,8},{10,9},{11,10},{12... | collective-permute-start | bytes 3128 | tf_op jit(solution)/shard_map/while/body/eval_jaxpr/ppermute | solution.py:22
  453.7 7.9 collective-permute-start.3
  470.0 8.5 %collective-permute-start = (f32[2,1,2048]{2,1,0:T(1,128)S(1)}, f32[2,1,2048]{2,1,0:T(1,128)S(1)}, u32[]{:S(2)}, u32[]{:S(2)}) collective-permute-start(f32[2,1,2048]{2,1,0:T(1,128)S(1)} %get-tuple-element.164), channel_id=1, source_target_pairs={{8,0},{16,8},{24,16},{32,24},{40,32},{48,40},{56,48},{64,56},{72,6... | collective-permute-start | bytes 49160 | tf_op jit(solution)/shard_map/while/body/eval_jaxpr/ppermute | solution.py:22
  481.4 9.2 %collective-permute-start.2 = (f32[2,130,1]{2,1,0:T(8,128)}, f32[2,130,1]{2,1,0:T(8,128)}, u32[]{:S(2)}, u32[]{:S(2)}) collective-permute-start(f32[2,130,1]{2,1,0:T(8,128)} %get-tuple-element.166), channel_id=1, source_target_pairs={{1,0},{2,1},{3,2},{4,3},{5,4},{6,5},{7,6},{9,8},{10,9},{11,10},{12... | collective-permute-start | bytes 3128 | tf_op jit(solution)/shard_map/while/body/eval_jaxpr/ppermute | solution.py:22
  482.7 7.9 collective-permute-start.3
  499.0 8.5 %collective-permute-start = (f32[2,1,2048]{2,1,0:T(1,128)S(1)}, f32[2,1,2048]{2,1,0:T(1,128)S(1)}, u32[]{:S(2)}, u32[]{:S(2)}) collective-permute-start(f32[2,1,2048]{2,1,0:T(1,128)S(1)} %get-tuple-element.164), channel_id=1, source_target_pairs={{8,0},{16,8},{24,16},{32,24},{40,32},{48,40},{56,48},{64,56},{72,6... | collective-permute-start | bytes 49160 | tf_op jit(solution)/shard_map/while/body/eval_jaxpr/ppermute | solution.py:22
  510.4 9.2 %collective-permute-start.2 = (f32[2,130,1]{2,1,0:T(8,128)}, f32[2,130,1]{2,1,0:T(8,128)}, u32[]{:S(2)}, u32[]{:S(2)}) collective-permute-start(f32[2,130,1]{2,1,0:T(8,128)} %get-tuple-element.166), channel_id=1, source_target_pairs={{1,0},{2,1},{3,2},{4,3},{5,4},{6,5},{7,6},{9,8},{10,9},{11,10},{12... | collective-permute-start | bytes 3128 | tf_op jit(solution)/shard_map/while/body/eval_jaxpr/ppermute | solution.py:22
  528.1 8.5 %collective-permute-start = (f32[2,1,2048]{2,1,0:T(1,128)S(1)}, f32[2,1,2048]{2,1,0:T(1,128)S(1)}, u32[]{:S(2)}, u32[]{:S(2)}) collective-permute-start(f32[2,1,2048]{2,1,0:T(1,128)S(1)} %get-tuple-element.164), channel_id=1, source_target_pairs={{8,0},{16,8},{24,16},{32,24},{40,32},{48,40},{56,48},{64,56},{72,6... | collective-permute-start | bytes 49160 | tf_op jit(solution)/shard_map/while/body/eval_jaxpr/ppermute | solution.py:22
  539.5 9.2 %collective-permute-start.2 = (f32[2,130,1]{2,1,0:T(8,128)}, f32[2,130,1]{2,1,0:T(8,128)}, u32[]{:S(2)}, u32[]{:S(2)}) collective-permute-start(f32[2,130,1]{2,1,0:T(8,128)} %get-tuple-element.166), channel_id=1, source_target_pairs={{1,0},{2,1},{3,2},{4,3},{5,4},{6,5},{7,6},{9,8},{10,9},{11,10},{12... | collective-permute-start | bytes 3128 | tf_op jit(solution)/shard_map/while/body/eval_jaxpr/ppermute | solution.py:22
  557.1 8.5 %collective-permute-start = (f32[2,1,2048]{2,1,0:T(1,128)S(1)}, f32[2,1,2048]{2,1,0:T(1,128)S(1)}, u32[]{:S(2)}, u32[]{:S(2)}) collective-permute-start(f32[2,1,2048]{2,1,0:T(1,128)S(1)} %get-tuple-element.164), channel_id=1, source_target_pairs={{8,0},{16,8},{24,16},{32,24},{40,32},{48,40},{56,48},{64,56},{72,6... | collective-permute-start | bytes 49160 | tf_op jit(solution)/shard_map/while/body/eval_jaxpr/ppermute | solution.py:22
  568.5 9.2 %collective-permute-start.2 = (f32[2,130,1]{2,1,0:T(8,128)}, f32[2,130,1]{2,1,0:T(8,128)}, u32[]{:S(2)}, u32[]{:S(2)}) collective-permute-start(f32[2,130,1]{2,1,0:T(8,128)} %get-tuple-element.166), channel_id=1, source_target_pairs={{1,0},{2,1},{3,2},{4,3},{5,4},{6,5},{7,6},{9,8},{10,9},{11,10},{12... | collective-permute-start | bytes 3128 | tf_op jit(solution)/shard_map/while/body/eval_jaxpr/ppermute | solution.py:22
  586.1 8.5 %collective-permute-start = (f32[2,1,2048]{2,1,0:T(1,128)S(1)}, f32[2,1,2048]{2,1,0:T(1,128)S(1)}, u32[]{:S(2)}, u32[]{:S(2)}) collective-permute-start(f32[2,1,2048]{2,1,0:T(1,128)S(1)} %get-tuple-element.164), channel_id=1, source_target_pairs={{8,0},{16,8},{24,16},{32,24},{40,32},{48,40},{56,48},{64,56},{72,6... | collective-permute-start | bytes 49160 | tf_op jit(solution)/shard_map/while/body/eval_jaxpr/ppermute | solution.py:22
  597.5 9.2 %collective-permute-start.2 = (f32[2,130,1]{2,1,0:T(8,128)}, f32[2,130,1]{2,1,0:T(8,128)}, u32[]{:S(2)}, u32[]{:S(2)}) collective-permute-start(f32[2,130,1]{2,1,0:T(8,128)} %get-tuple-element.166), channel_id=1, source_target_pairs={{1,0},{2,1},{3,2},{4,3},{5,4},{6,5},{7,6},{9,8},{10,9},{11,10},{12... | collective-permute-start | bytes 3128 | tf_op jit(solution)/shard_map/while/body/eval_jaxpr/ppermute | solution.py:22
  614.5 8.0 %collective-permute-start.11 = (f32[2,1,2048]{2,1,0:T(1,128)S(1)}, f32[2,1,2048]{2,1,0:T(1,128)S(1)}, u32[]{:S(2)}, u32[]{:S(2)}) collective-permute-start(f32[2,1,2048]{2,1,0:T(1,128)S(1)} %get-tuple-element.103), channel_id=1, source_target_pairs={{0,8},{8,16},{16,24},{24,32},{32,40},{40,48},{48,56},{56,64},{64,7... | collective-permute-start | bytes 49160 | tf_op jit(solution)/shard_map/ppermute | solution.py:21
  649.8 18.6 %collective-permute-start.15 = (f32[2048,128]{1,0:T(8,128)}, f32[2048,128]{1,0:T(8,128)S(1)}, u32[]{:S(2)}, u32[]{:S(2)}) collective-permute-start(f32[2048,128]{1,0:T(8,128)} %copy.24), channel_id=1, source_target_pairs={{0,127},{1,0},{2,1},{3,2},{4,3},{5,4},{6,5},{7,6},{8,7},{9,8},{10,... | collective-permute-start | bytes 3145736 | tf_op jit(solution)/shard_map/ppermute | solution.py:29
  765.6 18.4 %collective-permute-start.16 = (f32[2048,128]{1,0:T(8,128)S(1)}, f32[2048,128]{1,0:T(8,128)S(1)}, u32[]{:S(2)}, u32[]{:S(2)}) collective-permute-start(f32[2048,128]{1,0:T(8,128)S(1)} %get-tuple-element.99), channel_id=1, source_target_pairs={{0,127},{1,0},{2,1},{3,2},{4,3},{5,4},{6,5},{7,6},{8,7},{9,8},{10,... | collective-permute-start | bytes 3145736 | tf_op jit(solution)/shard_map/ppermute | solution.py:29
  771.7 18.4 %collective-permute-start.17 = (f32[2048,128]{1,0:T(8,128)S(1)}, f32[2048,128]{1,0:T(8,128)S(1)}, u32[]{:S(2)}, u32[]{:S(2)}) collective-permute-start(f32[2048,128]{1,0:T(8,128)S(1)} %get-tuple-element.100), channel_id=1, source_target_pairs={{0,1},{1,2},{2,3},{3,4},{4,5},{5,6},{6,7},{7,8},{8,9},{9,10},{10,1... | collective-permute-start | bytes 3145736 | tf_op jit(solution)/shard_map/ppermute | solution.py:29
  (140 other events, 1051.5 us)
where the time goes:
time: 796 us; the launch traced here: 793 us
  other arithmetic  260 us (33%)
  starting transfers between devices  217 us (27%)
  local copies, waits for them, and re-layouts  204 us (26%)
  waiting for transfers between devices  92.4 us (12%)
  matrix products  16.4 us (2%)
    ppermute x37, starting transfers between devices, extended_2(): before = lax.ppermute(last, axis, up)  113 us
    mul x16, other arithmetic, relax(): (window(sources, 0, 0) + coupled) / diagonal * window(solid_mask, 0, 0)  105 us
    ppermute x37, starting transfers between devices, extended_2(): after = lax.ppermute(first, axis, down)  92 us
    scatter-add x1, other arithmetic, local(): jnp.zeros((3 * owned, 128), jnp.float32).at[local_rows].add(spread)  56.9 us
    ppermute x37, waiting for transfers between devices, extended_2(): before = lax.ppermute(last, axis, up)  47.1 us
    ppermute x4, waiting for transfers between devices, passed_along(): lax.ppermute(x, axis, [(i, (i + by) % length) for i in range(length)])  42.5 us
    gather x2, local copies, waits for them, and re-layouts, local(): picked = jnp.where(present[:, :, None], extended[local_rows], 0.0)  41.9 us
    squeeze x16, local copies, waits for them, and re-layouts, single_sweep(): grown_static[3]  41 us
  transfers between devices with their start and end apart: 78, of which 24 were waited for; matrix products, arithmetic and copies ran while one was open for 15% of the time, Pallas kernels for 0%

commit v1 on v0

v1 whole, which is shorter than its diff:
```python
import jax
import jax.numpy as jnp
from jax import lax
from jax.experimental import pallas as pl
from jax.experimental.pallas import tpu as pltpu
from jax.sharding import PartitionSpec as P

SWEEPS = 16
COND_FLOOR = 0.01
SQUEEZE_DAMPING = 0.25

SLOTS = 2048
SENT = 1536
BROWS = 16
QS = 17
MAIN = 8 * QS * 16
EXT = MAIN + QS * 32
OWNERS = ("wide", "narrow")


def main_row(a, slot, half):
    return (a * QS + slot) * 16 + half * 8


def rim_row(slot, part):
    return MAIN + slot * 32 + part * 8


def lane_ids(shape=(8, 128)):
    return lax.broadcasted_iota(jnp.int32, shape, 1)


def sub_ids(shape=(8, 128)):
    return lax.broadcasted_iota(jnp.int32, shape, 0)


def roll(x, by, axis):
    by = by % x.shape[axis]
    return x if by == 0 else pltpu.roll(x, by, axis)


def curve_offset(first_block):
    inner = first_block & (SLOTS - 1)
    row, col = inner >> 7, inner & 127
    h = (col >> 4) << 8
    for bit in range(4):
        h = h | (((col >> bit) & 1) << (2 * bit)) | (((row >> bit) & 1) << (2 * bit + 1))
    return SENT - h


def inner_place(brow, group):
    low, third = group >> 1, group & 1
    col = third * 8 + low
    place = 0
    for bit in range(4):
        place |= ((col >> bit) & 1) << (2 * bit)
        place |= ((brow >> bit) & 1) << (2 * bit + 1)
    return place


def swap_stages(vecs):
    lane = lane_ids(vecs[0].shape)
    vecs = list(vecs)
    for vec_bit, weight in ((0, 8), (3, 4), (2, 2), (1, 1)):
        upper = (lane & weight) != 0
        new = list(vecs)
        for i in range(16):
            if i & (1 << vec_bit):
                continue
            j = i | (1 << vec_bit)
            a, b = vecs[i], vecs[j]
            new[i] = jnp.where(upper, roll(b, weight, 1), a)
            new[j] = jnp.where(upper, b, roll(a, -weight, 1))
        vecs = new
    return vecs


def column_of(i):
    return ((i & 1) << 3) | (((i >> 3) & 1) << 2) | (((i >> 2) & 1) << 1) | ((i >> 1) & 1)


def east_west(ctr):
    lane = lane_ids()
    first, last, side = ctr[0], ctr[15], ctr[16]
    side_up, side_down = roll(side, 1, 1), roll(side, -1, 1)
    east15 = jnp.where(lane < 112, roll(first, -16, 1), roll(first, 104, 1))
    east15 = jnp.where(lane < 120, east15, roll(first, 119, 1))
    east15 = jnp.where(lane == 127, side_down, east15)
    west0 = jnp.where(lane >= 16, roll(last, 16, 1), roll(last, 24, 1))
    west0 = jnp.where(lane >= 8, west0, roll(last, 9, 1))
    west0 = jnp.where(lane == 0, side_up, west0)
    east16 = jnp.where(lane == 127, roll(first, -1, 1), side_down)
    west16 = jnp.where(lane == 0, roll(last, 1, 1), side_up)
    east = list(ctr[1:16]) + [east15, east16]
    west = [west0] + list(ctr[0:15]) + [west16]
    return east, west


def split3(x):
    high = x.astype(jnp.bfloat16)
    low = (x - high.astype(jnp.float32)).astype(jnp.bfloat16)
    return high, low


def dot3(x, w_high, w_low):
    high, low = split3(x)
    out = jnp.dot(high, w_high, preferred_element_type=jnp.float32)
    out = out + jnp.dot(low, w_high, preferred_element_type=jnp.float32)
    return out + jnp.dot(high, w_low, preferred_element_type=jnp.float32)


def inverse_denoms(sums):
    sub = sub_ids()
    table = {}
    for kind in range(3):
        base = sums[0]
        if kind != 0:
            base = base + sums[1]
        if kind != 2:
            base = base + sums[2]
        left = jnp.broadcast_to(sums[3], (8, 128))
        right = jnp.broadcast_to(sums[4], (8, 128))
        table[kind, 1] = 1.0 / (base + left + right)
        table[kind, 0] = 1.0 / (base + jnp.where(sub == 0, 0.0, left) + right)
        table[kind, 15] = 1.0 / (base + left + jnp.where(sub == 7, 0.0, right))

    def pick(brow, group):
        kind = 0 if brow == 0 else (2 if brow == BROWS - 1 else 1)
        return table[kind, group if group in (0, 15) else 1]

    return pick


def from_left(vecs, group):
    if group >= 2:
        return vecs(group - 2)
    if group == 1:
        return vecs(14)
    return jnp.where(sub_ids() == 0, 0.0, roll(vecs(15), 1, 0))


def from_right(vecs, group):
    if group < 14:
        return vecs(group + 2)
    if group == 14:
        return vecs(1)
    return jnp.where(sub_ids() == 7, 0.0, roll(vecs(0), -1, 0))


def sources_kernel(ok_ref, sq_ref, fw_ref, holes_ref, below_ref, above_ref, left_ref, right_ref,
                   out_sq, out_fw):
    lane = lane_ids()

    def spread(load, store):
        vecs = swap_stages([load(v) for v in range(16)])
        for i in range(16):
            store(column_of(i), vecs[i])

    def tile_rows(brow, carry):
        rows = pl.ds(pl.multiple_of(brow * 8, 8), 8)

        def masked(v):
            cols = pl.ds(v * 128, 128)
            return jnp.where(holes_ref[rows, cols] > 0, 0.0, fw_ref[rows, cols])

        def put(ref):
            def store(c, x):
                ref[pl.ds(c * 16 + brow, 8, stride=QS * 16), :] = x

            return store

        spread(lambda v: sq_ref[rows, pl.ds(v * 128, 128)], put(out_sq))
        spread(masked, put(out_fw))
        return carry

    lax.fori_loop(0, BROWS, tile_rows, 0)

    for field, out in ((0, out_sq), (1, out_fw)):
        for part in range(4):
            src = below_ref if part < 2 else above_ref
            ok = ok_ref[1] if part < 2 else ok_ref[0]
            rows = pl.ds(field * 16 + (part % 2) * 8, 8)

            def load(v, src=src, rows=rows, ok=ok):
                return jnp.where(ok > 0, src[rows, pl.ds(v * 128, 128)], 0.0)

            def store(c, x, part=part, out=out):
                out[pl.ds(rim_row(c, part), 8), :] = x

            spread(load, store)
        for block in range(20):
            rows = pl.ds(field * 160 + block * 8, 8)
            keep_right = (lane <= 16) & (ok_ref[3] > 0)
            keep_left = (lane >= 111) & (ok_ref[2] > 0)
            side = jnp.where(keep_right, right_ref[rows, :], jnp.where(keep_left, left_ref[rows, :], 0.0))
            if block < 16:
                out[pl.ds(16 * 16 + block, 8, stride=QS * 16), :] = side
            else:
                part = block - 16
                ok = ok_ref[1] if part < 2 else ok_ref[0]
                out[pl.ds(rim_row(16, part), 8), :] = jnp.where(ok > 0, side, 0.0)


def filter_kernel(first_ref, got_ref, own_ref, tiles_ref, dens_ref, up_ref, down_ref, cols_ref,
                  slots, blocks, prod, edge, sems):
    get = pltpu.make_async_copy(got_ref, slots.at[pl.ds(0, SENT)], sems.at[0])
    own = pltpu.make_async_copy(own_ref, slots.at[pl.ds(SENT, SLOTS)], sems.at[1])
    get.start()
    own.start()
    tiles = tiles_ref[...]
    t_high, t_low = split3(tiles)
    sums = [jnp.sum(tiles[:, k * 128:(k + 1) * 128], axis=0, keepdims=True) for k in range(5)]
    inverse = inverse_denoms(sums)
    offset = curve_offset(first_ref[0])
    get.wait()
    own.wait()
    for brow in range(BROWS):
        for group in range(16):
            blocks[pl.ds(brow * 128 + group * 8, 8), :] = slots[
                pl.ds(offset + inner_place(brow, group), 8, stride=256), :
            ]

    def multiply(brow, carry):
        rows = pl.ds(pl.multiple_of(brow * 128, 128), 128)
        prod[rows, :] = dot3(blocks[rows, :], t_high, t_low)
        return carry

    lax.fori_loop(0, BROWS, multiply, 0)

    def part(k, brow):
        return lambda group: prod[pl.ds(brow * 128 + group * 8, 8), pl.ds(k * 128, 128)]

    for brow in range(BROWS):
        vecs = []
        for group in range(16):
            x = part(0, brow)(group)
            if brow > 0:
                x = x + part(1, brow - 1)(group)
            if brow < BROWS - 1:
                x = x + part(2, brow + 1)(group)
            x = x + from_left(part(3, brow), group)
            x = x + from_right(part(4, brow), group)
            vecs.append(x * inverse(brow, group))
        edge[pl.ds(0 * 16 + brow, 1), :] = vecs[0][0:1]
        edge[pl.ds(1 * 16 + brow, 1), :] = vecs[2][0:1]
        edge[pl.ds(2 * 16 + brow, 1), :] = vecs[13][7:8]
        edge[pl.ds(3 * 16 + brow, 1), :] = vecs[15][7:8]
        turned = jnp.concatenate(vecs, axis=0).T
        for a in range(8):
            dens_ref[pl.ds(a * QS * 16 + brow, 16, stride=16), :] = turned[a * 16:(a + 1) * 16]
        if brow == 0:
            up_ref[0:128, :] = turned
        if brow == 1:
            up_ref[128:256, :] = turned
        if brow == 2:
            up_ref[256:272, :] = turned[0:16]
        if brow == 13:
            down_ref[256:272, :] = turned[112:128]
        if brow == 14:
            down_ref[0:128, :] = turned
        if brow == 15:
            down_ref[128:256, :] = turned
    lane = lane_ids((16, 128))
    c0, c1, c126, c127 = (edge[pl.ds(i * 16, 16), :] for i in range(4))
    for a in range(8):
        x = jnp.where(lane < 16, roll(c0, -16 * a, 1), 0.0)
        x = jnp.where(lane == 16, roll(c1, 16 - 16 * a, 1), x)
        x = jnp.where(lane == 111, roll(c126, 96 - 16 * a, 1), x)
        x = jnp.where(lane >= 112, roll(c127, 112 - 16 * a, 1), x)
        cols_ref[pl.ds(a * 16, 16), :] = x


def corner_kernel(below_ref, above_ref, cols_ref, out_ref):
    out_ref[0:128, :] = cols_ref[...]
    lane = lane_ids()
    sub = sub_ids()
    for part in range(5):
        if part < 4:
            src = below_ref if part < 2 else above_ref

            def load(c, src=src, part=part):
                return src[pl.ds(c + (part % 2) * 128, 8, stride=16), :]
        else:

            def load(c):
                low = jnp.broadcast_to(below_ref[pl.ds(256 + c, 1), :], (8, 128))
                high = jnp.broadcast_to(above_ref[pl.ds(256 + c, 1), :], (8, 128))
                return jnp.where(sub == 0, low, high)

        x = jnp.zeros((8, 128), jnp.float32)
        for c in range(16):
            here = load(c)
            x = jnp.where(lane == c, roll(here, c, 1), x)
            x = jnp.where(lane == 112 + c, roll(here, c - 15, 1), x)
            if c == 0:
                x = jnp.where(lane == 16, here, x)
            if c == 15:
                x = jnp.where(lane == 111, here, x)
        out_ref[pl.ds(128 + part * 8, 8), :] = x


def solve_kernel(ok_ref, first_ref, dens_ref, below_ref, above_ref, left_ref, right_ref, sq_ref, fw_ref,
                 tiles_ref, p_out, back_ref, keep_ref,
                 k, far, wn, ws, we, ww, bp, ba, pp, aa, blocks, prod, slots, sems):
    lane = lane_ids()
    sub = sub_ids()
    up_ok, down_ok, left_ok, right_ok = (ok_ref[i] > 0 for i in range(4))

    def conduct(d):
        return COND_FLOOR + (1.0 - COND_FLOOR) * d * d * d

    def fill(a, carry):
        for slot in range(16):
            for half in range(2):
                rows = pl.ds(pl.multiple_of((a * QS + slot) * 16 + half * 8, 8), 8)
                k[rows, :] = conduct(dens_ref[rows, :])
        return carry

    lax.fori_loop(0, 8, fill, 0)
    keep_right = (lane <= 16) & right_ok
    keep_left = (lane >= 111) & left_ok

    def side(rows):
        d = jnp.where(lane < 64, right_ref[rows, :], left_ref[rows, :])
        return jnp.where(keep_right | keep_left, conduct(d), 0.0)

    for a in range(8):
        for half in range(2):
            k[pl.ds(main_row(a, 16, half), 8), :] = side(pl.ds(a * 16 + half * 8, 8))
    for part in range(4):
        src, ok = (below_ref, down_ok) if part < 2 else (above_ref, up_ok)
        for slot in range(16):
            d = src[pl.ds(slot + (part % 2) * 128, 8, stride=16), :]
            k[pl.ds(rim_row(slot, part), 8), :] = jnp.where(ok, conduct(d), 0.0)
        k[pl.ds(rim_row(16, part), 8), :] = jnp.where(ok, side(pl.ds(128 + part * 8, 8)), 0.0)
    keep_far = ((sub == 0) & down_ok) | ((sub == 7) & up_ok)
    for slot in range(16):
        low = jnp.broadcast_to(below_ref[pl.ds(256 + slot, 1), :], (8, 128))
        high = jnp.broadcast_to(above_ref[pl.ds(256 + slot, 1), :], (8, 128))
        d = jnp.where(sub == 0, low, high)
        far[pl.ds(slot * 8, 8), :] = jnp.where(keep_far, conduct(d), 0.0)
    far[pl.ds(128, 8), :] = jnp.where(keep_far, side(pl.ds(160, 8)), 0.0)

    def vec(ref, base, row):
        if isinstance(base, int) and isinstance(row, int):
            return ref[pl.ds(base + row, 8), :]
        return ref[pl.ds(pl.multiple_of(base + row, 8), 8), :]

    def down_by_one(above, here):
        return jnp.where(sub == 0, roll(above, 1, 0), roll(here, 1, 0))

    def up_by_one(below, here):
        return jnp.where(sub == 7, roll(below, -1, 0), roll(here, -1, 0))

    def group(ref, base, a, half):
        ctr = [vec(ref, base, main_row(a, s, half)) for s in range(QS)]
        north, south = [], []
        for s in range(QS):
            if isinstance(a, int) and a == 0:
                if half == 0:
                    north.append(down_by_one(vec(ref, base, rim_row(s, 3)), vec(ref, base, main_row(7, s, 0))))
                else:
                    north.append(down_by_one(vec(ref, base, main_row(7, s, 0)), vec(ref, base, main_row(7, s, 1))))
            else:
                north.append(vec(ref, base, main_row(a - 1, s, half)))
            if isinstance(a, int) and a == 7:
                if half == 0:
                    south.append(up_by_one(vec(ref, base, main_row(0, s, 1)), vec(ref, base, main_row(0, s, 0))))
                else:
                    south.append(up_by_one(vec(ref, base, rim_row(s, 0)), vec(ref, base, main_row(0, s, 1))))
            else:
                south.append(vec(ref, base, main_row(a + 1, s, half)))
        return ctr, north, south

    def rim_group(ref, base, part, outer=None):
        ctr = [vec(ref, base, rim_row(s, part)) for s in range(QS)]
        north, south = [], []
        for s in range(QS):
            if part == 0:
                above = vec(ref, base, main_row(7, s, 1))
            elif part == 2:
                above = ctr[s] if outer is None else outer[pl.ds(s * 8, 8), :]
            else:
                above = vec(ref, base, rim_row(s, part - 1))
            if part == 3:
                below = vec(ref, base, main_row(0, s, 0))
            elif part == 1:
                below = ctr[s] if outer is None else outer[pl.ds(s * 8, 8), :]
            else:
                below = vec(ref, base, rim_row(s, part + 1))
            north.append(down_by_one(above, ctr[s]))
            south.append(up_by_one(below, ctr[s]))
        return ctr, north, south

    def each_group(body, parts):
        def inner(a, carry):
            for half in range(2):
                body(a, half, None)
            return carry

        lax.fori_loop(1, 7, inner, 0)
        for a in (0, 7):
            for half in range(2):
                body(a, half, None)
        for part in parts:
            body(None, None, part)

    def row_of(a, half, part, s):
        if part is not None:
            return rim_row(s, part)
        return main_row(a, s, half)

    def coefficients(a, half, part):
        ctr, north, south = group(k, 0, a, half) if part is None else rim_group(k, 0, part, far)
        east, west = east_west(ctr)
        for s in range(QS):
            row = row_of(a, half, part, s)
            rows = pl.ds(row if isinstance(row, int) else pl.multiple_of(row, 8), 8)
            fn, fs, fe, fv = (0.5 * (ctr[s] + other[s]) for other in (north, south, east, west))
            weight = fw_ref[rows, :]
            inv = jnp.where(weight > 0.0, 1.0, 0.0) / (fn + fs + fv + fe + SQUEEZE_DAMPING)
            wn[rows, :] = fn * inv
            ws[rows, :] = fs * inv
            we[rows, :] = fe * inv
            ww[rows, :] = fv * inv
            first_p = sq_ref[rows, :] * inv
            first_a = weight * inv
            bp[rows, :] = first_p
            ba[rows, :] = first_a
            pp[rows, :] = first_p
            aa[rows, :] = first_a

    each_group(coefficients, range(4))

    def sweep(src, dst, parts):
        def body(a, half, part):
            for ref, start in ((pp, bp), (aa, ba)):
                ctr, north, south = group(ref, src, a, half) if part is None else rim_group(ref, src, part)
                east, west = east_west(ctr)
                for s in range(QS):
                    row = row_of(a, half, part, s)
                    x = vec(start, 0, row) + vec(wn, 0, row) * north[s]
                    x = x + vec(ws, 0, row) * south[s]
                    x = x + vec(we, 0, row) * east[s]
                    x = x + vec(ww, 0, row) * west[s]
                    ref[pl.ds(pl.multiple_of(dst + row, 8), 8), :] = x

        each_group(body, parts)

    def one(parts):
        def step(i, carry):
            src = lax.rem(i, 2) * EXT
            sweep(src, EXT - src, parts)
            return carry

        return step

    half_way = SWEEPS // 2
    lax.fori_loop(0, half_way - 1, one(range(4)), 0)
    lax.fori_loop(half_way - 1, SWEEPS - 1, one((0, 3)), 0)
    last = ((SWEEPS - 1) % 2) * EXT

    def gradient(a, half, part):
        p_c, p_n, p_s = group(pp, last, a, half)
        p_e, p_w = east_west(p_c)
        a_c, a_n, a_s = group(aa, last, a, half)
        a_e, a_w = east_west(a_c)
        for s in range(16):
            row = main_row(a, s, half)
            total = (a_c[s] - a_n[s]) * (p_c[s] - p_n[s])
            total = total + (a_c[s] - a_s[s]) * (p_c[s] - p_s[s])
            total = total + (a_c[s] - a_w[s]) * (p_c[s] - p_w[s])
            total = total + (a_c[s] - a_e[s]) * (p_c[s] - p_e[s])
            d = vec(dens_ref, 0, row)
            rows = pl.ds(row if isinstance(row, int) else pl.multiple_of(row, 8), 8)
            k[rows, :] = -0.5 * total * (3.0 * (1.0 - COND_FLOOR)) * d * d
            p_out[rows, :] = p_c[s]

    each_group(gradient, ())

    tiles = tiles_ref[...]
    t_high, t_low = split3(tiles[:, :640])
    sums = [jnp.sum(tiles[:, 640 + i * 128:640 + (i + 1) * 128], axis=0, keepdims=True) for i in range(5)]
    inverse = inverse_denoms(sums)
    for brow in range(BROWS):
        film = jnp.concatenate(
            [k[pl.ds(a * QS * 16 + brow, 16, stride=16), :] for a in range(8)], axis=0
        ).T
        for g in range(16):
            blocks[pl.ds(brow * 128 + g * 8, 8), :] = film[g * 8:(g + 1) * 8] * inverse(brow, g)

    def multiply(brow, carry):
        rows = pl.ds(pl.multiple_of(brow * 128, 128), 128)
        prod[rows, :] = dot3(blocks[rows, :], t_high, t_low)
        return carry

    lax.fori_loop(0, BROWS, multiply, 0)

    def piece(i, brow):
        return lambda g: prod[pl.ds(brow * 128 + g * 8, 8), pl.ds(i * 128, 128)]

    offset = curve_offset(first_ref[0])
    for brow in range(BROWS):
        for g in range(16):
            x = piece(0, brow)(g)
            if brow < BROWS - 1:
                x = x + piece(1, brow + 1)(g)
            if brow > 0:
                x = x + piece(2, brow - 1)(g)
            x = x + from_right(piece(3, brow), g)
            x = x + from_left(piece(4, brow), g)
            slots[pl.ds(offset + inner_place(brow, g), 8, stride=256), :] = x
    back = pltpu.make_async_copy(slots.at[pl.ds(0, SENT)], back_ref, sems.at[0])
    keep = pltpu.make_async_copy(slots.at[pl.ds(SENT, SLOTS)], keep_ref, sems.at[1])
    back.start()
    keep.start()
    back.wait()
    keep.wait()


def pressure_kernel(p_ref, out_ref):
    order = [column_of(i) for i in range(16)]

    def tile_rows(brow, carry):
        vecs = [p_ref[pl.ds(c * 16 + brow, 8, stride=QS * 16), :] for c in order]
        vecs = swap_stages(vecs)
        rows = pl.ds(pl.multiple_of(brow * 8, 8), 8)
        for v in range(16):
            out_ref[rows, pl.ds(v * 128, 128)] = vecs[v]
        return carry

    lax.fori_loop(0, BROWS, tile_rows, 0)


def moved(x, axis, by):
    length = lax.axis_size(axis)
    return lax.ppermute(x, axis, [(i, (i + by) % length) for i in range(length)])


def f32(*shape):
    return jax.ShapeDtypeStruct(shape, jnp.float32)


def local(design, filter_tiles, filter_cols, slot_block, holes, squeeze_source, force_weight):
    smem = pl.BlockSpec(memory_space=pltpu.SMEM)
    vmem = pl.BlockSpec(memory_space=pltpu.VMEM)
    hbm = pl.BlockSpec(memory_space=pl.ANY)
    params = pltpu.CompilerParams(vmem_limit_bytes=56 * 1024 * 1024)
    wide, narrow = lax.axis_index("wide"), lax.axis_index("narrow")
    inside = jnp.stack([
        wide > 0, wide < lax.axis_size("wide") - 1, narrow > 0, narrow < lax.axis_size("narrow") - 1,
    ]).astype(jnp.int32)
    first = slot_block[0:1]
    taps = filter_tiles.transpose(2, 0, 1).reshape(128, 640)
    back_taps = jnp.concatenate([filter_tiles.transpose(1, 0, 2).reshape(128, 640), taps], axis=1)

    got = moved(design[SLOTS - SENT:], OWNERS, 1)

    def edge_rows(rows):
        weight = jnp.where(holes[rows] > 0, 0.0, force_weight[rows])
        return jnp.concatenate([squeeze_source[rows], weight], axis=0)

    below = moved(edge_rows(slice(0, 16)), "wide", -1)
    above = moved(edge_rows(slice(112, 128)), "wide", 1)

    def ends(x):
        lane = lax.broadcasted_iota(jnp.int32, (1, 128), 1)
        return jnp.where(lane < 64, x[:, :128], x[:, -128:])

    masked = jnp.where(ends(holes) > 0, 0.0, ends(force_weight))
    sides = jnp.concatenate([
        ends(squeeze_source), ends(below[:16]), ends(above[:16]),
        masked, ends(below[16:]), ends(above[16:]),
    ], axis=0)
    right = moved(sides, "narrow", -1)
    left = moved(sides, "narrow", 1)
    sq, fw = pl.pallas_call(
        sources_kernel,
        out_shape=(f32(EXT, 128), f32(EXT, 128)),
        in_specs=[smem] + [vmem] * 7,
        compiler_params=params,
        name="sources",
    )(inside, squeeze_source, force_weight, holes, below, above, left, right)

    dens, up, down, cols = pl.pallas_call(
        filter_kernel,
        out_shape=(f32(MAIN, 128), f32(272, 128), f32(272, 128), f32(128, 128)),
        in_specs=[smem, hbm, hbm, vmem],
        scratch_shapes=[
            pltpu.VMEM((SENT + SLOTS, 128), jnp.float32),
            pltpu.VMEM((SLOTS, 128), jnp.float32),
            pltpu.VMEM((SLOTS, 640), jnp.float32),
            pltpu.VMEM((64, 128), jnp.float32),
            pltpu.SemaphoreType.DMA((2,)),
        ],
        compiler_params=params,
        name="filter",
    )(first, got, design, taps)
    d_below = moved(up, "wide", -1)
    d_above = moved(down, "wide", 1)
    d_sides = pl.pallas_call(
        corner_kernel, out_shape=f32(168, 128), compiler_params=params, name="corners",
    )(d_below, d_above, cols)
    d_right = moved(d_sides, "narrow", -1)
    d_left = moved(d_sides, "narrow", 1)

    big = pltpu.VMEM((EXT, 128), jnp.float32)
    twice = pltpu.VMEM((2 * EXT, 128), jnp.float32)
    p_film, back, keep = pl.pallas_call(
        solve_kernel,
        out_shape=(f32(MAIN, 128), f32(SENT, 128), f32(SLOTS, 128)),
        in_specs=[smem, smem] + [vmem] * 8,
        out_specs=(vmem, hbm, hbm),
        scratch_shapes=[
            big, pltpu.VMEM((QS * 8, 128), jnp.float32), big, big, big, big, big, big, twice, twice,
            pltpu.VMEM((SLOTS, 128), jnp.float32),
            pltpu.VMEM((SLOTS, 640), jnp.float32),
            pltpu.VMEM((SENT + SLOTS, 128), jnp.float32),
            pltpu.SemaphoreType.DMA((2,)),
        ],
        compiler_params=params,
        name="solve",
    )(inside, first, dens, d_below, d_above, d_left, d_right, sq, fw, back_taps)
    returned = moved(back, OWNERS, -1)
    pressure = pl.pallas_call(
        pressure_kernel, out_shape=f32(128, 2048), compiler_params=params, name="pressure",
    )(p_film)
    held = curve_offset(first[0]) + (SLOTS - SENT)
    slot = lax.broadcasted_iota(jnp.int32, (SLOTS, 1), 0)
    tail = jnp.pad(returned, ((SLOTS - SENT, 0), (0, 0)))
    sensitivity = jnp.where(slot < held, keep, tail)
    return pressure, sensitivity


def solution(mesh):
    placed = (
        P(OWNERS, None),
        P(),
        P(OWNERS, None),
        P(OWNERS),
        P("wide", "narrow"),
        P("wide", "narrow"),
        P("wide", "narrow"),
    )
    return jax.shard_map(
        local,
        mesh=mesh,
        in_specs=placed,
        out_specs=(P("wide", "narrow"), P(OWNERS, None)),
        check_vma=False,
    )
```

time: 796 us -> 129 us (0.16)
  the two profiles are of different devices: /device:TPU:64 before, /device:TPU:25 now
where the time goes in v1:
time: 129 us
  Pallas kernels  75.6 us (59%)
  waiting for transfers between devices  19.2 us (15%)
  starting transfers between devices  18.8 us (15%)
  other arithmetic  7.52 us (6%)
  local copies, waits for them, and re-layouts  6.08 us (5%)
  between operations  1.57 us (1%)
    pallas_call x1, Pallas kernels, local(): pl.pallas_call(solve_kernel, out_shape=(f32(MAIN, 128), f32(SENT, 128), f...  45.3 us
    ppermute x10, waiting for transfers between devices, moved(): lax.ppermute(x, axis, [(i, (i + by) % length) for i in range(length)])  19.2 us
    ppermute x10, starting transfers between devices, moved(): lax.ppermute(x, axis, [(i, (i + by) % length) for i in range(length)])  18.8 us
    pallas_call x1, Pallas kernels, local(): pl.pallas_call(sources_kernel, out_shape=(f32(EXT, 128), f32(EXT, 128)),...  10.6 us
    pallas_call x1, Pallas kernels, local(): pl.pallas_call(filter_kernel, out_shape=(f32(MAIN, 128), f32(272, 128), f...  10.5 us
    pallas_call x1, Pallas kernels, local(): pl.pallas_call(pressure_kernel, out_shape=f32(128, 2048), compiler_params...  7.35 us
    unnamed x27, local copies, waits for them, and re-layouts  3.69 us
  transfers between devices with their start and end apart: 10, of which 5 were waited for; matrix products, arithmetic and copies ran while one was open for 5% of the time, Pallas kernels for 24%

profile of v1, /device:TPU:25, one launch (start us, length us, event | category | flops | bytes accessed | tf_op | source)
XLA Modules:
  0.0 128.8 jit_solution(8536798109615736727)
XLA Ops:
  0.6 0.0 copy-start
  0.6 1.3 %slice_select_fusion = (f32[16,2048]{1,0:T(8,128)S(1)}, f32[16,2048]{1,0:T(8,128)S(1)}, f32[16,2048]{1,0:T(8,128)S(1)}, f32[16,2048]{1,0:T(8,128)S(1)}) fusion(f32[128,2048]{1,0:T(8,128)} %fw_ref.1, s32[128,2048]{1,0:T(8,128)} %holes_ref.1, f32[128,2048]{1,0:T(8,128)} %sq_ref.1), kind=kLoop, calls=%fused_computation.4 | loop fusion | flops 131072 | bytes 1310720 | tf_op jit(solution)/shard_map/jit(_where)/select_n | solution.py:560
  2.0 0.0 copy-start.2
  2.0 0.7 pad_maximum_fusion.1
  2.7 6.0 %collective-permute-start.5 = (f32[32,2048]{1,0:T(8,128)}, f32[32,2048]{1,0:T(8,128)S(1)}, u32[]{:S(2)}, u32[]{:S(2)}) collective-permute-start(f32[32,2048]{1,0:T(8,128)} %pad_maximum_fusion.1), channel_id=1, source_target_pairs={{0,120},{8,0},{16,8},{24,16},{32,24},{40,32},{48,40},{56,48},{64,5... | collective-permute-start | bytes 786440 | tf_op jit(solution)/shard_map/ppermute | solution.py:537
  8.7 0.7 pad_maximum_fusion.2
  9.4 0.0 collective-permute-start.6
  9.4 0.1 slice.79
  9.4 0.1 collective-permute-start
  9.5 0.9 select_dynamic-update-slice_fusion.1
  10.4 1.3 slice.78.first_ref
  11.7 0.2 copy.11
  11.9 0.9 copy.10.tiles_ref
  12.8 0.2 copy.12
  12.9 0.0 copy-start.1
  12.9 1.0 collective-permute-done.5.below_ref
  14.0 5.8 %collective-permute-done.6.above_ref = f32[32,2048]{1,0:T(8,128)S(1)} collective-permute-done((f32[32,2048]{1,0:T(8,128)}, f32[32,2048]{1,0:T(8,128)S(1)}, u32[]{:S(2)}, u32[]{:S(2)}) %collective-permute-start.6) | collective-permute-done | bytes 262176 | tf_op jit(solution)/shard_map/ppermute | solution.py:537
  19.8 1.0 select_dynamic-update-slice_fusion
  20.9 1.7 %collective-permute-start.7 = (f32[320,128]{1,0:T(8,128)S(1)}, f32[320,128]{1,0:T(8,128)S(1)}, u32[]{:S(2)}, u32[]{:S(2)}) collective-permute-start(f32[320,128]{1,0:T(8,128)S(1)} %constant_dynamic-update-slice_fusion), channel_id=1, source_target_pairs={{0,1},{1,2},{2,3},{3,4},{4,5},{5,6},{6,7},{7,0},{8,9},{9,10},{10,1... | collective-permute-start | bytes 491528 | tf_op jit(solution)/shard_map/ppermute | solution.py:537
  22.6 1.7 %collective-permute-start.8 = (f32[320,128]{1,0:T(8,128)S(1)}, f32[320,128]{1,0:T(8,128)S(1)}, u32[]{:S(2)}, u32[]{:S(2)}) collective-permute-start(f32[320,128]{1,0:T(8,128)S(1)} %constant_dynamic-update-slice_fusion), channel_id=1, source_target_pairs={{0,7},{1,0},{2,1},{3,2},{4,3},{5,4},{6,5},{7,6},{8,15},{9,8},{10,9... | collective-permute-start | bytes 491528 | tf_op jit(solution)/shard_map/ppermute | solution.py:537
  24.2 0.0 collective-permute-done.got_ref
  24.2 0.9 copy-done.4
  25.1 10.5 %filter.1 = (f32[2176,128]{1,0:T(8,128)}, f32[272,128]{1,0:T(8,128)}, f32[272,128]{1,0:T(8,128)}, f32[128,128]{1,0:T(8,128)}) custom-call(s32[1]{0:T(128)} %slice.78.first_ref, f32[1536,128]{1,0:T(8,128)} %copy-done.4, f32[2048,128]{1,0:T(8,128)} %own_ref.1, f32[128,640]{1,0:T(8,128)} %copy.10.tiles_ref), custom_call_target="tpu_custom_call" | custom-call | tf_op jit(solution)/shard_map/filter/pallas_call | solution.py:585
  35.6 4.8 %collective-permute-start.1 = (f32[272,128]{1,0:T(8,128)}, f32[272,128]{1,0:T(8,128)S(1)}, u32[]{:S(2)}, u32[]{:S(2)}) collective-permute-start(f32[272,128]{1,0:T(8,128)} %get-tuple-element.12), channel_id=1, source_target_pairs={{0,120},{8,0},{16,8},{24,16},{32,24},{40,32},{48,40},{56,48},{64,5... | collective-permute-start | bytes 417800 | tf_op jit(solution)/shard_map/ppermute | solution.py:537
  40.4 0.0 collective-permute-start.2
  40.4 0.9 pad_maximum_fusion.tiles_ref
  41.3 1.5 %collective-permute-done.1.below_ref = f32[272,128]{1,0:T(8,128)S(1)} collective-permute-done((f32[272,128]{1,0:T(8,128)}, f32[272,128]{1,0:T(8,128)S(1)}, u32[]{:S(2)}, u32[]{:S(2)}) %collective-permute-start.1) | collective-permute-done | bytes 139296 | tf_op jit(solution)/shard_map/ppermute | solution.py:537
  42.8 5.3 %collective-permute-done.2.above_ref = f32[272,128]{1,0:T(8,128)S(1)} collective-permute-done((f32[272,128]{1,0:T(8,128)}, f32[272,128]{1,0:T(8,128)S(1)}, u32[]{:S(2)}, u32[]{:S(2)}) %collective-permute-start.2) | collective-permute-done | bytes 139296 | tf_op jit(solution)/shard_map/ppermute | solution.py:537
  48.1 0.7 copy-done.6
  48.7 1.8 %corners.1 = f32[168,128]{1,0:T(8,128)} custom-call(f32[272,128]{1,0:T(8,128)} %copy-done.5, f32[272,128]{1,0:T(8,128)} %copy-done.6, f32[128,128]{1,0:T(8,128)} %get-tuple-element.14.cols_ref), custom_call_target="tpu_custom_call" | custom-call | tf_op jit(solution)/shard_map/corners/pallas_call | solution.py:601
  50.6 4.5 %collective-permute-start.3 = (f32[168,128]{1,0:T(8,128)}, f32[168,128]{1,0:T(8,128)S(1)}, u32[]{:S(2)}, u32[]{:S(2)}) collective-permute-start(f32[168,128]{1,0:T(8,128)} %corners.1), channel_id=1, source_target_pairs={{0,1},{1,2},{2,3},{3,4},{4,5},{5,6},{6,7},{7,0},{8,9},{9,10},{10,1... | collective-permute-start | bytes 258056 | tf_op jit(solution)/shard_map/ppermute | solution.py:537
  55.1 0.0 collective-permute-start.4
  55.1 0.6 add_convert_fusion.ok_ref
  55.7 0.0 collective-permute-done.7.left_ref
  55.7 0.0 collective-permute-done.8.right_ref
  55.7 0.6 copy-done.9
  56.3 0.7 copy-done.10
  57.0 10.6 %sources.1 = (f32[2720,128]{1,0:T(8,128)}, f32[2720,128]{1,0:T(8,128)}) custom-call(s32[4]{0:T(128)} %add_convert_fusion.ok_ref, f32[128,2048]{1,0:T(8,128)} %sq_ref.1, f32[128,2048]{1,0:T(8,128)} %fw_ref.1, s32[128,2048]{1,0:T(8,128)} %holes_ref.1, f32[32,2048]{1,0:T(8,128)} %copy-done.7, f32[32,2048]{1,0:T(8,128)} %copy-done.8, f32[320,128]{1,0:T(8,128)} %copy-done.9, ...), custom_call_target="tpu_custom_call" | custom-call | tf_op jit(solution)/shard_map/sources/pallas_call | solution.py:577
  67.6 0.0 collective-permute-done.3.left_ref
  67.6 0.0 collective-permute-done.4.right_ref
  67.7 0.6 copy-done.11
  68.3 0.0 copy-done.12
  68.3 45.3 %solve.1 = (f32[2176,128]{1,0:T(8,128)}, f32[1536,128]{1,0:T(8,128)}, f32[2048,128]{1,0:T(8,128)}) custom-call(s32[4]{0:T(128)} %add_convert_fusion.ok_ref, s32[1]{0:T(128)} %slice.78.first_ref, f32[2176,128]{1,0:T(8,128)} %get-tuple-element.11.dens_ref, f32[272,128]{1,0:T(8,128)} %copy-done.5, f32[272,128]{1,0:T(8,128)} %copy-done.6, ...), custom_call_target="tpu_custom_call" | custom-call | tf_op jit(solution)/shard_map/solve/pallas_call | solution.py:609
  113.6 0.0 copy-start.3
  113.7 0.1 collective-permute-start.9
  114.5 7.3 %pressure.1 = f32[128,2048]{1,0:T(8,128)} custom-call(f32[2176,128]{1,0:T(8,128)} %get-tuple-element.17.p_ref), custom_call_target="tpu_custom_call" | custom-call | tf_op jit(solution)/shard_map/pressure/pallas_call | solution.py:625
  121.9 5.6 %collective-permute-done.9 = f32[1536,128]{1,0:T(8,128)S(1)} collective-permute-done((f32[1536,128]{1,0:T(8,128)}, f32[1536,128]{1,0:T(8,128)S(1)}, u32[]{:S(2)}, u32[]{:S(2)}) %collective-permute-start.9) | collective-permute-done | bytes 786464 | tf_op jit(solution)/shard_map/ppermute | solution.py:537
  127.5 1.3 %pad_select_fusion = f32[2048,128]{1,0:T(8,128)} fusion(f32[2048,128]{1,0:T(8,128)S(1)} %copy-done.3, f32[1536,128]{1,0:T(8,128)S(1)} %collective-permute-done.9, pred[2048]{0:T(1024)(128)(4,1)S(1)} %iota_compare_fusion), kind=kLoop, calls=%fused_computation | loop fusion | flops 262144 | bytes 2885632 | tf_op jit(solution)/shard_map/jit(_where)/select_n | solution.py:631
  (22 shorter events, 0.1 us)
Async XLA Ops:
  0.6 8.8 %copy-start = (f32[2048,128]{1,0:T(8,128)S(1)}, f32[2048,128]{1,0:T(8,128)}, u32[]{:S(2)}) copy-start(f32[2048,128]{1,0:T(8,128)} %own_ref.1) | copy-start | bytes 3145732
  2.0 9.7 %copy-start.2 = (f32[5,128,128]{2,1,0:T(8,128)S(1)}, f32[5,128,128]{2,1,0:T(8,128)}, u32[]{:S(2)}) copy-start(f32[5,128,128]{2,1,0:T(8,128)} %param.8) | copy-start | bytes 983044
  2.7 11.2 %collective-permute-start.5 = (f32[32,2048]{1,0:T(8,128)}, f32[32,2048]{1,0:T(8,128)S(1)}, u32[]{:S(2)}, u32[]{:S(2)}) collective-permute-start(f32[32,2048]{1,0:T(8,128)} %pad_maximum_fusion.1), channel_id=1, source_target_pairs={{0,120},{8,0},{16,8},{24,16},{32,24},{40,32},{48,40},{56,48},{64,5... | collective-permute-start | bytes 786440 | tf_op jit(solution)/shard_map/ppermute | solution.py:537
  9.4 10.4 %collective-permute-start.6 = (f32[32,2048]{1,0:T(8,128)}, f32[32,2048]{1,0:T(8,128)S(1)}, u32[]{:S(2)}, u32[]{:S(2)}) collective-permute-start(f32[32,2048]{1,0:T(8,128)} %pad_maximum_fusion.2), channel_id=1, source_target_pairs={{0,8},{8,16},{16,24},{24,32},{32,40},{40,48},{48,56},{56,64},{64,7... | collective-permute-start | bytes 786440 | tf_op jit(solution)/shard_map/ppermute | solution.py:537
  9.4 14.8 %collective-permute-start = (f32[1536,128]{1,0:T(8,128)S(1)}, f32[1536,128]{1,0:T(8,128)S(1)}, u32[]{:S(2)}, u32[]{:S(2)}) collective-permute-start(f32[1536,128]{1,0:T(8,128)S(1)} %slice.79), channel_id=1, source_target_pairs={{0,1},{1,2},{2,3},{3,4},{4,5},{5,6},{6,7},{7,8},{8,9},{9,10},{10,1... | collective-permute-start | bytes 2359304 | tf_op jit(solution)/shard_map/ppermute | solution.py:537
  12.9 27.5 %copy-start.1 = (f32[128,640]{1,0:T(8,128)S(1)}, f32[128,640]{1,0:T(8,128)}, u32[]{:S(2)}) copy-start(f32[128,640]{1,0:T(8,128)} %copy.10.tiles_ref) | copy-start | bytes 983044
  14.0 27.3 %copy-start.7 = (f32[32,2048]{1,0:T(8,128)}, f32[32,2048]{1,0:T(8,128)S(1)}, u32[]{:S(2)}) copy-start(f32[32,2048]{1,0:T(8,128)S(1)} %collective-permute-done.5.below_ref) | copy-start | bytes 786436
  19.8 35.9 %copy-start.8 = (f32[32,2048]{1,0:T(8,128)}, f32[32,2048]{1,0:T(8,128)S(1)}, u32[]{:S(2)}) copy-start(f32[32,2048]{1,0:T(8,128)S(1)} %collective-permute-done.6.above_ref) | copy-start | bytes 786436
  20.9 34.8 %collective-permute-start.7 = (f32[320,128]{1,0:T(8,128)S(1)}, f32[320,128]{1,0:T(8,128)S(1)}, u32[]{:S(2)}, u32[]{:S(2)}) collective-permute-start(f32[320,128]{1,0:T(8,128)S(1)} %constant_dynamic-update-slice_fusion), channel_id=1, source_target_pairs={{0,1},{1,2},{2,3},{3,4},{4,5},{5,6},{6,7},{7,0},{8,9},{9,10},{10,1... | collective-permute-start | bytes 491528 | tf_op jit(solution)/shard_map/ppermute | solution.py:537
  22.6 33.1 %collective-permute-start.8 = (f32[320,128]{1,0:T(8,128)S(1)}, f32[320,128]{1,0:T(8,128)S(1)}, u32[]{:S(2)}, u32[]{:S(2)}) collective-permute-start(f32[320,128]{1,0:T(8,128)S(1)} %constant_dynamic-update-slice_fusion), channel_id=1, source_target_pairs={{0,7},{1,0},{2,1},{3,2},{4,3},{5,4},{6,5},{7,6},{8,15},{9,8},{10,9... | collective-permute-start | bytes 491528 | tf_op jit(solution)/shard_map/ppermute | solution.py:537
  24.2 0.9 copy-start.4
  35.6 7.2 %collective-permute-start.1 = (f32[272,128]{1,0:T(8,128)}, f32[272,128]{1,0:T(8,128)S(1)}, u32[]{:S(2)}, u32[]{:S(2)}) collective-permute-start(f32[272,128]{1,0:T(8,128)} %get-tuple-element.12), channel_id=1, source_target_pairs={{0,120},{8,0},{16,8},{24,16},{32,24},{40,32},{48,40},{56,48},{64,5... | collective-permute-start | bytes 417800 | tf_op jit(solution)/shard_map/ppermute | solution.py:537
  40.4 7.6 %collective-permute-start.2 = (f32[272,128]{1,0:T(8,128)}, f32[272,128]{1,0:T(8,128)S(1)}, u32[]{:S(2)}, u32[]{:S(2)}) collective-permute-start(f32[272,128]{1,0:T(8,128)} %get-tuple-element.13), channel_id=1, source_target_pairs={{0,8},{8,16},{16,24},{24,32},{32,40},{40,48},{48,56},{56,64},{64,7... | collective-permute-start | bytes 417800 | tf_op jit(solution)/shard_map/ppermute | solution.py:537
  42.7 5.3 %copy-start.5 = (f32[272,128]{1,0:T(8,128)}, f32[272,128]{1,0:T(8,128)S(1)}, u32[]{:S(2)}) copy-start(f32[272,128]{1,0:T(8,128)S(1)} %collective-permute-done.1.below_ref) | copy-start | bytes 417796
  48.0 0.7 copy-start.6
  50.6 17.1 %collective-permute-start.3 = (f32[168,128]{1,0:T(8,128)}, f32[168,128]{1,0:T(8,128)S(1)}, u32[]{:S(2)}, u32[]{:S(2)}) collective-permute-start(f32[168,128]{1,0:T(8,128)} %corners.1), channel_id=1, source_target_pairs={{0,1},{1,2},{2,3},{3,4},{4,5},{5,6},{6,7},{7,0},{8,9},{9,10},{10,1... | collective-permute-start | bytes 258056 | tf_op jit(solution)/shard_map/ppermute | solution.py:537
  55.1 12.6 %collective-permute-start.4 = (f32[168,128]{1,0:T(8,128)}, f32[168,128]{1,0:T(8,128)S(1)}, u32[]{:S(2)}, u32[]{:S(2)}) collective-permute-start(f32[168,128]{1,0:T(8,128)} %corners.1), channel_id=1, source_target_pairs={{0,7},{1,0},{2,1},{3,2},{4,3},{5,4},{6,5},{7,6},{8,15},{9,8},{10,9... | collective-permute-start | bytes 258056 | tf_op jit(solution)/shard_map/ppermute | solution.py:537
  55.7 0.7 copy-start.9
  56.3 0.7 copy-start.10
  67.6 0.6 copy-start.11
  67.7 0.6 copy-start.12
  113.6 13.8 %copy-start.3 = (f32[2048,128]{1,0:T(8,128)S(1)}, f32[2048,128]{1,0:T(8,128)}, u32[]{:S(2)}) copy-start(f32[2048,128]{1,0:T(8,128)} %get-tuple-element.18) | copy-start | bytes 3145732
  113.7 13.8 %collective-permute-start.9 = (f32[1536,128]{1,0:T(8,128)}, f32[1536,128]{1,0:T(8,128)S(1)}, u32[]{:S(2)}, u32[]{:S(2)}) collective-permute-start(f32[1536,128]{1,0:T(8,128)} %get-tuple-element.19), channel_id=1, source_target_pairs={{0,127},{1,0},{2,1},{3,2},{4,3},{5,4},{6,5},{7,6},{8,7},{9,8},{10,... | collective-permute-start | bytes 2359304 | tf_op jit(solution)/shard_map/ppermute | solution.py:537

commit v2 on v1

--- a/solution.py
+++ b/solution.py
@@ -6,6 +6,10 @@
 from jax.sharding import PartitionSpec as P
 
 SWEEPS = 16
+CHUNK = 3
+UNROLL = False
+MROWS = 512
+ROOM = (10, 16, 4, 34, 4, 4)
 COND_FLOOR = 0.01
 SQUEEZE_DAMPING = 0.25
 
@@ -14,7 +18,8 @@
 BROWS = 16
 QS = 17
 MAIN = 8 * QS * 16
-EXT = MAIN + QS * 32
+RIMS = QS * 32
+EXT = MAIN + RIMS
 OWNERS = ("wide", "narrow")
 
 
@@ -96,17 +101,22 @@
     return east, west
 
 
-def split3(x):
+def split(x):
     high = x.astype(jnp.bfloat16)
     low = (x - high.astype(jnp.float32)).astype(jnp.bfloat16)
     return high, low
 
 
-def dot3(x, w_high, w_low):
-    high, low = split3(x)
-    out = jnp.dot(high, w_high, preferred_element_type=jnp.float32)
-    out = out + jnp.dot(low, w_high, preferred_element_type=jnp.float32)
-    return out + jnp.dot(high, w_low, preferred_element_type=jnp.float32)
+def stacked(w):
+    high, low = split(w)
+    return jnp.concatenate([high, high, low], axis=0)
+
+
+def put_parts(parts, rows, x):
+    high, low = split(x)
+    parts[rows, 0:128] = high
+    parts[rows, 128:256] = low
+    parts[rows, 256:384] = high
 
 
 def inverse_denoms(sums):
@@ -147,15 +157,13 @@
     return jnp.where(sub_ids() == 7, 0.0, roll(vecs(0), -1, 0))
 
 
-def sources_kernel(ok_ref, sq_ref, fw_ref, holes_ref, below_ref, above_ref, left_ref, right_ref,
-                   out_sq, out_fw):
-    lane = lane_ids()
-
-    def spread(load, store):
-        vecs = swap_stages([load(v) for v in range(16)])
-        for i in range(16):
-            store(column_of(i), vecs[i])
-
+def spread(load, store):
+    vecs = swap_stages([load(v) for v in range(16)])
+    for i in range(16):
+        store(column_of(i), vecs[i])
+
+
+def sources_kernel(sq_ref, fw_ref, holes_ref, out_sq, out_fw):
     def tile_rows(brow, carry):
         rows = pl.ds(pl.multiple_of(brow * 8, 8), 8)
 
@@ -165,7 +173,7 @@
 
         def put(ref):
             def store(c, x):
-                ref[pl.ds(c * 16 + brow, 8, stride=QS * 16), :] = x
+                ref[pl.ds(c * 16 + brow, 8, stride=256), :] = x
 
             return store
 
@@ -173,8 +181,13 @@
         spread(masked, put(out_fw))
         return carry
 
-    lax.fori_loop(0, BROWS, tile_rows, 0)
-
+    lax.fori_loop(0, BROWS, tile_rows, 0, unroll=2)
+
+
+def rims_kernel(ok_ref, below_ref, above_ref, left_ref, right_ref, out_sq, out_fw):
+    lane = lane_ids()
+    keep_right = (lane <= 16) & (ok_ref[3] > 0)
+    keep_left = (lane >= 111) & (ok_ref[2] > 0)
     for field, out in ((0, out_sq), (1, out_fw)):
         for part in range(4):
             src = below_ref if part < 2 else above_ref
@@ -185,47 +198,36 @@
                 return jnp.where(ok > 0, src[rows, pl.ds(v * 128, 128)], 0.0)
 
             def store(c, x, part=part, out=out):
-                out[pl.ds(rim_row(c, part), 8), :] = x
+                out[pl.ds(c * 32 + part * 8, 8), :] = x
 
             spread(load, store)
         for block in range(20):
             rows = pl.ds(field * 160 + block * 8, 8)
-            keep_right = (lane <= 16) & (ok_ref[3] > 0)
-            keep_left = (lane >= 111) & (ok_ref[2] > 0)
             side = jnp.where(keep_right, right_ref[rows, :], jnp.where(keep_left, left_ref[rows, :], 0.0))
             if block < 16:
-                out[pl.ds(16 * 16 + block, 8, stride=QS * 16), :] = side
+                out[pl.ds(RIMS + block, 8, stride=16), :] = side
             else:
                 part = block - 16
                 ok = ok_ref[1] if part < 2 else ok_ref[0]
-                out[pl.ds(rim_row(16, part), 8), :] = jnp.where(ok > 0, side, 0.0)
+                out[pl.ds(16 * 32 + part * 8, 8), :] = jnp.where(ok > 0, side, 0.0)
 
 
 def filter_kernel(first_ref, got_ref, own_ref, tiles_ref, dens_ref, up_ref, down_ref, cols_ref,
-                  slots, blocks, prod, edge, sems):
-    get = pltpu.make_async_copy(got_ref, slots.at[pl.ds(0, SENT)], sems.at[0])
-    own = pltpu.make_async_copy(own_ref, slots.at[pl.ds(SENT, SLOTS)], sems.at[1])
-    get.start()
-    own.start()
-    tiles = tiles_ref[...]
-    t_high, t_low = split3(tiles)
-    sums = [jnp.sum(tiles[:, k * 128:(k + 1) * 128], axis=0, keepdims=True) for k in range(5)]
-    inverse = inverse_denoms(sums)
+                  slots, parts, prod, edge):
+    tiles = [tiles_ref[i].T for i in range(5)]
+    inverse = inverse_denoms([jnp.sum(t, axis=0, keepdims=True) for t in tiles])
+    weights = stacked(jnp.concatenate(tiles, axis=1))
     offset = curve_offset(first_ref[0])
-    get.wait()
-    own.wait()
+    slots[pl.ds(0, SENT), :] = got_ref[...]
+    slots[pl.ds(SENT, SLOTS), :] = own_ref[...]
     for brow in range(BROWS):
-        for group in range(16):
-            blocks[pl.ds(brow * 128 + group * 8, 8), :] = slots[
-                pl.ds(offset + inner_place(brow, group), 8, stride=256), :
-            ]
-
-    def multiply(brow, carry):
-        rows = pl.ds(pl.multiple_of(brow * 128, 128), 128)
-        prod[rows, :] = dot3(blocks[rows, :], t_high, t_low)
-        return carry
-
-    lax.fori_loop(0, BROWS, multiply, 0)
+        x = jnp.concatenate(
+            [slots[pl.ds(offset + inner_place(brow, g), 8, stride=256), :] for g in range(16)], axis=0
+        )
+        put_parts(parts, pl.ds(brow * 128, 128), x)
+    for i in range(SLOTS // MROWS):
+        rows = pl.ds(i * MROWS, MROWS)
+        prod[rows, :] = jnp.dot(parts[rows, :], weights, preferred_element_type=jnp.float32)
 
     def part(k, brow):
         return lambda group: prod[pl.ds(brow * 128 + group * 8, 8), pl.ds(k * 128, 128)]
@@ -300,8 +302,8 @@
 
 
 def solve_kernel(ok_ref, first_ref, dens_ref, below_ref, above_ref, left_ref, right_ref, sq_ref, fw_ref,
-                 tiles_ref, p_out, back_ref, keep_ref,
-                 k, far, wn, ws, we, ww, bp, ba, pp, aa, blocks, prod, slots, sems):
+                 sq_rim, fw_rim, tiles_ref, p_out, back_ref, keep_ref,
+                 k, far, wn, ws, we, ww, bp, ba, p0, p1, a0, a1, parts, prod, slots):
     lane = lane_ids()
     sub = sub_ids()
     up_ok, down_ok, left_ok, right_ok = (ok_ref[i] > 0 for i in range(4))
@@ -345,6 +347,9 @@
         if isinstance(base, int) and isinstance(row, int):
             return ref[pl.ds(base + row, 8), :]
         return ref[pl.ds(pl.multiple_of(base + row, 8), 8), :]
+
+    def rows_at(row):
+        return pl.ds(row if isinstance(row, int) else pl.multiple_of(row, 8), 8)
 
     def down_by_one(above, here):
         return jnp.where(sub == 0, roll(above, 1, 0), roll(here, 1, 0))
@@ -416,54 +421,114 @@
         for s in range(QS):
             row = row_of(a, half, part, s)
             rows = pl.ds(row if isinstance(row, int) else pl.multiple_of(row, 8), 8)
+            if part is not None:
+                source, sources = pl.ds(s * 32 + part * 8, 8), (sq_rim, fw_rim)
+            elif s == 16:
+                source, sources = rows_at(RIMS + a * 16 + half * 8), (sq_rim, fw_rim)
+            else:
+                source, sources = rows_at((a * 16 + s) * 16 + half * 8), (sq_ref, fw_ref)
             fn, fs, fe, fv = (0.5 * (ctr[s] + other[s]) for other in (north, south, east, west))
-            weight = fw_ref[rows, :]
+            weight = sources[1][source, :]
             inv = jnp.where(weight > 0.0, 1.0, 0.0) / (fn + fs + fv + fe + SQUEEZE_DAMPING)
             wn[rows, :] = fn * inv
             ws[rows, :] = fs * inv
             we[rows, :] = fe * inv
             ww[rows, :] = fv * inv
-            first_p = sq_ref[rows, :] * inv
+            first_p = sources[0][source, :] * inv
             first_a = weight * inv
             bp[rows, :] = first_p
             ba[rows, :] = first_a
-            pp[rows, :] = first_p
-            aa[rows, :] = first_a
+            p0[rows, :] = first_p
+            a0[rows, :] = first_a
 
     each_group(coefficients, range(4))
 
-    def sweep(src, dst, parts):
-        def body(a, half, part):
-            for ref, start in ((pp, bp), (aa, ba)):
-                ctr, north, south = group(ref, src, a, half) if part is None else rim_group(ref, src, part)
-                east, west = east_west(ctr)
-                for s in range(QS):
-                    row = row_of(a, half, part, s)
-                    x = vec(start, 0, row) + vec(wn, 0, row) * north[s]
-                    x = x + vec(ws, 0, row) * south[s]
-                    x = x + vec(we, 0, row) * east[s]
-                    x = x + vec(ww, 0, row) * west[s]
-                    ref[pl.ds(pl.multiple_of(dst + row, 8), 8), :] = x
-
-        each_group(body, parts)
-
-    def one(parts):
+    def ends_of(ref, row):
+        first, last, beside = (vec(ref, 0, row(s)) for s in (0, 15, 16))
+        east, west = east_west([first] + [None] * 14 + [last, beside])
+        return {15: east[15], 16: east[16]}, {0: west[0], 16: west[16]}
+
+    def sweep(old, new, full):
+        def relax(rows, neighbours):
+            ends = [[ends_of(ref, row) for row in rows] for ref in old]
+            before = [[None] * len(rows) for _ in old]
+            here = [[vec(ref, 0, row(0)) for row in rows] for ref in old]
+            for s in range(QS):
+                after = [[vec(ref, 0, row(s + 1)) if s < QS - 1 else None for row in rows] for ref in old]
+                around = [neighbours(f, s, here[f]) for f in range(2)]
+                for i, row in enumerate(rows):
+                    at = row(s)
+                    cn, cs, ce, cw = (vec(c, 0, at) for c in (wn, ws, we, ww))
+                    for f, start in enumerate((bp, ba)):
+                        north, south = around[f][i]
+                        east = ends[f][i][0].get(s, after[f][i])
+                        west = ends[f][i][1].get(s, before[f][i])
+                        x = (vec(start, 0, at) + cn * north) + (cs * south + (ce * east + cw * west))
+                        new[f][rows_at(at), :] = x
+                before, here = here, after
+
+        def chunk(i, carry):
+            a = CHUNK * i + 1
+            for half in range(2):
+                def neighbours(f, s, ctr, half=half):
+                    north = vec(old[f], 0, main_row(a - 1, s, half))
+                    south = vec(old[f], 0, main_row(a + CHUNK, s, half))
+                    column = [north] + ctr + [south]
+                    return [(column[j], column[j + 2]) for j in range(CHUNK)]
+
+                relax([lambda s, half=half, j=j: main_row(a + j, s, half) for j in range(CHUNK)], neighbours)
+            return carry
+
+        if UNROLL:
+            for i in range(6 // CHUNK):
+                chunk(i, 0)
+        else:
+            lax.fori_loop(0, 6 // CHUNK, chunk, 0)
+
+        ring = [
+            lambda s: main_row(7, s, 0), lambda s: main_row(7, s, 1),
+            lambda s: main_row(0, s, 0), lambda s: main_row(0, s, 1),
+            lambda s: rim_row(s, 0), lambda s: rim_row(s, 3),
+        ]
+        if full:
+            ring += [lambda s: rim_row(s, 1), lambda s: rim_row(s, 2)]
+
+        def ring_neighbours(f, s, ctr):
+            down = [roll(x, 1, 0) for x in ctr]
+            up = [roll(x, -1, 0) for x in ctr]
+            top, low = sub == 0, sub == 7
+            ref = old[f]
+            out = [
+                (vec(ref, 0, main_row(6, s, 0)), jnp.where(low, up[3], up[2])),
+                (vec(ref, 0, main_row(6, s, 1)), jnp.where(low, up[4], up[3])),
+                (jnp.where(top, down[5], down[0]), vec(ref, 0, main_row(1, s, 0))),
+                (jnp.where(top, down[0], down[1]), vec(ref, 0, main_row(1, s, 1))),
+                (jnp.where(top, down[1], down[4]), jnp.where(low, up[6], up[4]) if full else up[4]),
+                (jnp.where(top, down[7], down[5]) if full else down[5], jnp.where(low, up[2], up[5])),
+            ]
+            if full:
+                out += [(jnp.where(top, down[4], down[6]), up[6]), (down[7], jnp.where(low, up[5], up[7]))]
+            return out
+
+        relax(ring, ring_neighbours)
+
+    def two_sweeps(full):
         def step(i, carry):
-            src = lax.rem(i, 2) * EXT
-            sweep(src, EXT - src, parts)
+            sweep((p0, a0), (p1, a1), full)
+            sweep((p1, a1), (p0, a0), full)
             return carry
 
         return step
 
-    half_way = SWEEPS // 2
-    lax.fori_loop(0, half_way - 1, one(range(4)), 0)
-    lax.fori_loop(half_way - 1, SWEEPS - 1, one((0, 3)), 0)
-    last = ((SWEEPS - 1) % 2) * EXT
+    lax.fori_loop(0, 4, two_sweeps(True), 0)
+    lax.fori_loop(0, 3, two_sweeps(False), 0)
+    sweep((p0, a0), (p1, a1), False)
+    last = 0
 
     def gradient(a, half, part):
-        p_c, p_n, p_s = group(pp, last, a, half)
+        p_c, p_n, p_s = group(p1, last, a, half)
         p_e, p_w = east_west(p_c)
-        a_c, a_n, a_s = group(aa, last, a, half)
+        a_c, a_n, a_s = group(a1, last, a, half)
         a_e, a_w = east_west(a_c)
         for s in range(16):
             row = main_row(a, s, half)
@@ -478,23 +543,17 @@
 
     each_group(gradient, ())
 
-    tiles = tiles_ref[...]
-    t_high, t_low = split3(tiles[:, :640])
-    sums = [jnp.sum(tiles[:, 640 + i * 128:640 + (i + 1) * 128], axis=0, keepdims=True) for i in range(5)]
-    inverse = inverse_denoms(sums)
+    inverse = inverse_denoms([jnp.sum(tiles_ref[i].T, axis=0, keepdims=True) for i in range(5)])
+    weights = stacked(jnp.concatenate([tiles_ref[i] for i in range(5)], axis=1))
     for brow in range(BROWS):
         film = jnp.concatenate(
             [k[pl.ds(a * QS * 16 + brow, 16, stride=16), :] for a in range(8)], axis=0
         ).T
-        for g in range(16):
-            blocks[pl.ds(brow * 128 + g * 8, 8), :] = film[g * 8:(g + 1) * 8] * inverse(brow, g)
-
-    def multiply(brow, carry):
-        rows = pl.ds(pl.multiple_of(brow * 128, 128), 128)
-        prod[rows, :] = dot3(blocks[rows, :], t_high, t_low)
-        return carry
-
-    lax.fori_loop(0, BROWS, multiply, 0)
+        film = jnp.concatenate([film[g * 8:(g + 1) * 8] * inverse(brow, g) for g in range(16)], axis=0)
+        put_parts(parts, pl.ds(brow * 128, 128), film)
+    for i in range(SLOTS // MROWS):
+        rows = pl.ds(i * MROWS, MROWS)
+        prod[rows, :] = jnp.dot(parts[rows, :], weights, preferred_element_type=jnp.float32)
 
     def piece(i, brow):
         return lambda g: prod[pl.ds(brow * 128 + g * 8, 8), pl.ds(i * 128, 128)]
@@ -510,12 +569,8 @@
             x = x + from_right(piece(3, brow), g)
             x = x + from_left(piece(4, brow), g)
             slots[pl.ds(offset + inner_place(brow, g), 8, stride=256), :] = x
-    back = pltpu.make_async_copy(slots.at[pl.ds(0, SENT)], back_ref, sems.at[0])
-    keep = pltpu.make_async_copy(slots.at[pl.ds(SENT, SLOTS)], keep_ref, sems.at[1])
-    back.start()
-    keep.start()
-    back.wait()
-    keep.wait()
+    back_ref[...] = slots[pl.ds(0, SENT), :]
+    keep_ref[...] = slots[pl.ds(SENT, SLOTS), :]
 
 
 def pressure_kernel(p_ref, out_ref):
@@ -529,7 +584,7 @@
             out_ref[rows, pl.ds(v * 128, 128)] = vecs[v]
         return carry
 
-    lax.fori_loop(0, BROWS, tile_rows, 0)
+    lax.fori_loop(0, BROWS, tile_rows, 0, unroll=4)
 
 
 def moved(x, axis, by):
@@ -537,6 +592,14 @@
     return lax.ppermute(x, axis, [(i, (i + by) % length) for i in range(length)])
 
 
+def room(mib):
+    return pltpu.CompilerParams(vmem_limit_bytes=mib * 1024 * 1024)
+
+
+def work(flops, moved_bytes):
+    return pl.CostEstimate(flops=flops, transcendentals=0, bytes_accessed=moved_bytes)
+
+
 def f32(*shape):
     return jax.ShapeDtypeStruct(shape, jnp.float32)
 
@@ -544,17 +607,25 @@
 def local(design, filter_tiles, filter_cols, slot_block, holes, squeeze_source, force_weight):
     smem = pl.BlockSpec(memory_space=pltpu.SMEM)
     vmem = pl.BlockSpec(memory_space=pltpu.VMEM)
-    hbm = pl.BlockSpec(memory_space=pl.ANY)
-    params = pltpu.CompilerParams(vmem_limit_bytes=56 * 1024 * 1024)
     wide, narrow = lax.axis_index("wide"), lax.axis_index("narrow")
     inside = jnp.stack([
         wide > 0, wide < lax.axis_size("wide") - 1, narrow > 0, narrow < lax.axis_size("narrow") - 1,
     ]).astype(jnp.int32)
     first = slot_block[0:1]
-    taps = filter_tiles.transpose(2, 0, 1).reshape(128, 640)
-    back_taps = jnp.concatenate([filter_tiles.transpose(1, 0, 2).reshape(128, 640), taps], axis=1)
-
-    got = moved(design[SLOTS - SENT:], OWNERS, 1)
+    tail, holes, squeeze_source, force_weight = lax.optimization_barrier(
+        (design[SLOTS - SENT:], holes, squeeze_source, force_weight)
+    )
+    got = moved(tail, OWNERS, 1)
+    sq, fw = pl.pallas_call(
+        sources_kernel,
+        out_shape=(f32(SLOTS, 128), f32(SLOTS, 128)),
+        compiler_params=room(ROOM[0]),
+        cost_estimate=work(2000000, 5000000),
+        name="sources",
+    )(squeeze_source, force_weight, holes)
+    sq, fw, first, holes, squeeze_source, force_weight = lax.optimization_barrier(
+        (sq, fw, first, holes, squeeze_source, force_weight)
+    )
 
     def edge_rows(rows):
         weight = jnp.where(holes[rows] > 0, 0.0, force_weight[rows])
@@ -574,61 +645,60 @@
     ], axis=0)
     right = moved(sides, "narrow", -1)
     left = moved(sides, "narrow", 1)
-    sq, fw = pl.pallas_call(
-        sources_kernel,
-        out_shape=(f32(EXT, 128), f32(EXT, 128)),
-        in_specs=[smem] + [vmem] * 7,
-        compiler_params=params,
-        name="sources",
-    )(inside, squeeze_source, force_weight, holes, below, above, left, right)
+    sq_rim, fw_rim = pl.pallas_call(
+        rims_kernel,
+        out_shape=(f32(RIMS + 128, 128), f32(RIMS + 128, 128)),
+        in_specs=[smem] + [vmem] * 4,
+        compiler_params=room(ROOM[5]),
+        cost_estimate=work(500000, 1200000),
+        name="rims",
+    )(inside, below, above, left, right)
 
     dens, up, down, cols = pl.pallas_call(
         filter_kernel,
         out_shape=(f32(MAIN, 128), f32(272, 128), f32(272, 128), f32(128, 128)),
-        in_specs=[smem, hbm, hbm, vmem],
+        in_specs=[smem, vmem, vmem, vmem],
         scratch_shapes=[
             pltpu.VMEM((SENT + SLOTS, 128), jnp.float32),
-            pltpu.VMEM((SLOTS, 128), jnp.float32),
+            pltpu.VMEM((SLOTS, 384), jnp.bfloat16),
             pltpu.VMEM((SLOTS, 640), jnp.float32),
             pltpu.VMEM((64, 128), jnp.float32),
-            pltpu.SemaphoreType.DMA((2,)),
         ],
-        compiler_params=params,
+        compiler_params=room(ROOM[1]),
+        cost_estimate=work(1100000000, 3500000),
         name="filter",
-    )(first, got, design, taps)
+    )(first, got, design, filter_tiles)
     d_below = moved(up, "wide", -1)
     d_above = moved(down, "wide", 1)
     d_sides = pl.pallas_call(
-        corner_kernel, out_shape=f32(168, 128), compiler_params=params, name="corners",
+        corner_kernel, out_shape=f32(168, 128), compiler_params=room(ROOM[2]), cost_estimate=work(200000, 500000), name="corners",
     )(d_below, d_above, cols)
     d_right = moved(d_sides, "narrow", -1)
     d_left = moved(d_sides, "narrow", 1)
 
     big = pltpu.VMEM((EXT, 128), jnp.float32)
-    twice = pltpu.VMEM((2 * EXT, 128), jnp.float32)
     p_film, back, keep = pl.pallas_call(
         solve_kernel,
         out_shape=(f32(MAIN, 128), f32(SENT, 128), f32(SLOTS, 128)),
-        in_specs=[smem, smem] + [vmem] * 8,
-        out_specs=(vmem, hbm, hbm),
+        in_specs=[smem, smem] + [vmem] * 10,
         scratch_shapes=[
-            big, pltpu.VMEM((QS * 8, 128), jnp.float32), big, big, big, big, big, big, twice, twice,
-            pltpu.VMEM((SLOTS, 128), jnp.float32),
+            big, pltpu.VMEM((QS * 8, 128), jnp.float32), big, big, big, big, big, big, big, big, big, big,
+            pltpu.VMEM((SLOTS, 384), jnp.bfloat16),
             pltpu.VMEM((SLOTS, 640), jnp.float32),
             pltpu.VMEM((SENT + SLOTS, 128), jnp.float32),
-            pltpu.SemaphoreType.DMA((2,)),
         ],
-        compiler_params=params,
+        compiler_params=room(ROOM[3]),
+        cost_estimate=work(1400000000, 9000000),
         name="solve",
-    )(inside, first, dens, d_below, d_above, d_left, d_right, sq, fw, back_taps)
+    )(inside, first, dens, d_below, d_above, d_left, d_right, sq, fw, sq_rim, fw_rim, filter_tiles)
     returned = moved(back, OWNERS, -1)
     pressure = pl.pallas_call(
-        pressure_kernel, out_shape=f32(128, 2048), compiler_params=params, name="pressure",
+        pressure_kernel, out_shape=f32(128, 2048), compiler_params=room(ROOM[4]), cost_estimate=work(2000000, 2100000), name="pressure",
     )(p_film)
     held = curve_offset(first[0]) + (SLOTS - SENT)
     slot = lax.broadcasted_iota(jnp.int32, (SLOTS, 1), 0)
-    tail = jnp.pad(returned, ((SLOTS - SENT, 0), (0, 0)))
-    sensitivity = jnp.where(slot < held, keep, tail)
+    upper = jnp.pad(returned, ((SLOTS - SENT, 0), (0, 0)))
+    sensitivity = jnp.where(slot < held, keep, upper)
     return pressure, sensitivity
 
 

time: 129 us -> 95.8 us (0.74)
  Pallas kernels: 75.6 us -> 40 us
  waiting for transfers between devices: 19.2 us -> 24.5 us
  starting transfers between devices: 18.8 us -> 15.1 us
    pallas_call x1, Pallas kernels: 45.3 us -> 26.4 us  [local(): pl.pallas_call(solve_kernel, out_shape=(f32(MAIN, 128), f32(SENT, 128), f...]
    pallas_call x1, Pallas kernels: 10.5 us -> 3.94 us  [local(): pl.pallas_call(filter_kernel, out_shape=(f32(MAIN, 128), f32(272, 128), f...]
    pallas_call x2 -> x3, Pallas kernels: 12.5 us -> 6.6 us  [the longest x1 4.44 us: local(): pl.pallas_call(sources_kernel, out_shape=(f32(SLOTS, 128), f32(SLOTS, 128...]
    ppermute x10, waiting for transfers between devices: 19.2 us -> 24.5 us  [moved(): lax.ppermute(x, axis, [(i, (i + by) % length) for i in range(length)])]
    pallas_call x1, Pallas kernels: 7.35 us -> 3.03 us  [local(): pl.pallas_call(pressure_kernel, out_shape=f32(128, 2048), compiler_params...]
    ppermute x10, starting transfers between devices: 18.8 us -> 15.1 us  [moved(): lax.ppermute(x, axis, [(i, (i + by) % length) for i in range(length)])]
    unnamed x5, other arithmetic: 1.94 us -> 4.02 us
    concatenate x2, other arithmetic: 1.44 us -> 0.04 us  [edge_rows(): return jnp.concatenate([squeeze_source[rows], weight], axis=0)]
  transfers between devices with their start and end apart: 10 -> 10, of which waited for: 5 -> 5; matrix products, arithmetic and copies ran while one was open for 5% -> 7% of each run, Pallas kernels for 24% -> 10%
where the time goes in v2:
time: 95.8 us; the launch traced here: 95.5 us
  Pallas kernels  40 us (42%)
  waiting for transfers between devices  24.5 us (26%)
  starting transfers between devices  15.1 us (16%)
  local copies, waits for them, and re-layouts  7.29 us (8%)
  other arithmetic  7.21 us (8%)
  between operations  1.4 us (1%)
    pallas_call x1, Pallas kernels, local(): pl.pallas_call(solve_kernel, out_shape=(f32(MAIN, 128), f32(SENT, 128), f...  26.4 us
    ppermute x10, waiting for transfers between devices, moved(): lax.ppermute(x, axis, [(i, (i + by) % length) for i in range(length)])  24.5 us
    ppermute x10, starting transfers between devices, moved(): lax.ppermute(x, axis, [(i, (i + by) % length) for i in range(length)])  15.1 us
    unnamed x16, local copies, waits for them, and re-layouts  4.75 us
    pallas_call x1, Pallas kernels, local(): pl.pallas_call(sources_kernel, out_shape=(f32(SLOTS, 128), f32(SLOTS, 128...  4.44 us
    unnamed x5, other arithmetic  4.02 us
    pallas_call x1, Pallas kernels, local(): pl.pallas_call(filter_kernel, out_shape=(f32(MAIN, 128), f32(272, 128), f...  3.94 us
    pallas_call x1, Pallas kernels, local(): pl.pallas_call(pressure_kernel, out_shape=f32(128, 2048), compiler_params...  3.03 us
  transfers between devices with their start and end apart: 10, of which 5 were waited for; matrix products, arithmetic and copies ran while one was open for 7% of the time, Pallas kernels for 10%

profile of v2, /device:TPU:25, one launch (start us, length us, event | category | flops | bytes accessed | tf_op | source)
XLA Modules:
  0.0 95.5 jit_solution(12676691193833632596)
XLA Ops:
  0.6 0.0 copy-start
  0.6 1.3 %slice.78 = f32[1536,128]{1,0:T(8,128)S(1)} slice(f32[2048,128]{1,0:T(8,128)} %own_ref.1), slice={[512:2048], [0:128]} | slice | bytes 1572864 | tf_op jit(solution)/shard_map/slice | solution.py:616
  1.9 1.5 %collective-permute-start = (f32[1536,128]{1,0:T(8,128)S(1)}, f32[1536,128]{1,0:T(8,128)S(1)}, u32[]{:S(2)}, u32[]{:S(2)}) collective-permute-start(f32[1536,128]{1,0:T(8,128)S(1)} %slice.78), channel_id=1, source_target_pairs={{0,1},{1,2},{2,3},{3,4},{4,5},{5,6},{6,7},{7,8},{8,9},{9,10},{10,1... | collective-permute-start | bytes 2359304 | tf_op jit(solution)/shard_map/ppermute | solution.py:592
  3.4 1.3 %slice.79.first_ref = s32[1]{0:T(128)} slice(s32[2048]{0:T(1024)} %param.9), slice={[0:1]} | slice | bytes 8 | tf_op jit(solution)/shard_map/slice | solution.py:614
  4.7 0.0 copy-done
  4.7 1.2 %copy-done.1 = f32[128,2048]{1,0:T(8,128)S(1)} copy-done((f32[128,2048]{1,0:T(8,128)S(1)}, f32[128,2048]{1,0:T(8,128)}, u32[]{:S(2)}) %copy-start.1) | copy-done | bytes 1048600
  5.9 1.2 %copy-done.2 = s32[128,2048]{1,0:T(8,128)S(1)} copy-done((s32[128,2048]{1,0:T(8,128)S(1)}, s32[128,2048]{1,0:T(8,128)}, u32[]{:S(2)}) %copy-start.2) | copy-done | bytes 1048600
  7.1 4.4 %sources.1 = (f32[2048,128]{1,0:T(8,128)S(1)}, f32[2048,128]{1,0:T(8,128)S(1)}) custom-call(f32[128,2048]{1,0:T(8,128)S(1)} %copy-done, f32[128,2048]{1,0:T(8,128)S(1)} %copy-done.1, s32[128,2048]{1,0:T(8,128)S(1)} %copy-done.2), custom_call_target="tpu_custom_call" | custom-call | flops 2000000 | bytes 5000000 | tf_op jit(solution)/shard_map/sources/pallas_call | solution.py:619
  11.6 1.1 %slice_select_fusion = (f32[16,2048]{1,0:T(8,128)S(1)}, f32[16,2048]{1,0:T(8,128)S(1)}, f32[16,2048]{1,0:T(8,128)S(1)}, f32[16,2048]{1,0:T(8,128)S(1)}) fusion(f32[128,2048]{1,0:T(8,128)} %fw_ref, s32[128,2048]{1,0:T(8,128)} %holes_ref, f32[128,2048]{1,0:T(8,128)S(1)} %copy-done), kind=kLoop, calls=%fused_computation.3 | loop fusion | flops 131072 | bytes 1310720 | tf_op jit(solution)/shard_map/jit(_where)/select_n | solution.py:631
  12.7 0.0 copy-start.3
  12.7 0.0 copy-start.4
  12.8 4.6 %collective-permute-start.5 = (f32[32,2048]{1,0:T(8,128)S(1)}, f32[32,2048]{1,0:T(8,128)S(1)}, u32[]{:S(2)}, u32[]{:S(2)}) collective-permute-start(f32[32,2048]{1,0:T(8,128)S(1)} %pad_maximum_fusion), channel_id=1, source_target_pairs={{0,120},{8,0},{16,8},{24,16},{32,24},{40,32},{48,40},{56,48},{64,5... | collective-permute-start | bytes 786440 | tf_op jit(solution)/shard_map/ppermute | solution.py:592
  17.4 0.1 collective-permute-start.6
  17.5 0.6 select_dynamic-update-slice_fusion.1
  18.1 4.2 %collective-permute-done.5.below_ref = f32[32,2048]{1,0:T(8,128)S(1)} collective-permute-done((f32[32,2048]{1,0:T(8,128)S(1)}, f32[32,2048]{1,0:T(8,128)S(1)}, u32[]{:S(2)}, u32[]{:S(2)}) %collective-permute-start.5) | collective-permute-done | bytes 262176 | tf_op jit(solution)/shard_map/ppermute | solution.py:592
  22.4 0.6 constant_dynamic-update-slice_fusion.3
  23.0 4.7 %collective-permute-done.6.above_ref = f32[32,2048]{1,0:T(8,128)S(1)} collective-permute-done((f32[32,2048]{1,0:T(8,128)S(1)}, f32[32,2048]{1,0:T(8,128)S(1)}, u32[]{:S(2)}, u32[]{:S(2)}) %collective-permute-start.6) | collective-permute-done | bytes 262176 | tf_op jit(solution)/shard_map/ppermute | solution.py:592
  27.7 0.6 constant_dynamic-update-slice_fusion.2
  28.3 1.6 %select_dynamic-update-slice_fusion = f32[320,128]{1,0:T(8,128)} fusion(f32[320,128]{1,0:T(8,128)} %constant_dynamic-update-slice_fusion.2, f32[128,2048]{1,0:T(8,128)} %fw_ref, s32[128,2048]{1,0:T(8,128)} %holes_ref, pred[128]{0:T(512)(128)(4,1)S(1)} %iota_compare_fusion.1), kind=kLoop, calls=%fused_computation.7 | loop fusion | flops 65536 | bytes 327808
  29.8 0.6 constant_dynamic-update-slice_fusion.1
  30.4 0.0 collective-permute-done.got_ref
  30.4 0.0 copy-done.3
  30.4 0.0 copy-done.4
  30.5 3.9 %filter.1 = (f32[2176,128]{1,0:T(8,128)S(1)}, f32[272,128]{1,0:T(8,128)}, f32[272,128]{1,0:T(8,128)S(1)}, f32[128,128]{1,0:T(8,128)S(1)}) custom-call(s32[1]{0:T(128)} %slice.79.first_ref, f32[1536,128]{1,0:T(8,128)S(1)} %collective-permute-done.got_ref, f32[2048,128]{1,0:T(8,128)S(1)} %copy-done.3, f32[5,128,128]{2,1,0:T(8,128)S(1)} %copy-done.4), custom_call_target="tpu_custom_call" | custom-call | flops 1100000000 | bytes 3500000 | tf_op jit(solution)/shard_map/filter/pallas_call | solution.py:657
  34.4 1.0 %copy-done.6 = f32[2176,128]{1,0:T(8,128)} copy-done((f32[2176,128]{1,0:T(8,128)}, f32[2176,128]{1,0:T(8,128)S(1)}, u32[]{:S(2)}) %copy-start.6) | copy-done | bytes 1114136
  35.4 0.8 collective-permute-start.1
  36.3 0.6 collective-permute-start.2
  36.9 0.6 constant_dynamic-update-slice_fusion
  37.5 3.3 %collective-permute-start.7 = (f32[320,128]{1,0:T(8,128)}, f32[320,128]{1,0:T(8,128)S(1)}, u32[]{:S(2)}, u32[]{:S(2)}) collective-permute-start(f32[320,128]{1,0:T(8,128)} %constant_dynamic-update-slice_fusion), channel_id=1, source_target_pairs={{0,1},{1,2},{2,3},{3,4},{4,5},{5,6},{6,7},{7,0},{8,9},{9,10},{10,1... | collective-permute-start | bytes 491528 | tf_op jit(solution)/shard_map/ppermute | solution.py:592
  40.8 0.0 collective-permute-start.8
  40.8 0.0 collective-permute-done.1.below_ref
  40.8 2.7 %collective-permute-done.2.above_ref = f32[272,128]{1,0:T(8,128)S(1)} collective-permute-done((f32[272,128]{1,0:T(8,128)S(1)}, f32[272,128]{1,0:T(8,128)S(1)}, u32[]{:S(2)}, u32[]{:S(2)}) %collective-permute-start.2) | collective-permute-done | bytes 139296 | tf_op jit(solution)/shard_map/ppermute | solution.py:592
  43.5 0.2 corners.1
  43.7 4.0 %collective-permute-start.3 = (f32[168,128]{1,0:T(8,128)S(1)}, f32[168,128]{1,0:T(8,128)S(1)}, u32[]{:S(2)}, u32[]{:S(2)}) collective-permute-start(f32[168,128]{1,0:T(8,128)S(1)} %corners.1), channel_id=1, source_target_pairs={{0,1},{1,2},{2,3},{3,4},{4,5},{5,6},{6,7},{7,0},{8,9},{9,10},{10,1... | collective-permute-start | bytes 258056 | tf_op jit(solution)/shard_map/ppermute | solution.py:592
  47.7 0.0 collective-permute-start.4
  47.7 0.1 add_convert_fusion.ok_ref
  47.8 0.0 collective-permute-done.7.left_ref
  47.8 0.0 collective-permute-done.8.right_ref
  47.8 1.9 %rims.1 = (f32[672,128]{1,0:T(8,128)S(1)}, f32[672,128]{1,0:T(8,128)S(1)}) custom-call(s32[4]{0:T(128)S(1)} %add_convert_fusion.ok_ref, f32[32,2048]{1,0:T(8,128)S(1)} %collective-permute-done.5.below_ref, f32[32,2048]{1,0:T(8,128)S(1)} %collective-permute-done.6.above_ref, f32[320,128]{1,0:T(8,128)S(1)} %collective-permute-done.7.left_ref, ...), custom_call_target="tpu_custom_call" | custom-call | flops 500000 | bytes 1200000 | tf_op jit(solution)/shard_map/rims/pallas_call | solution.py:648
  49.8 0.0 collective-permute-done.3.left_ref
  49.8 3.1 %collective-permute-done.4.right_ref = f32[168,128]{1,0:T(8,128)S(1)} collective-permute-done((f32[168,128]{1,0:T(8,128)S(1)}, f32[168,128]{1,0:T(8,128)S(1)}, u32[]{:S(2)}, u32[]{:S(2)}) %collective-permute-start.4) | collective-permute-done | bytes 86048 | tf_op jit(solution)/shard_map/ppermute | solution.py:592
  52.9 0.0 copy-done.5
  52.9 1.2 %copy-done.7 = f32[2176,128]{1,0:T(8,128)S(1)} copy-done((f32[2176,128]{1,0:T(8,128)S(1)}, f32[2176,128]{1,0:T(8,128)}, u32[]{:S(2)}) %copy-start.7) | copy-done | bytes 1114136
  54.1 26.4 %solve.1 = (f32[2176,128]{1,0:T(8,128)S(1)}, f32[1536,128]{1,0:T(8,128)S(1)}, f32[2048,128]{1,0:T(8,128)S(1)}) custom-call(s32[4]{0:T(128)S(1)} %add_convert_fusion.ok_ref, s32[1]{0:T(128)} %slice.79.first_ref, f32[2176,128]{1,0:T(8,128)S(1)} %copy-done.7, f32[272,128]{1,0:T(8,128)S(1)} %collective-permute-done.1.below_ref, ...), custom_call_target="tpu_custom_call" | custom-call | flops 1400000000 | bytes 9000000 | tf_op jit(solution)/shard_map/solve/pallas_call | solution.py:680
  80.5 0.1 collective-permute-start.9
  81.3 3.0 %pressure.1 = f32[128,2048]{1,0:T(8,128)} custom-call(f32[2176,128]{1,0:T(8,128)S(1)} %get-tuple-element.41.p_ref), custom_call_target="tpu_custom_call" | custom-call | flops 2000000 | bytes 2100000 | tf_op jit(solution)/shard_map/pressure/pallas_call | solution.py:695
  84.3 9.8 %collective-permute-done.9 = f32[1536,128]{1,0:T(8,128)S(1)} collective-permute-done((f32[1536,128]{1,0:T(8,128)S(1)}, f32[1536,128]{1,0:T(8,128)S(1)}, u32[]{:S(2)}, u32[]{:S(2)}) %collective-permute-start.9) | collective-permute-done | bytes 786464 | tf_op jit(solution)/shard_map/ppermute | solution.py:592
  94.1 1.3 %pad_select_fusion = f32[2048,128]{1,0:T(8,128)} fusion(f32[2048,128]{1,0:T(8,128)S(1)} %get-tuple-element.42, f32[1536,128]{1,0:T(8,128)S(1)} %collective-permute-done.9, pred[2048]{0:T(1024)(128)(4,1)S(1)} %iota_compare_fusion), kind=kLoop, calls=%fused_computation | loop fusion | flops 262144 | bytes 2885632 | tf_op jit(solution)/shard_map/jit(_where)/select_n | solution.py:701
  (9 shorter events, 0.1 us)
Async XLA Ops:
  0.6 4.0 %copy-start = (f32[128,2048]{1,0:T(8,128)S(1)}, f32[128,2048]{1,0:T(8,128)}, u32[]{:S(2)}) copy-start(f32[128,2048]{1,0:T(8,128)} %sq_ref) | copy-start | bytes 3145732
  1.9 28.5 %collective-permute-start = (f32[1536,128]{1,0:T(8,128)S(1)}, f32[1536,128]{1,0:T(8,128)S(1)}, u32[]{:S(2)}, u32[]{:S(2)}) collective-permute-start(f32[1536,128]{1,0:T(8,128)S(1)} %slice.78), channel_id=1, source_target_pairs={{0,1},{1,2},{2,3},{3,4},{4,5},{5,6},{6,7},{7,8},{8,9},{9,10},{10,1... | collective-permute-start | bytes 2359304 | tf_op jit(solution)/shard_map/ppermute | solution.py:592
  4.7 1.2 %copy-start.1 = (f32[128,2048]{1,0:T(8,128)S(1)}, f32[128,2048]{1,0:T(8,128)}, u32[]{:S(2)}) copy-start(f32[128,2048]{1,0:T(8,128)} %fw_ref) | copy-start | bytes 3145732
  5.9 1.2 %copy-start.2 = (s32[128,2048]{1,0:T(8,128)S(1)}, s32[128,2048]{1,0:T(8,128)}, u32[]{:S(2)}) copy-start(s32[128,2048]{1,0:T(8,128)} %holes_ref) | copy-start | bytes 3145732
  12.7 17.7 %copy-start.3 = (f32[2048,128]{1,0:T(8,128)S(1)}, f32[2048,128]{1,0:T(8,128)}, u32[]{:S(2)}) copy-start(f32[2048,128]{1,0:T(8,128)} %own_ref.1) | copy-start | bytes 3145732
  12.7 17.7 %copy-start.4 = (f32[5,128,128]{2,1,0:T(8,128)S(1)}, f32[5,128,128]{2,1,0:T(8,128)}, u32[]{:S(2)}) copy-start(f32[5,128,128]{2,1,0:T(8,128)} %tiles_ref.3) | copy-start | bytes 983044
  12.8 9.6 %collective-permute-start.5 = (f32[32,2048]{1,0:T(8,128)S(1)}, f32[32,2048]{1,0:T(8,128)S(1)}, u32[]{:S(2)}, u32[]{:S(2)}) collective-permute-start(f32[32,2048]{1,0:T(8,128)S(1)} %pad_maximum_fusion), channel_id=1, source_target_pairs={{0,120},{8,0},{16,8},{24,16},{32,24},{40,32},{48,40},{56,48},{64,5... | collective-permute-start | bytes 786440 | tf_op jit(solution)/shard_map/ppermute | solution.py:592
  17.4 10.2 %collective-permute-start.6 = (f32[32,2048]{1,0:T(8,128)S(1)}, f32[32,2048]{1,0:T(8,128)S(1)}, u32[]{:S(2)}, u32[]{:S(2)}) collective-permute-start(f32[32,2048]{1,0:T(8,128)S(1)} %pad_maximum_fusion.1), channel_id=1, source_target_pairs={{0,8},{8,16},{16,24},{24,32},{32,40},{40,48},{48,56},{56,64},{64,7... | collective-permute-start | bytes 786440 | tf_op jit(solution)/shard_map/ppermute | solution.py:592
  34.4 1.0 %copy-start.6 = (f32[2176,128]{1,0:T(8,128)}, f32[2176,128]{1,0:T(8,128)S(1)}, u32[]{:S(2)}) copy-start(f32[2176,128]{1,0:T(8,128)S(1)} %get-tuple-element.30.dens_ref) | copy-start | bytes 3342340
  35.4 5.4 %collective-permute-start.1 = (f32[272,128]{1,0:T(8,128)}, f32[272,128]{1,0:T(8,128)S(1)}, u32[]{:S(2)}, u32[]{:S(2)}) collective-permute-start(f32[272,128]{1,0:T(8,128)} %get-tuple-element.31), channel_id=1, source_target_pairs={{0,120},{8,0},{16,8},{24,16},{32,24},{40,32},{48,40},{56,48},{64,5... | collective-permute-start | bytes 417800 | tf_op jit(solution)/shard_map/ppermute | solution.py:592
  36.3 7.2 %collective-permute-start.2 = (f32[272,128]{1,0:T(8,128)S(1)}, f32[272,128]{1,0:T(8,128)S(1)}, u32[]{:S(2)}, u32[]{:S(2)}) collective-permute-start(f32[272,128]{1,0:T(8,128)S(1)} %get-tuple-element.32), channel_id=1, source_target_pairs={{0,8},{8,16},{16,24},{24,32},{32,40},{40,48},{48,56},{56,64},{64,7... | collective-permute-start | bytes 417800 | tf_op jit(solution)/shard_map/ppermute | solution.py:592
  37.5 10.3 %collective-permute-start.7 = (f32[320,128]{1,0:T(8,128)}, f32[320,128]{1,0:T(8,128)S(1)}, u32[]{:S(2)}, u32[]{:S(2)}) collective-permute-start(f32[320,128]{1,0:T(8,128)} %constant_dynamic-update-slice_fusion), channel_id=1, source_target_pairs={{0,1},{1,2},{2,3},{3,4},{4,5},{5,6},{6,7},{7,0},{8,9},{9,10},{10,1... | collective-permute-start | bytes 491528 | tf_op jit(solution)/shard_map/ppermute | solution.py:592
  40.8 7.0 %collective-permute-start.8 = (f32[320,128]{1,0:T(8,128)}, f32[320,128]{1,0:T(8,128)S(1)}, u32[]{:S(2)}, u32[]{:S(2)}) collective-permute-start(f32[320,128]{1,0:T(8,128)} %constant_dynamic-update-slice_fusion), channel_id=1, source_target_pairs={{0,7},{1,0},{2,1},{3,2},{4,3},{5,4},{6,5},{7,6},{8,15},{9,8},{10,9... | collective-permute-start | bytes 491528 | tf_op jit(solution)/shard_map/ppermute | solution.py:592
  40.8 12.0 %copy-start.5 = (f32[5,128,128]{2,1,0:T(8,128)S(1)}, f32[5,128,128]{2,1,0:T(8,128)}, u32[]{:S(2)}) copy-start(f32[5,128,128]{2,1,0:T(8,128)} %tiles_ref.3) | copy-start | bytes 983044
  43.7 6.0 %collective-permute-start.3 = (f32[168,128]{1,0:T(8,128)S(1)}, f32[168,128]{1,0:T(8,128)S(1)}, u32[]{:S(2)}, u32[]{:S(2)}) collective-permute-start(f32[168,128]{1,0:T(8,128)S(1)} %corners.1), channel_id=1, source_target_pairs={{0,1},{1,2},{2,3},{3,4},{4,5},{5,6},{6,7},{7,0},{8,9},{9,10},{10,1... | collective-permute-start | bytes 258056 | tf_op jit(solution)/shard_map/ppermute | solution.py:592
  47.7 5.1 %collective-permute-start.4 = (f32[168,128]{1,0:T(8,128)S(1)}, f32[168,128]{1,0:T(8,128)S(1)}, u32[]{:S(2)}, u32[]{:S(2)}) collective-permute-start(f32[168,128]{1,0:T(8,128)S(1)} %corners.1), channel_id=1, source_target_pairs={{0,7},{1,0},{2,1},{3,2},{4,3},{5,4},{6,5},{7,6},{8,15},{9,8},{10,9... | collective-permute-start | bytes 258056 | tf_op jit(solution)/shard_map/ppermute | solution.py:592
  52.9 1.2 %copy-start.7 = (f32[2176,128]{1,0:T(8,128)S(1)}, f32[2176,128]{1,0:T(8,128)}, u32[]{:S(2)}) copy-start(f32[2176,128]{1,0:T(8,128)} %copy-done.6) | copy-start | bytes 3342340
  80.5 13.6 %collective-permute-start.9 = (f32[1536,128]{1,0:T(8,128)S(1)}, f32[1536,128]{1,0:T(8,128)S(1)}, u32[]{:S(2)}, u32[]{:S(2)}) collective-permute-start(f32[1536,128]{1,0:T(8,128)S(1)} %get-tuple-element.43), channel_id=1, source_target_pairs={{0,127},{1,0},{2,1},{3,2},{4,3},{5,4},{6,5},{7,6},{8,7},{9,8},{10,... | collective-permute-start | bytes 2359304 | tf_op jit(solution)/shard_map/ppermute | solution.py:592

commit v3 on v2

--- a/solution.py
+++ b/solution.py
@@ -9,7 +9,7 @@
 CHUNK = 3
 UNROLL = False
 MROWS = 512
-ROOM = (10, 16, 4, 34, 4, 4)
+ROOM = (10, 11, 4, 30, 4, 4)
 COND_FLOOR = 0.01
 SQUEEZE_DAMPING = 0.25
 
@@ -163,7 +163,22 @@
         store(column_of(i), vecs[i])
 
 
-def sources_kernel(sq_ref, fw_ref, holes_ref, out_sq, out_fw):
+def outer_columns(ref, rows):
+    return jnp.where(lane_ids() < 64, ref[rows, 0:128], ref[rows, 1920:2048])
+
+
+def sources_kernel(sq_ref, fw_ref, holes_ref, out_sq, out_fw, sides, edge_up, edge_down):
+    for edge, start in ((edge_up, 0), (edge_down, 112)):
+        for part in range(2):
+            rows = pl.ds(start + part * 8, 8)
+            edge[pl.ds(part * 8, 8), :] = sq_ref[rows, :]
+            edge[pl.ds(16 + part * 8, 8), :] = jnp.where(holes_ref[rows, :] > 0, 0.0, fw_ref[rows, :])
+    for brow in range(BROWS):
+        rows = pl.ds(brow * 8, 8)
+        sides[rows, :] = outer_columns(sq_ref, rows)
+        outer = jnp.where(outer_columns(holes_ref, rows) > 0, 0.0, outer_columns(fw_ref, rows))
+        sides[pl.ds(128 + brow * 8, 8), :] = outer
+
     def tile_rows(brow, carry):
         rows = pl.ds(pl.multiple_of(brow * 8, 8), 8)
 
@@ -184,10 +199,7 @@
     lax.fori_loop(0, BROWS, tile_rows, 0, unroll=2)
 
 
-def rims_kernel(ok_ref, below_ref, above_ref, left_ref, right_ref, out_sq, out_fw):
-    lane = lane_ids()
-    keep_right = (lane <= 16) & (ok_ref[3] > 0)
-    keep_left = (lane >= 111) & (ok_ref[2] > 0)
+def rims_kernel(ok_ref, below_ref, above_ref, sides_ref, out_sq, out_fw, out_sides):
     for field, out in ((0, out_sq), (1, out_fw)):
         for part in range(4):
             src = below_ref if part < 2 else above_ref
@@ -201,15 +213,9 @@
                 out[pl.ds(c * 32 + part * 8, 8), :] = x
 
             spread(load, store)
-        for block in range(20):
-            rows = pl.ds(field * 160 + block * 8, 8)
-            side = jnp.where(keep_right, right_ref[rows, :], jnp.where(keep_left, left_ref[rows, :], 0.0))
-            if block < 16:
-                out[pl.ds(RIMS + block, 8, stride=16), :] = side
-            else:
-                part = block - 16
-                ok = ok_ref[1] if part < 2 else ok_ref[0]
-                out[pl.ds(16 * 32 + part * 8, 8), :] = jnp.where(ok > 0, side, 0.0)
+            outer = jnp.where(ok > 0, outer_columns(src, rows), 0.0)
+            out_sides[pl.ds(field * 160 + 128 + part * 8, 8), :] = outer
+        out_sides[pl.ds(field * 160, 128), :] = sides_ref[pl.ds(field * 128, 128), :]
 
 
 def filter_kernel(first_ref, got_ref, own_ref, tiles_ref, dens_ref, up_ref, down_ref, cols_ref,
@@ -272,8 +278,9 @@
         cols_ref[pl.ds(a * 16, 16), :] = x
 
 
-def corner_kernel(below_ref, above_ref, cols_ref, out_ref):
+def corner_kernel(below_ref, above_ref, cols_ref, sides_ref, out_ref):
     out_ref[0:128, :] = cols_ref[...]
+    out_ref[168:488, :] = sides_ref[...]
     lane = lane_ids()
     sub = sub_ids()
     for part in range(5):
@@ -415,26 +422,38 @@
             return rim_row(s, part)
         return main_row(a, s, half)
 
+    def side_sources(a, half, part):
+        for field in range(2):
+            if part is None:
+                rows = pl.ds(168 + field * 160 + half * 64 + a, 8, stride=8)
+                ok = True
+            else:
+                rows = pl.ds(168 + field * 160 + 128 + part * 8, 8)
+                ok = down_ok if part < 2 else up_ok
+            x = jnp.where(lane < 64, right_ref[rows, :], left_ref[rows, :])
+            yield jnp.where((keep_right | keep_left) & ok, x, 0.0)
+
     def coefficients(a, half, part):
         ctr, north, south = group(k, 0, a, half) if part is None else rim_group(k, 0, part, far)
         east, west = east_west(ctr)
         for s in range(QS):
             row = row_of(a, half, part, s)
             rows = pl.ds(row if isinstance(row, int) else pl.multiple_of(row, 8), 8)
-            if part is not None:
-                source, sources = pl.ds(s * 32 + part * 8, 8), (sq_rim, fw_rim)
-            elif s == 16:
-                source, sources = rows_at(RIMS + a * 16 + half * 8), (sq_rim, fw_rim)
+            if s == 16:
+                source, weight = side_sources(a, half, part)
+            elif part is not None:
+                here = pl.ds(s * 32 + part * 8, 8)
+                source, weight = sq_rim[here, :], fw_rim[here, :]
             else:
-                source, sources = rows_at((a * 16 + s) * 16 + half * 8), (sq_ref, fw_ref)
+                here = rows_at((a * 16 + s) * 16 + half * 8)
+                source, weight = sq_ref[here, :], fw_ref[here, :]
             fn, fs, fe, fv = (0.5 * (ctr[s] + other[s]) for other in (north, south, east, west))
-            weight = sources[1][source, :]
             inv = jnp.where(weight > 0.0, 1.0, 0.0) / (fn + fs + fv + fe + SQUEEZE_DAMPING)
             wn[rows, :] = fn * inv
             ws[rows, :] = fs * inv
             we[rows, :] = fe * inv
             ww[rows, :] = fv * inv
-            first_p = sources[0][source, :] * inv
+            first_p = source * inv
             first_a = weight * inv
             bp[rows, :] = first_p
             ba[rows, :] = first_a
@@ -616,43 +635,15 @@
         (design[SLOTS - SENT:], holes, squeeze_source, force_weight)
     )
     got = moved(tail, OWNERS, 1)
-    sq, fw = pl.pallas_call(
+    sq, fw, sides, edge_up, edge_down = pl.pallas_call(
         sources_kernel,
-        out_shape=(f32(SLOTS, 128), f32(SLOTS, 128)),
+        out_shape=(f32(SLOTS, 128), f32(SLOTS, 128), f32(256, 128), f32(32, 2048), f32(32, 2048)),
         compiler_params=room(ROOM[0]),
-        cost_estimate=work(2000000, 5000000),
+        cost_estimate=work(2000000, 5500000),
         name="sources",
     )(squeeze_source, force_weight, holes)
-    sq, fw, first, holes, squeeze_source, force_weight = lax.optimization_barrier(
-        (sq, fw, first, holes, squeeze_source, force_weight)
-    )
-
-    def edge_rows(rows):
-        weight = jnp.where(holes[rows] > 0, 0.0, force_weight[rows])
-        return jnp.concatenate([squeeze_source[rows], weight], axis=0)
-
-    below = moved(edge_rows(slice(0, 16)), "wide", -1)
-    above = moved(edge_rows(slice(112, 128)), "wide", 1)
-
-    def ends(x):
-        lane = lax.broadcasted_iota(jnp.int32, (1, 128), 1)
-        return jnp.where(lane < 64, x[:, :128], x[:, -128:])
-
-    masked = jnp.where(ends(holes) > 0, 0.0, ends(force_weight))
-    sides = jnp.concatenate([
-        ends(squeeze_source), ends(below[:16]), ends(above[:16]),
-        masked, ends(below[16:]), ends(above[16:]),
-    ], axis=0)
-    right = moved(sides, "narrow", -1)
-    left = moved(sides, "narrow", 1)
-    sq_rim, fw_rim = pl.pallas_call(
-        rims_kernel,
-        out_shape=(f32(RIMS + 128, 128), f32(RIMS + 128, 128)),
-        in_specs=[smem] + [vmem] * 4,
-        compiler_params=room(ROOM[5]),
-        cost_estimate=work(500000, 1200000),
-        name="rims",
-    )(inside, below, above, left, right)
+    below = moved(edge_up, "wide", -1)
+    above = moved(edge_down, "wide", 1)
 
     dens, up, down, cols = pl.pallas_call(
         filter_kernel,
@@ -670,9 +661,19 @@
     )(first, got, design, filter_tiles)
     d_below = moved(up, "wide", -1)
     d_above = moved(down, "wide", 1)
+    below, above, cols = lax.optimization_barrier((below, above, cols))
+    sq_rim, fw_rim, sides = pl.pallas_call(
+        rims_kernel,
+        out_shape=(f32(512, 128), f32(512, 128), f32(320, 128)),
+        in_specs=[smem] + [vmem] * 3,
+        compiler_params=room(ROOM[5]),
+        cost_estimate=work(500000, 1200000),
+        name="rims",
+    )(inside, below, above, sides)
     d_sides = pl.pallas_call(
-        corner_kernel, out_shape=f32(168, 128), compiler_params=room(ROOM[2]), cost_estimate=work(200000, 500000), name="corners",
-    )(d_below, d_above, cols)
+        corner_kernel, out_shape=f32(488, 128), compiler_params=room(ROOM[2]),
+        cost_estimate=work(200000, 700000), name="corners",
+    )(d_below, d_above, cols, sides)
     d_right = moved(d_sides, "narrow", -1)
     d_left = moved(d_sides, "narrow", 1)
 

time: 95.8 us -> 86.6 us (0.904)
  other arithmetic: 7.21 us -> 1.4 us
  waiting for transfers between devices: 24.5 us -> 22.1 us
  local copies, waits for them, and re-layouts: 7.29 us -> 6.02 us
    unnamed x5 -> x0, other arithmetic: 4.02 us -> none
    ppermute x10 -> x8, waiting for transfers between devices: 24.5 us -> 22.1 us  [moved(): lax.ppermute(x, axis, [(i, (i + by) % length) for i in range(length)])]
    unnamed x16 -> x14, local copies, waits for them, and re-layouts: 4.75 us -> 3.48 us
    select_n x1 -> x0, other arithmetic: 1.15 us -> none  [edge_rows(): weight = jnp.where(holes[rows] > 0, 0.0, force_weight[rows])]
    ppermute x10 -> x8, starting transfers between devices: 15.1 us -> 14.8 us  [moved(): lax.ppermute(x, axis, [(i, (i + by) % length) for i in range(length)])]
  transfers between devices with their start and end apart: 10 -> 8, of which waited for: 5 -> 5; matrix products, arithmetic and copies ran while one was open for 7% -> 2% of each run, Pallas kernels for 10% -> 16%
where the time goes in v3:
time: 86.6 us; the launch traced here: 86.3 us
  Pallas kernels  40.7 us (47%)
  waiting for transfers between devices  22.1 us (26%)
  starting transfers between devices  14.8 us (17%)
  local copies, waits for them, and re-layouts  6.02 us (7%)
  other arithmetic  1.4 us (2%)
  between operations  1.39 us (2%)
    pallas_call x1, Pallas kernels, local(): pl.pallas_call(solve_kernel, out_shape=(f32(MAIN, 128), f32(SENT, 128), f...  26.6 us
    ppermute x8, waiting for transfers between devices, moved(): lax.ppermute(x, axis, [(i, (i + by) % length) for i in range(length)])  22.1 us
    ppermute x8, starting transfers between devices, moved(): lax.ppermute(x, axis, [(i, (i + by) % length) for i in range(length)])  14.8 us
    pallas_call x1, Pallas kernels, local(): pl.pallas_call(sources_kernel, out_shape=(f32(SLOTS, 128), f32(SLOTS, 128...  4.91 us
    pallas_call x1, Pallas kernels, local(): pl.pallas_call(filter_kernel, out_shape=(f32(MAIN, 128), f32(272, 128), f...  4.02 us
    unnamed x14, local copies, waits for them, and re-layouts  3.48 us
    pallas_call x1, Pallas kernels, local(): pl.pallas_call(pressure_kernel, out_shape=f32(128, 2048), compiler_params...  3.03 us
    pallas_call x1, Pallas kernels, local(): pl.pallas_call(rims_kernel, out_shape=(f32(512, 128), f32(512, 128), f32(...  1.92 us
  transfers between devices with their start and end apart: 8, of which 5 were waited for; matrix products, arithmetic and copies ran while one was open for 2% of the time, Pallas kernels for 16%

profile of v3, /device:TPU:25, one launch (start us, length us, event | category | flops | bytes accessed | tf_op | source)
XLA Modules:
  0.0 86.3 jit_solution(13854868382443929394)
XLA Ops:
  0.6 0.0 copy-start
  0.6 1.3 %slice.7 = f32[1536,128]{1,0:T(8,128)S(1)} slice(f32[2048,128]{1,0:T(8,128)} %own_ref.1), slice={[512:2048], [0:128]} | slice | bytes 1572864 | tf_op jit(solution)/shard_map/slice | solution.py:635
  1.9 1.5 %collective-permute-start = (f32[1536,128]{1,0:T(8,128)S(1)}, f32[1536,128]{1,0:T(8,128)S(1)}, u32[]{:S(2)}, u32[]{:S(2)}) collective-permute-start(f32[1536,128]{1,0:T(8,128)S(1)} %slice.7), channel_id=1, source_target_pairs={{0,1},{1,2},{2,3},{3,4},{4,5},{5,6},{6,7},{7,8},{8,9},{9,10},{10,1... | collective-permute-start | bytes 2359304 | tf_op jit(solution)/shard_map/ppermute | solution.py:611
  3.4 0.0 copy-done
  3.4 0.0 copy-start.1
  3.4 1.2 %copy-done.1 = f32[128,2048]{1,0:T(8,128)S(1)} copy-done((f32[128,2048]{1,0:T(8,128)S(1)}, f32[128,2048]{1,0:T(8,128)}, u32[]{:S(2)}) %copy-start.1) | copy-done | bytes 1048600
  4.6 0.0 copy-start.2
  4.6 1.2 %copy-done.2 = s32[128,2048]{1,0:T(8,128)S(1)} copy-done((s32[128,2048]{1,0:T(8,128)S(1)}, s32[128,2048]{1,0:T(8,128)}, u32[]{:S(2)}) %copy-start.2) | copy-done | bytes 1048600
  5.9 0.0 copy-start.3
  5.9 0.0 copy-start.4
  5.9 4.9 %sources.1 = (f32[2048,128]{1,0:T(8,128)S(1)}, f32[2048,128]{1,0:T(8,128)S(1)}, f32[256,128]{1,0:T(8,128)S(1)}, f32[32,2048]{1,0:T(8,128)}, f32[32,2048]{1,0:T(8,128)}) custom-call(f32[128,2048]{1,0:T(8,128)S(1)} %copy-done, f32[128,2048]{1,0:T(8,128)S(1)} %copy-done.1, s32[128,2048]{1,0:T(8,128)S(1)} %copy-done.2), custom_call_target="tpu_custom_call" | custom-call | flops 2000000 | bytes 5500000 | tf_op jit(solution)/shard_map/sources/pallas_call | solution.py:638
  10.8 4.6 %collective-permute-start.3 = (f32[32,2048]{1,0:T(8,128)}, f32[32,2048]{1,0:T(8,128)S(1)}, u32[]{:S(2)}, u32[]{:S(2)}) collective-permute-start(f32[32,2048]{1,0:T(8,128)} %get-tuple-element.31), channel_id=1, source_target_pairs={{0,120},{8,0},{16,8},{24,16},{32,24},{40,32},{48,40},{56,48},{64,5... | collective-permute-start | bytes 786440 | tf_op jit(solution)/shard_map/ppermute | solution.py:611
  15.4 0.0 collective-permute-start.4
  15.4 1.3 %slice.6.first_ref = s32[1]{0:T(128)} slice(s32[2048]{0:T(1024)} %param.9), slice={[0:1]} | slice | bytes 8 | tf_op jit(solution)/shard_map/slice | solution.py:633
  16.7 0.0 collective-permute-done.got_ref
  16.7 0.0 copy-done.3
  16.7 0.0 copy-done.4
  16.7 4.0 %filter.1 = (f32[2176,128]{1,0:T(8,128)S(1)}, f32[272,128]{1,0:T(8,128)}, f32[272,128]{1,0:T(8,128)}, f32[128,128]{1,0:T(8,128)S(1)}) custom-call(s32[1]{0:T(128)} %slice.6.first_ref, f32[1536,128]{1,0:T(8,128)S(1)} %collective-permute-done.got_ref, f32[2048,128]{1,0:T(8,128)S(1)} %copy-done.3, f32[5,128,128]{2,1,0:T(8,128)S(1)} %copy-done.4), custom_call_target="tpu_custom_call" | custom-call | flops 1100000000 | bytes 3500000 | tf_op jit(solution)/shard_map/filter/pallas_call | solution.py:648
  20.7 0.0 copy-start.5
  20.7 1.0 %copy-done.5 = f32[2176,128]{1,0:T(8,128)} copy-done((f32[2176,128]{1,0:T(8,128)}, f32[2176,128]{1,0:T(8,128)S(1)}, u32[]{:S(2)}) %copy-start.5) | copy-done | bytes 1114136
  21.7 4.8 %collective-permute-start.1 = (f32[272,128]{1,0:T(8,128)}, f32[272,128]{1,0:T(8,128)S(1)}, u32[]{:S(2)}, u32[]{:S(2)}) collective-permute-start(f32[272,128]{1,0:T(8,128)} %get-tuple-element.26), channel_id=1, source_target_pairs={{0,120},{8,0},{16,8},{24,16},{32,24},{40,32},{48,40},{56,48},{64,5... | collective-permute-start | bytes 417800 | tf_op jit(solution)/shard_map/ppermute | solution.py:611
  26.5 0.0 collective-permute-start.2
  26.5 0.0 copy-start.6
  26.5 0.1 add_convert_fusion.ok_ref
  26.6 0.0 collective-permute-done.3.below_ref
  26.6 0.0 collective-permute-done.4.above_ref
  26.6 1.9 %rims.1 = (f32[512,128]{1,0:T(8,128)S(1)}, f32[512,128]{1,0:T(8,128)S(1)}, f32[320,128]{1,0:T(8,128)S(1)}) custom-call(s32[4]{0:T(128)S(1)} %add_convert_fusion.ok_ref, f32[32,2048]{1,0:T(8,128)S(1)} %collective-permute-done.3.below_ref, f32[32,2048]{1,0:T(8,128)S(1)} %collective-permute-done.4.above_ref, f32[256,128]{1,0:T(8,128)S(1)} %get-tuple-element.37.sides_ref), custom_call_target="tpu_custom_call" | custom-call | flops 500000 | bytes 1200000 | tf_op jit(solution)/shard_map/rims/pallas_call | solution.py:665
  28.5 0.3 collective-permute-done.1.below_ref
  28.9 5.1 %collective-permute-done.2.above_ref = f32[272,128]{1,0:T(8,128)S(1)} collective-permute-done((f32[272,128]{1,0:T(8,128)}, f32[272,128]{1,0:T(8,128)S(1)}, u32[]{:S(2)}, u32[]{:S(2)}) %collective-permute-start.2) | collective-permute-done | bytes 139296 | tf_op jit(solution)/shard_map/ppermute | solution.py:611
  34.0 0.2 corners.1
  34.2 3.8 %collective-permute-start.5 = (f32[488,128]{1,0:T(8,128)S(1)}, f32[488,128]{1,0:T(8,128)S(1)}, u32[]{:S(2)}, u32[]{:S(2)}) collective-permute-start(f32[488,128]{1,0:T(8,128)S(1)} %corners.1), channel_id=1, source_target_pairs={{0,1},{1,2},{2,3},{3,4},{4,5},{5,6},{6,7},{7,0},{8,9},{9,10},{10,1... | collective-permute-start | bytes 749576 | tf_op jit(solution)/shard_map/ppermute | solution.py:611
  38.0 0.0 collective-permute-start.6
  38.0 3.2 %collective-permute-done.5.left_ref = f32[488,128]{1,0:T(8,128)S(1)} collective-permute-done((f32[488,128]{1,0:T(8,128)S(1)}, f32[488,128]{1,0:T(8,128)S(1)}, u32[]{:S(2)}, u32[]{:S(2)}) %collective-permute-start.5) | collective-permute-done | bytes 249888 | tf_op jit(solution)/shard_map/ppermute | solution.py:611
  41.2 3.7 %collective-permute-done.6.right_ref = f32[488,128]{1,0:T(8,128)S(1)} collective-permute-done((f32[488,128]{1,0:T(8,128)S(1)}, f32[488,128]{1,0:T(8,128)S(1)}, u32[]{:S(2)}, u32[]{:S(2)}) %collective-permute-start.6) | collective-permute-done | bytes 249888 | tf_op jit(solution)/shard_map/ppermute | solution.py:611
  44.8 0.0 copy-done.6
  44.8 26.6 %solve.1 = (f32[2176,128]{1,0:T(8,128)S(1)}, f32[1536,128]{1,0:T(8,128)S(1)}, f32[2048,128]{1,0:T(8,128)S(1)}) custom-call(s32[4]{0:T(128)S(1)} %add_convert_fusion.ok_ref, s32[1]{0:T(128)} %slice.6.first_ref, f32[2176,128]{1,0:T(8,128)S(1)} %copy-done.6, f32[272,128]{1,0:T(8,128)S(1)} %collective-permute-done.1.below_ref, ...), custom_call_target="tpu_custom_call" | custom-call | flops 1400000000 | bytes 9000000 | tf_op jit(solution)/shard_map/solve/pallas_call | solution.py:681
  71.4 0.1 collective-permute-start.7
  72.2 3.0 %pressure.1 = f32[128,2048]{1,0:T(8,128)} custom-call(f32[2176,128]{1,0:T(8,128)S(1)} %get-tuple-element.43.p_ref), custom_call_target="tpu_custom_call" | custom-call | flops 2000000 | bytes 2100000 | tf_op jit(solution)/shard_map/pressure/pallas_call | solution.py:696
  75.2 9.8 %collective-permute-done.7 = f32[1536,128]{1,0:T(8,128)S(1)} collective-permute-done((f32[1536,128]{1,0:T(8,128)S(1)}, f32[1536,128]{1,0:T(8,128)S(1)}, u32[]{:S(2)}, u32[]{:S(2)}) %collective-permute-start.7) | collective-permute-done | bytes 786464 | tf_op jit(solution)/shard_map/ppermute | solution.py:611
  85.0 1.3 %pad_select_fusion = f32[2048,128]{1,0:T(8,128)} fusion(f32[2048,128]{1,0:T(8,128)S(1)} %get-tuple-element.44, f32[1536,128]{1,0:T(8,128)S(1)} %collective-permute-done.7, pred[2048]{0:T(1024)(128)(4,1)S(1)} %iota_compare_fusion), kind=kLoop, calls=%fused_computation | loop fusion | flops 262144 | bytes 2885632 | tf_op jit(solution)/shard_map/jit(_where)/select_n | solution.py:702
  (1 shorter events, 0.0 us)
Async XLA Ops:
  0.6 2.8 %copy-start = (f32[128,2048]{1,0:T(8,128)S(1)}, f32[128,2048]{1,0:T(8,128)}, u32[]{:S(2)}) copy-start(f32[128,2048]{1,0:T(8,128)} %sq_ref) | copy-start | bytes 3145732
  1.9 14.8 %collective-permute-start = (f32[1536,128]{1,0:T(8,128)S(1)}, f32[1536,128]{1,0:T(8,128)S(1)}, u32[]{:S(2)}, u32[]{:S(2)}) collective-permute-start(f32[1536,128]{1,0:T(8,128)S(1)} %slice.7), channel_id=1, source_target_pairs={{0,1},{1,2},{2,3},{3,4},{4,5},{5,6},{6,7},{7,8},{8,9},{9,10},{10,1... | collective-permute-start | bytes 2359304 | tf_op jit(solution)/shard_map/ppermute | solution.py:611
  3.4 1.2 %copy-start.1 = (f32[128,2048]{1,0:T(8,128)S(1)}, f32[128,2048]{1,0:T(8,128)}, u32[]{:S(2)}) copy-start(f32[128,2048]{1,0:T(8,128)} %fw_ref) | copy-start | bytes 3145732
  4.6 1.2 %copy-start.2 = (s32[128,2048]{1,0:T(8,128)S(1)}, s32[128,2048]{1,0:T(8,128)}, u32[]{:S(2)}) copy-start(s32[128,2048]{1,0:T(8,128)} %holes_ref) | copy-start | bytes 3145732
  5.9 10.8 %copy-start.3 = (f32[2048,128]{1,0:T(8,128)S(1)}, f32[2048,128]{1,0:T(8,128)}, u32[]{:S(2)}) copy-start(f32[2048,128]{1,0:T(8,128)} %own_ref.1) | copy-start | bytes 3145732
  5.9 10.8 %copy-start.4 = (f32[5,128,128]{2,1,0:T(8,128)S(1)}, f32[5,128,128]{2,1,0:T(8,128)}, u32[]{:S(2)}) copy-start(f32[5,128,128]{2,1,0:T(8,128)} %tiles_ref.3) | copy-start | bytes 983044
  10.8 15.8 %collective-permute-start.3 = (f32[32,2048]{1,0:T(8,128)}, f32[32,2048]{1,0:T(8,128)S(1)}, u32[]{:S(2)}, u32[]{:S(2)}) collective-permute-start(f32[32,2048]{1,0:T(8,128)} %get-tuple-element.31), channel_id=1, source_target_pairs={{0,120},{8,0},{16,8},{24,16},{32,24},{40,32},{48,40},{56,48},{64,5... | collective-permute-start | bytes 786440 | tf_op jit(solution)/shard_map/ppermute | solution.py:611
  15.4 11.2 %collective-permute-start.4 = (f32[32,2048]{1,0:T(8,128)}, f32[32,2048]{1,0:T(8,128)S(1)}, u32[]{:S(2)}, u32[]{:S(2)}) collective-permute-start(f32[32,2048]{1,0:T(8,128)} %get-tuple-element.32), channel_id=1, source_target_pairs={{0,8},{8,16},{16,24},{24,32},{32,40},{40,48},{48,56},{56,64},{64,7... | collective-permute-start | bytes 786440 | tf_op jit(solution)/shard_map/ppermute | solution.py:611
  20.7 1.0 %copy-start.5 = (f32[2176,128]{1,0:T(8,128)}, f32[2176,128]{1,0:T(8,128)S(1)}, u32[]{:S(2)}) copy-start(f32[2176,128]{1,0:T(8,128)S(1)} %get-tuple-element.25.dens_ref) | copy-start | bytes 3342340
  21.7 7.1 %collective-permute-start.1 = (f32[272,128]{1,0:T(8,128)}, f32[272,128]{1,0:T(8,128)S(1)}, u32[]{:S(2)}, u32[]{:S(2)}) collective-permute-start(f32[272,128]{1,0:T(8,128)} %get-tuple-element.26), channel_id=1, source_target_pairs={{0,120},{8,0},{16,8},{24,16},{32,24},{40,32},{48,40},{56,48},{64,5... | collective-permute-start | bytes 417800 | tf_op jit(solution)/shard_map/ppermute | solution.py:611
  26.5 7.4 %collective-permute-start.2 = (f32[272,128]{1,0:T(8,128)}, f32[272,128]{1,0:T(8,128)S(1)}, u32[]{:S(2)}, u32[]{:S(2)}) collective-permute-start(f32[272,128]{1,0:T(8,128)} %get-tuple-element.27), channel_id=1, source_target_pairs={{0,8},{8,16},{16,24},{24,32},{32,40},{40,48},{48,56},{56,64},{64,7... | collective-permute-start | bytes 417800 | tf_op jit(solution)/shard_map/ppermute | solution.py:611
  26.5 18.3 %copy-start.6 = (f32[2176,128]{1,0:T(8,128)S(1)}, f32[2176,128]{1,0:T(8,128)}, u32[]{:S(2)}) copy-start(f32[2176,128]{1,0:T(8,128)} %copy-done.5) | copy-start | bytes 3342340
  34.2 7.0 %collective-permute-start.5 = (f32[488,128]{1,0:T(8,128)S(1)}, f32[488,128]{1,0:T(8,128)S(1)}, u32[]{:S(2)}, u32[]{:S(2)}) collective-permute-start(f32[488,128]{1,0:T(8,128)S(1)} %corners.1), channel_id=1, source_target_pairs={{0,1},{1,2},{2,3},{3,4},{4,5},{5,6},{6,7},{7,0},{8,9},{9,10},{10,1... | collective-permute-start | bytes 749576 | tf_op jit(solution)/shard_map/ppermute | solution.py:611
  38.0 6.9 %collective-permute-start.6 = (f32[488,128]{1,0:T(8,128)S(1)}, f32[488,128]{1,0:T(8,128)S(1)}, u32[]{:S(2)}, u32[]{:S(2)}) collective-permute-start(f32[488,128]{1,0:T(8,128)S(1)} %corners.1), channel_id=1, source_target_pairs={{0,7},{1,0},{2,1},{3,2},{4,3},{5,4},{6,5},{7,6},{8,15},{9,8},{10,9... | collective-permute-start | bytes 749576 | tf_op jit(solution)/shard_map/ppermute | solution.py:611
  71.4 13.6 %collective-permute-start.7 = (f32[1536,128]{1,0:T(8,128)S(1)}, f32[1536,128]{1,0:T(8,128)S(1)}, u32[]{:S(2)}, u32[]{:S(2)}) collective-permute-start(f32[1536,128]{1,0:T(8,128)S(1)} %get-tuple-element.45), channel_id=1, source_target_pairs={{0,127},{1,0},{2,1},{3,2},{4,3},{5,4},{6,5},{7,6},{8,7},{9,8},{10,... | collective-permute-start | bytes 2359304 | tf_op jit(solution)/shard_map/ppermute | solution.py:611

commit v4 on v3

--- a/solution.py
+++ b/solution.py
@@ -167,39 +167,50 @@
     return jnp.where(lane_ids() < 64, ref[rows, 0:128], ref[rows, 1920:2048])
 
 
-def sources_kernel(sq_ref, fw_ref, holes_ref, out_sq, out_fw, sides, edge_up, edge_down):
+def sources_kernel(sq_hbm, fw_hbm, holes_hbm, out_sq, out_fw, sides, edge_up, edge_down,
+                   sq_ref, fw_ref, holes_ref, sems):
+    copies = []
+    for piece in range(4):
+        rows = pl.ds(piece * 32, 32)
+        copies.append([
+            pltpu.make_async_copy(src.at[rows, :], dst.at[rows, :], sems.at[piece, i])
+            for i, (src, dst) in enumerate(((sq_hbm, sq_ref), (fw_hbm, fw_ref), (holes_hbm, holes_ref)))
+        ])
+        for copy in copies[-1]:
+            copy.start()
+
+    def tile_rows(brow, carry):
+        rows = pl.ds(pl.multiple_of(brow * 8, 8), 8)
+
+        def masked(v):
+            cols = pl.ds(v * 128, 128)
+            return jnp.where(holes_ref[rows, cols] > 0, 0.0, fw_ref[rows, cols])
+
+        def put(ref):
+            def store(c, x):
+                ref[pl.ds(c * 16 + brow, 8, stride=256), :] = x
+
+            return store
+
+        spread(lambda v: sq_ref[rows, pl.ds(v * 128, 128)], put(out_sq))
+        spread(masked, put(out_fw))
+        sides[rows, :] = outer_columns(sq_ref, rows)
+        outer = jnp.where(outer_columns(holes_ref, rows) > 0, 0.0, outer_columns(fw_ref, rows))
+        sides[pl.ds(pl.multiple_of(128 + brow * 8, 8), 8), :] = outer
+        return carry
+
+    for piece in range(4):
+        for copy in copies[piece]:
+            copy.wait()
+        lax.fori_loop(piece * 4, piece * 4 + 4, tile_rows, 0, unroll=2)
     for edge, start in ((edge_up, 0), (edge_down, 112)):
         for part in range(2):
             rows = pl.ds(start + part * 8, 8)
             edge[pl.ds(part * 8, 8), :] = sq_ref[rows, :]
             edge[pl.ds(16 + part * 8, 8), :] = jnp.where(holes_ref[rows, :] > 0, 0.0, fw_ref[rows, :])
-    for brow in range(BROWS):
-        rows = pl.ds(brow * 8, 8)
-        sides[rows, :] = outer_columns(sq_ref, rows)
-        outer = jnp.where(outer_columns(holes_ref, rows) > 0, 0.0, outer_columns(fw_ref, rows))
-        sides[pl.ds(128 + brow * 8, 8), :] = outer
-
-    def tile_rows(brow, carry):
-        rows = pl.ds(pl.multiple_of(brow * 8, 8), 8)
-
-        def masked(v):
-            cols = pl.ds(v * 128, 128)
-            return jnp.where(holes_ref[rows, cols] > 0, 0.0, fw_ref[rows, cols])
-
-        def put(ref):
-            def store(c, x):
-                ref[pl.ds(c * 16 + brow, 8, stride=256), :] = x
-
-            return store
-
-        spread(lambda v: sq_ref[rows, pl.ds(v * 128, 128)], put(out_sq))
-        spread(masked, put(out_fw))
-        return carry
-
-    lax.fori_loop(0, BROWS, tile_rows, 0, unroll=2)
-
-
-def rims_kernel(ok_ref, below_ref, above_ref, sides_ref, out_sq, out_fw, out_sides):
+
+
+def rims_kernel(ok_ref, below_ref, above_ref, sides_ref, dens_ref, out_sq, out_fw, out_sides, out_dens):
     for field, out in ((0, out_sq), (1, out_fw)):
         for part in range(4):
             src = below_ref if part < 2 else above_ref
@@ -216,16 +227,20 @@
             outer = jnp.where(ok > 0, outer_columns(src, rows), 0.0)
             out_sides[pl.ds(field * 160 + 128 + part * 8, 8), :] = outer
         out_sides[pl.ds(field * 160, 128), :] = sides_ref[pl.ds(field * 128, 128), :]
+    out_dens[...] = dens_ref[...]
 
 
 def filter_kernel(first_ref, got_ref, own_ref, tiles_ref, dens_ref, up_ref, down_ref, cols_ref,
-                  slots, parts, prod, edge):
+                  slots, parts, prod, edge, first_block, sem):
+    fetch = pltpu.make_async_copy(first_ref, first_block, sem)
+    fetch.start()
     tiles = [tiles_ref[i].T for i in range(5)]
     inverse = inverse_denoms([jnp.sum(t, axis=0, keepdims=True) for t in tiles])
     weights = stacked(jnp.concatenate(tiles, axis=1))
-    offset = curve_offset(first_ref[0])
     slots[pl.ds(0, SENT), :] = got_ref[...]
     slots[pl.ds(SENT, SLOTS), :] = own_ref[...]
+    fetch.wait()
+    offset = curve_offset(first_block[0])
     for brow in range(BROWS):
         x = jnp.concatenate(
             [slots[pl.ds(offset + inner_place(brow, g), 8, stride=256), :] for g in range(16)], axis=0
@@ -310,7 +325,9 @@
 
 def solve_kernel(ok_ref, first_ref, dens_ref, below_ref, above_ref, left_ref, right_ref, sq_ref, fw_ref,
                  sq_rim, fw_rim, tiles_ref, p_out, back_ref, keep_ref,
-                 k, far, wn, ws, we, ww, bp, ba, p0, p1, a0, a1, parts, prod, slots):
+                 k, far, wn, ws, we, ww, bp, ba, p0, p1, a0, a1, parts, prod, slots, first_block, sem):
+    fetch = pltpu.make_async_copy(first_ref, first_block, sem)
+    fetch.start()
     lane = lane_ids()
     sub = sub_ids()
     up_ok, down_ok, left_ok, right_ok = (ok_ref[i] > 0 for i in range(4))
@@ -577,7 +594,8 @@
     def piece(i, brow):
         return lambda g: prod[pl.ds(brow * 128 + g * 8, 8), pl.ds(i * 128, 128)]
 
-    offset = curve_offset(first_ref[0])
+    fetch.wait()
+    offset = curve_offset(first_block[0])
     for brow in range(BROWS):
         for g in range(16):
             x = piece(0, brow)(g)
@@ -626,11 +644,11 @@
 def local(design, filter_tiles, filter_cols, slot_block, holes, squeeze_source, force_weight):
     smem = pl.BlockSpec(memory_space=pltpu.SMEM)
     vmem = pl.BlockSpec(memory_space=pltpu.VMEM)
+    hbm = pl.BlockSpec(memory_space=pltpu.HBM)
     wide, narrow = lax.axis_index("wide"), lax.axis_index("narrow")
     inside = jnp.stack([
         wide > 0, wide < lax.axis_size("wide") - 1, narrow > 0, narrow < lax.axis_size("narrow") - 1,
     ]).astype(jnp.int32)
-    first = slot_block[0:1]
     tail, holes, squeeze_source, force_weight = lax.optimization_barrier(
         (design[SLOTS - SENT:], holes, squeeze_source, force_weight)
     )
@@ -638,38 +656,47 @@
     sq, fw, sides, edge_up, edge_down = pl.pallas_call(
         sources_kernel,
         out_shape=(f32(SLOTS, 128), f32(SLOTS, 128), f32(256, 128), f32(32, 2048), f32(32, 2048)),
+        in_specs=[hbm] * 3,
+        scratch_shapes=[
+            pltpu.VMEM((128, 2048), jnp.float32),
+            pltpu.VMEM((128, 2048), jnp.float32),
+            pltpu.VMEM((128, 2048), jnp.int32),
+            pltpu.SemaphoreType.DMA((4, 3)),
+        ],
         compiler_params=room(ROOM[0]),
         cost_estimate=work(2000000, 5500000),
         name="sources",
-    )(squeeze_source, force_weight, holes)
+    )(*(pltpu.with_memory_space_constraint(x, pltpu.HBM) for x in (squeeze_source, force_weight, holes)))
     below = moved(edge_up, "wide", -1)
     above = moved(edge_down, "wide", 1)
 
     dens, up, down, cols = pl.pallas_call(
         filter_kernel,
         out_shape=(f32(MAIN, 128), f32(272, 128), f32(272, 128), f32(128, 128)),
-        in_specs=[smem, vmem, vmem, vmem],
+        in_specs=[hbm, vmem, vmem, vmem],
         scratch_shapes=[
             pltpu.VMEM((SENT + SLOTS, 128), jnp.float32),
             pltpu.VMEM((SLOTS, 384), jnp.bfloat16),
             pltpu.VMEM((SLOTS, 640), jnp.float32),
             pltpu.VMEM((64, 128), jnp.float32),
+            pltpu.SMEM((SLOTS,), jnp.int32),
+            pltpu.SemaphoreType.DMA,
         ],
         compiler_params=room(ROOM[1]),
         cost_estimate=work(1100000000, 3500000),
         name="filter",
-    )(first, got, design, filter_tiles)
+    )(slot_block, got, design, filter_tiles)
     d_below = moved(up, "wide", -1)
     d_above = moved(down, "wide", 1)
     below, above, cols = lax.optimization_barrier((below, above, cols))
-    sq_rim, fw_rim, sides = pl.pallas_call(
+    sq_rim, fw_rim, sides, dens = pl.pallas_call(
         rims_kernel,
-        out_shape=(f32(512, 128), f32(512, 128), f32(320, 128)),
-        in_specs=[smem] + [vmem] * 3,
+        out_shape=(f32(512, 128), f32(512, 128), f32(320, 128), f32(MAIN, 128)),
+        in_specs=[smem] + [vmem] * 4,
         compiler_params=room(ROOM[5]),
         cost_estimate=work(500000, 1200000),
         name="rims",
-    )(inside, below, above, sides)
+    )(inside, below, above, sides, dens)
     d_sides = pl.pallas_call(
         corner_kernel, out_shape=f32(488, 128), compiler_params=room(ROOM[2]),
         cost_estimate=work(200000, 700000), name="corners",
@@ -681,22 +708,24 @@
     p_film, back, keep = pl.pallas_call(
         solve_kernel,
         out_shape=(f32(MAIN, 128), f32(SENT, 128), f32(SLOTS, 128)),
-        in_specs=[smem, smem] + [vmem] * 10,
+        in_specs=[smem, hbm] + [vmem] * 10,
         scratch_shapes=[
             big, pltpu.VMEM((QS * 8, 128), jnp.float32), big, big, big, big, big, big, big, big, big, big,
             pltpu.VMEM((SLOTS, 384), jnp.bfloat16),
             pltpu.VMEM((SLOTS, 640), jnp.float32),
             pltpu.VMEM((SENT + SLOTS, 128), jnp.float32),
+            pltpu.SMEM((SLOTS,), jnp.int32),
+            pltpu.SemaphoreType.DMA,
         ],
         compiler_params=room(ROOM[3]),
         cost_estimate=work(1400000000, 9000000),
         name="solve",
-    )(inside, first, dens, d_below, d_above, d_left, d_right, sq, fw, sq_rim, fw_rim, filter_tiles)
+    )(inside, slot_block, dens, d_below, d_above, d_left, d_right, sq, fw, sq_rim, fw_rim, filter_tiles)
     returned = moved(back, OWNERS, -1)
     pressure = pl.pallas_call(
         pressure_kernel, out_shape=f32(128, 2048), compiler_params=room(ROOM[4]), cost_estimate=work(2000000, 2100000), name="pressure",
     )(p_film)
-    held = curve_offset(first[0]) + (SLOTS - SENT)
+    held = curve_offset(slot_block[0]) + (SLOTS - SENT)
     slot = lax.broadcasted_iota(jnp.int32, (SLOTS, 1), 0)
     upper = jnp.pad(returned, ((SLOTS - SENT, 0), (0, 0)))
     sensitivity = jnp.where(slot < held, keep, upper)

time: 86.6 us -> 83.9 us (0.969)
  local copies, waits for them, and re-layouts: 6.02 us -> 2.69 us
  Pallas kernels: 40.7 us -> 41.9 us
    unnamed x14 -> x10, local copies, waits for them, and re-layouts: 3.48 us -> 0.99 us
    pallas_call x1, Pallas kernels: 4.91 us -> 6.5 us  [local(): pl.pallas_call(sources_kernel, out_shape=(f32(SLOTS, 128), f32(SLOTS, 128...]
  transfers between devices with their start and end apart: 8 -> 8, of which waited for: 5 -> 5; matrix products, arithmetic and copies ran while one was open for 2% -> 1% of each run, Pallas kernels for 16% -> 18%
where the time goes in v4:
time: 83.9 us; the launch traced here: 83.8 us
  Pallas kernels  41.9 us (50%)
  waiting for transfers between devices  21.6 us (26%)
  starting transfers between devices  14.8 us (18%)
  local copies, waits for them, and re-layouts  2.69 us (3%)
  between operations  1.42 us (2%)
  other arithmetic  1.39 us (2%)
    pallas_call x1, Pallas kernels, local(): pl.pallas_call(solve_kernel, out_shape=(f32(MAIN, 128), f32(SENT, 128), f...  26.3 us
    ppermute x8, waiting for transfers between devices, moved(): lax.ppermute(x, axis, [(i, (i + by) % length) for i in range(length)])  21.6 us
    ppermute x8, starting transfers between devices, moved(): lax.ppermute(x, axis, [(i, (i + by) % length) for i in range(length)])  14.8 us
    pallas_call x1, Pallas kernels, local(): pl.pallas_call(sources_kernel, out_shape=(f32(SLOTS, 128), f32(SLOTS, 128...  6.5 us
    pallas_call x1, Pallas kernels, local(): pl.pallas_call(filter_kernel, out_shape=(f32(MAIN, 128), f32(272, 128), f...  3.92 us
    pallas_call x1, Pallas kernels, local(): pl.pallas_call(pressure_kernel, out_shape=f32(128, 2048), compiler_params...  3.03 us
    pallas_call x1, Pallas kernels, local(): pl.pallas_call(rims_kernel, out_shape=(f32(512, 128), f32(512, 128), f32(...  1.92 us
  transfers between devices with their start and end apart: 8, of which 5 were waited for; matrix products, arithmetic and copies ran while one was open for 1% of the time, Pallas kernels for 18%

profile of v4, /device:TPU:25, one launch (start us, length us, event | category | flops | bytes accessed | tf_op | source)
XLA Modules:
  0.0 83.8 jit_solution(10823053510037500324)
XLA Ops:
  0.6 1.2 %slice.6 = f32[1536,128]{1,0:T(8,128)S(1)} slice(f32[2048,128]{1,0:T(8,128)} %own_ref.1), slice={[512:2048], [0:128]} | slice | bytes 1572864 | tf_op jit(solution)/shard_map/slice | solution.py:653
  1.8 0.0 copy-start
  1.8 0.0 copy-start.3
  1.8 0.0 copy-start.4
  1.9 1.5 %collective-permute-start.2 = (f32[1536,128]{1,0:T(8,128)S(1)}, f32[1536,128]{1,0:T(8,128)S(1)}, u32[]{:S(2)}, u32[]{:S(2)}) collective-permute-start(f32[1536,128]{1,0:T(8,128)S(1)} %slice.6), channel_id=1, source_target_pairs={{0,1},{1,2},{2,3},{3,4},{4,5},{5,6},{6,7},{7,8},{8,9},{9,10},{10,1... | collective-permute-start | bytes 2359304 | tf_op jit(solution)/shard_map/ppermute | solution.py:629
  3.4 6.5 %sources.1 = (f32[2048,128]{1,0:T(8,128)S(1)}, f32[2048,128]{1,0:T(8,128)S(1)}, f32[256,128]{1,0:T(8,128)S(1)}, f32[32,2048]{1,0:T(8,128)}, f32[32,2048]{1,0:T(8,128)}) custom-call(f32[128,2048]{1,0:T(8,128)} %sq_hbm, f32[128,2048]{1,0:T(8,128)} %fw_hbm, s32[128,2048]{1,0:T(8,128)} %holes_hbm), custom_call_target="tpu_custom_call" | custom-call | flops 2000000 | bytes 5500000 | tf_op jit(solution)/shard_map/sources/pallas_call | solution.py:656
  9.9 0.0 copy-start.1
  9.9 1.0 %copy-done.1 = f32[2048,128]{1,0:T(8,128)} copy-done((f32[2048,128]{1,0:T(8,128)}, f32[2048,128]{1,0:T(8,128)S(1)}, u32[]{:S(2)}) %copy-start.1) | copy-done | bytes 1048600
  10.8 4.6 %collective-permute-start = (f32[32,2048]{1,0:T(8,128)}, f32[32,2048]{1,0:T(8,128)S(1)}, u32[]{:S(2)}, u32[]{:S(2)}) collective-permute-start(f32[32,2048]{1,0:T(8,128)} %get-tuple-element.28), channel_id=1, source_target_pairs={{0,120},{8,0},{16,8},{24,16},{32,24},{40,32},{48,40},{56,48},{64,5... | collective-permute-start | bytes 786440 | tf_op jit(solution)/shard_map/ppermute | solution.py:629
  15.5 0.0 collective-permute-start.1
  15.5 0.0 collective-permute-done.2.got_ref
  15.5 0.0 copy-done
  15.5 0.0 copy-done.3
  15.5 0.0 copy-done.4
  15.5 3.9 %filter.1 = (f32[2176,128]{1,0:T(8,128)S(1)}, f32[272,128]{1,0:T(8,128)}, f32[272,128]{1,0:T(8,128)}, f32[128,128]{1,0:T(8,128)S(1)}) custom-call(s32[2048]{0:T(1024)S(1)} %copy-done.4, f32[1536,128]{1,0:T(8,128)S(1)} %collective-permute-done.2.got_ref, f32[2048,128]{1,0:T(8,128)S(1)} %copy-done, f32[5,128,128]{2,1,0:T(8,128)S(1)} %copy-done.3), custom_call_target="tpu_custom_call" | custom-call | flops 1100000000 | bytes 3500000 | tf_op jit(solution)/shard_map/filter/pallas_call | solution.py:673
  19.4 4.8 %collective-permute-start.3 = (f32[272,128]{1,0:T(8,128)}, f32[272,128]{1,0:T(8,128)S(1)}, u32[]{:S(2)}, u32[]{:S(2)}) collective-permute-start(f32[272,128]{1,0:T(8,128)} %get-tuple-element.37), channel_id=1, source_target_pairs={{0,120},{8,0},{16,8},{24,16},{32,24},{40,32},{48,40},{56,48},{64,5... | collective-permute-start | bytes 417800 | tf_op jit(solution)/shard_map/ppermute | solution.py:629
  24.3 0.0 collective-permute-start.4
  24.3 0.1 add_convert_fusion.ok_ref
  24.3 0.0 collective-permute-done.below_ref
  24.3 1.5 %collective-permute-done.1.above_ref = f32[32,2048]{1,0:T(8,128)S(1)} collective-permute-done((f32[32,2048]{1,0:T(8,128)}, f32[32,2048]{1,0:T(8,128)S(1)}, u32[]{:S(2)}, u32[]{:S(2)}) %collective-permute-start.1) | collective-permute-done | bytes 262176 | tf_op jit(solution)/shard_map/ppermute | solution.py:629
  25.9 0.0 copy-start.2
  25.9 1.9 %rims.1 = (f32[512,128]{1,0:T(8,128)S(1)}, f32[512,128]{1,0:T(8,128)S(1)}, f32[320,128]{1,0:T(8,128)S(1)}, f32[2176,128]{1,0:T(8,128)S(1)}) custom-call(s32[4]{0:T(128)S(1)} %add_convert_fusion.ok_ref, f32[32,2048]{1,0:T(8,128)S(1)} %collective-permute-done.below_ref, f32[32,2048]{1,0:T(8,128)S(1)} %collective-permute-done.1.above_ref, ...), custom_call_target="tpu_custom_call" | custom-call | flops 500000 | bytes 1200000 | tf_op jit(solution)/shard_map/rims/pallas_call | solution.py:692
  27.8 0.0 collective-permute-done.3.below_ref
  27.8 3.9 %collective-permute-done.4.above_ref = f32[272,128]{1,0:T(8,128)S(1)} collective-permute-done((f32[272,128]{1,0:T(8,128)}, f32[272,128]{1,0:T(8,128)S(1)}, u32[]{:S(2)}, u32[]{:S(2)}) %collective-permute-start.4) | collective-permute-done | bytes 139296 | tf_op jit(solution)/shard_map/ppermute | solution.py:629
  31.7 0.2 corners.1
  31.9 3.8 %collective-permute-start.5 = (f32[488,128]{1,0:T(8,128)S(1)}, f32[488,128]{1,0:T(8,128)S(1)}, u32[]{:S(2)}, u32[]{:S(2)}) collective-permute-start(f32[488,128]{1,0:T(8,128)S(1)} %corners.1), channel_id=1, source_target_pairs={{0,1},{1,2},{2,3},{3,4},{4,5},{5,6},{6,7},{7,0},{8,9},{9,10},{10,1... | collective-permute-start | bytes 749576 | tf_op jit(solution)/shard_map/ppermute | solution.py:629
  35.7 0.0 collective-permute-start.6
  35.7 3.2 %collective-permute-done.5.left_ref = f32[488,128]{1,0:T(8,128)S(1)} collective-permute-done((f32[488,128]{1,0:T(8,128)S(1)}, f32[488,128]{1,0:T(8,128)S(1)}, u32[]{:S(2)}, u32[]{:S(2)}) %collective-permute-start.5) | collective-permute-done | bytes 249888 | tf_op jit(solution)/shard_map/ppermute | solution.py:629
  38.9 3.7 %collective-permute-done.6.right_ref = f32[488,128]{1,0:T(8,128)S(1)} collective-permute-done((f32[488,128]{1,0:T(8,128)S(1)}, f32[488,128]{1,0:T(8,128)S(1)}, u32[]{:S(2)}, u32[]{:S(2)}) %collective-permute-start.6) | collective-permute-done | bytes 249888 | tf_op jit(solution)/shard_map/ppermute | solution.py:629
  42.6 0.0 copy-done.2
  42.6 26.3 %solve.1 = (f32[2176,128]{1,0:T(8,128)S(1)}, f32[1536,128]{1,0:T(8,128)S(1)}, f32[2048,128]{1,0:T(8,128)S(1)}) custom-call(s32[4]{0:T(128)S(1)} %add_convert_fusion.ok_ref, s32[2048]{0:T(1024)S(1)} %copy-done.4, f32[2176,128]{1,0:T(8,128)S(1)} %get-tuple-element.36.dens_ref, f32[272,128]{1,0:T(8,128)S(1)} %collective-permute-done.3.below_ref, ...), custom_call_target="tpu_custom_call" | custom-call | flops 1400000000 | bytes 9000000 | tf_op jit(solution)/shard_map/solve/pallas_call | solution.py:708
  68.9 0.1 collective-permute-start.7
  69.0 0.5 slice.7
  70.2 3.0 %pressure.1 = f32[128,2048]{1,0:T(8,128)} custom-call(f32[2176,128]{1,0:T(8,128)S(1)} %get-tuple-element.45.p_ref), custom_call_target="tpu_custom_call" | custom-call | flops 2000000 | bytes 2100000 | tf_op jit(solution)/shard_map/pressure/pallas_call | solution.py:725
  73.2 9.3 %collective-permute-done.7 = f32[1536,128]{1,0:T(8,128)S(1)} collective-permute-done((f32[1536,128]{1,0:T(8,128)S(1)}, f32[1536,128]{1,0:T(8,128)S(1)}, u32[]{:S(2)}, u32[]{:S(2)}) %collective-permute-start.7) | collective-permute-done | bytes 786464 | tf_op jit(solution)/shard_map/ppermute | solution.py:629
  82.5 1.3 %pad_select_fusion = f32[2048,128]{1,0:T(8,128)} fusion(f32[2048,128]{1,0:T(8,128)S(1)} %get-tuple-element.46, f32[1536,128]{1,0:T(8,128)S(1)} %collective-permute-done.7, pred[2048]{0:T(1024)(128)(4,1)S(1)} %iota_compare_fusion), kind=kLoop, calls=%fused_computation | loop fusion | flops 262144 | bytes 2885632 | tf_op jit(solution)/shard_map/jit(_where)/select_n | solution.py:731
  (1 shorter events, 0.0 us)
Async XLA Ops:
  1.8 13.7 %copy-start = (f32[2048,128]{1,0:T(8,128)S(1)}, f32[2048,128]{1,0:T(8,128)}, u32[]{:S(2)}) copy-start(f32[2048,128]{1,0:T(8,128)} %own_ref.1) | copy-start | bytes 3145732
  1.8 13.6 %copy-start.3 = (f32[5,128,128]{2,1,0:T(8,128)S(1)}, f32[5,128,128]{2,1,0:T(8,128)}, u32[]{:S(2)}) copy-start(f32[5,128,128]{2,1,0:T(8,128)} %tiles_ref.3) | copy-start | bytes 983044
  1.8 13.6 %copy-start.4 = (s32[2048]{0:T(1024)S(1)}, s32[2048]{0:T(1024)}, u32[]{:S(2)}) copy-start(s32[2048]{0:T(1024)} %first_ref.3) | copy-start | bytes 24580
  1.9 13.6 %collective-permute-start.2 = (f32[1536,128]{1,0:T(8,128)S(1)}, f32[1536,128]{1,0:T(8,128)S(1)}, u32[]{:S(2)}, u32[]{:S(2)}) collective-permute-start(f32[1536,128]{1,0:T(8,128)S(1)} %slice.6), channel_id=1, source_target_pairs={{0,1},{1,2},{2,3},{3,4},{4,5},{5,6},{6,7},{7,8},{8,9},{9,10},{10,1... | collective-permute-start | bytes 2359304 | tf_op jit(solution)/shard_map/ppermute | solution.py:629
  9.9 1.0 %copy-start.1 = (f32[2048,128]{1,0:T(8,128)}, f32[2048,128]{1,0:T(8,128)S(1)}, u32[]{:S(2)}) copy-start(f32[2048,128]{1,0:T(8,128)S(1)} %get-tuple-element.42.fw_ref) | copy-start | bytes 3145732
  10.8 13.5 %collective-permute-start = (f32[32,2048]{1,0:T(8,128)}, f32[32,2048]{1,0:T(8,128)S(1)}, u32[]{:S(2)}, u32[]{:S(2)}) collective-permute-start(f32[32,2048]{1,0:T(8,128)} %get-tuple-element.28), channel_id=1, source_target_pairs={{0,120},{8,0},{16,8},{24,16},{32,24},{40,32},{48,40},{56,48},{64,5... | collective-permute-start | bytes 786440 | tf_op jit(solution)/shard_map/ppermute | solution.py:629
  15.5 10.4 %collective-permute-start.1 = (f32[32,2048]{1,0:T(8,128)}, f32[32,2048]{1,0:T(8,128)S(1)}, u32[]{:S(2)}, u32[]{:S(2)}) collective-permute-start(f32[32,2048]{1,0:T(8,128)} %get-tuple-element.29), channel_id=1, source_target_pairs={{0,8},{8,16},{16,24},{24,32},{32,40},{40,48},{48,56},{56,64},{64,7... | collective-permute-start | bytes 786440 | tf_op jit(solution)/shard_map/ppermute | solution.py:629
  19.4 8.4 %collective-permute-start.3 = (f32[272,128]{1,0:T(8,128)}, f32[272,128]{1,0:T(8,128)S(1)}, u32[]{:S(2)}, u32[]{:S(2)}) collective-permute-start(f32[272,128]{1,0:T(8,128)} %get-tuple-element.37), channel_id=1, source_target_pairs={{0,120},{8,0},{16,8},{24,16},{32,24},{40,32},{48,40},{56,48},{64,5... | collective-permute-start | bytes 417800 | tf_op jit(solution)/shard_map/ppermute | solution.py:629
  24.3 7.4 %collective-permute-start.4 = (f32[272,128]{1,0:T(8,128)}, f32[272,128]{1,0:T(8,128)S(1)}, u32[]{:S(2)}, u32[]{:S(2)}) collective-permute-start(f32[272,128]{1,0:T(8,128)} %get-tuple-element.38), channel_id=1, source_target_pairs={{0,8},{8,16},{16,24},{24,32},{32,40},{40,48},{48,56},{56,64},{64,7... | collective-permute-start | bytes 417800 | tf_op jit(solution)/shard_map/ppermute | solution.py:629
  25.9 16.8 %copy-start.2 = (f32[2048,128]{1,0:T(8,128)S(1)}, f32[2048,128]{1,0:T(8,128)}, u32[]{:S(2)}) copy-start(f32[2048,128]{1,0:T(8,128)} %copy-done.1) | copy-start | bytes 3145732
  31.9 7.0 %collective-permute-start.5 = (f32[488,128]{1,0:T(8,128)S(1)}, f32[488,128]{1,0:T(8,128)S(1)}, u32[]{:S(2)}, u32[]{:S(2)}) collective-permute-start(f32[488,128]{1,0:T(8,128)S(1)} %corners.1), channel_id=1, source_target_pairs={{0,1},{1,2},{2,3},{3,4},{4,5},{5,6},{6,7},{7,0},{8,9},{9,10},{10,1... | collective-permute-start | bytes 749576 | tf_op jit(solution)/shard_map/ppermute | solution.py:629
  35.7 6.9 %collective-permute-start.6 = (f32[488,128]{1,0:T(8,128)S(1)}, f32[488,128]{1,0:T(8,128)S(1)}, u32[]{:S(2)}, u32[]{:S(2)}) collective-permute-start(f32[488,128]{1,0:T(8,128)S(1)} %corners.1), channel_id=1, source_target_pairs={{0,7},{1,0},{2,1},{3,2},{4,3},{5,4},{6,5},{7,6},{8,15},{9,8},{10,9... | collective-permute-start | bytes 749576 | tf_op jit(solution)/shard_map/ppermute | solution.py:629
  68.9 13.6 %collective-permute-start.7 = (f32[1536,128]{1,0:T(8,128)S(1)}, f32[1536,128]{1,0:T(8,128)S(1)}, u32[]{:S(2)}, u32[]{:S(2)}) collective-permute-start(f32[1536,128]{1,0:T(8,128)S(1)} %get-tuple-element.47), channel_id=1, source_target_pairs={{0,127},{1,0},{2,1},{3,2},{4,3},{5,4},{6,5},{7,6},{8,7},{9,8},{10,... | collective-permute-start | bytes 2359304 | tf_op jit(solution)/shard_map/ppermute | solution.py:629

commit v5 on v4

--- a/solution.py
+++ b/solution.py
@@ -167,7 +167,7 @@
     return jnp.where(lane_ids() < 64, ref[rows, 0:128], ref[rows, 1920:2048])
 
 
-def sources_kernel(sq_hbm, fw_hbm, holes_hbm, out_sq, out_fw, sides, edge_up, edge_down,
+def sources_kernel(sq_hbm, fw_hbm, holes_hbm, out_sq, sides, edge_up, edge_down,
                    sq_ref, fw_ref, holes_ref, sems):
     copies = []
     for piece in range(4):
@@ -182,18 +182,10 @@
     def tile_rows(brow, carry):
         rows = pl.ds(pl.multiple_of(brow * 8, 8), 8)
 
-        def masked(v):
-            cols = pl.ds(v * 128, 128)
-            return jnp.where(holes_ref[rows, cols] > 0, 0.0, fw_ref[rows, cols])
-
-        def put(ref):
-            def store(c, x):
-                ref[pl.ds(c * 16 + brow, 8, stride=256), :] = x
-
-            return store
-
-        spread(lambda v: sq_ref[rows, pl.ds(v * 128, 128)], put(out_sq))
-        spread(masked, put(out_fw))
+        def store(c, x):
+            out_sq[pl.ds(c * 16 + brow, 8, stride=256), :] = x
+
+        spread(lambda v: sq_ref[rows, pl.ds(v * 128, 128)], store)
         sides[rows, :] = outer_columns(sq_ref, rows)
         outer = jnp.where(outer_columns(holes_ref, rows) > 0, 0.0, outer_columns(fw_ref, rows))
         sides[pl.ds(pl.multiple_of(128 + brow * 8, 8), 8), :] = outer
@@ -202,12 +194,42 @@
     for piece in range(4):
         for copy in copies[piece]:
             copy.wait()
-        lax.fori_loop(piece * 4, piece * 4 + 4, tile_rows, 0, unroll=2)
+        lax.fori_loop(piece * 4, piece * 4 + 4, tile_rows, 0, unroll=4)
     for edge, start in ((edge_up, 0), (edge_down, 112)):
         for part in range(2):
             rows = pl.ds(start + part * 8, 8)
             edge[pl.ds(part * 8, 8), :] = sq_ref[rows, :]
             edge[pl.ds(16 + part * 8, 8), :] = jnp.where(holes_ref[rows, :] > 0, 0.0, fw_ref[rows, :])
+
+
+def weights_kernel(fw_hbm, holes_hbm, out_fw, fw_ref, holes_ref, sems):
+    copies = []
+    for piece in range(4):
+        rows = pl.ds(piece * 32, 32)
+        copies.append([
+            pltpu.make_async_copy(src.at[rows, :], dst.at[rows, :], sems.at[piece, i])
+            for i, (src, dst) in enumerate(((fw_hbm, fw_ref), (holes_hbm, holes_ref)))
+        ])
+        for copy in copies[-1]:
+            copy.start()
+
+    def tile_rows(brow, carry):
+        rows = pl.ds(pl.multiple_of(brow * 8, 8), 8)
+
+        def masked(v):
+            cols = pl.ds(v * 128, 128)
+            return jnp.where(holes_ref[rows, cols] > 0, 0.0, fw_ref[rows, cols])
+
+        def store(c, x):
+            out_fw[pl.ds(c * 16 + brow, 8, stride=256), :] = x
+
+        spread(masked, store)
+        return carry
+
+    for piece in range(4):
+        for copy in copies[piece]:
+            copy.wait()
+        lax.fori_loop(piece * 4, piece * 4 + 4, tile_rows, 0, unroll=4)
 
 
 def rims_kernel(ok_ref, below_ref, above_ref, sides_ref, dens_ref, out_sq, out_fw, out_sides, out_dens):
@@ -653,9 +675,9 @@
         (design[SLOTS - SENT:], holes, squeeze_source, force_weight)
     )
     got = moved(tail, OWNERS, 1)
-    sq, fw, sides, edge_up, edge_down = pl.pallas_call(
+    sq, sides, edge_up, edge_down = pl.pallas_call(
         sources_kernel,
-        out_shape=(f32(SLOTS, 128), f32(SLOTS, 128), f32(256, 128), f32(32, 2048), f32(32, 2048)),
+        out_shape=(f32(SLOTS, 128), f32(256, 128), f32(32, 2048), f32(32, 2048)),
         in_specs=[hbm] * 3,
         scratch_shapes=[
             pltpu.VMEM((128, 2048), jnp.float32),
@@ -701,6 +723,20 @@
         corner_kernel, out_shape=f32(488, 128), compiler_params=room(ROOM[2]),
         cost_estimate=work(200000, 700000), name="corners",
     )(d_below, d_above, cols, sides)
+    d_sides, force_weight, holes = lax.optimization_barrier((d_sides, force_weight, holes))
+    fw = pl.pallas_call(
+        weights_kernel,
+        out_shape=f32(SLOTS, 128),
+        in_specs=[hbm] * 2,
+        scratch_shapes=[
+            pltpu.VMEM((128, 2048), jnp.float32),
+            pltpu.VMEM((128, 2048), jnp.int32),
+            pltpu.SemaphoreType.DMA((4, 2)),
+        ],
+        compiler_params=room(ROOM[0]),
+        cost_estimate=work(1000000, 3000000),
+        name="weights",
+    )(*(pltpu.with_memory_space_constraint(x, pltpu.HBM) for x in (force_weight, holes)))
     d_right = moved(d_sides, "narrow", -1)
     d_left = moved(d_sides, "narrow", 1)
 

time: 83.9 us -> 85.3 us (1.017)
  starting transfers between devices: 14.8 us -> 19.4 us
  waiting for transfers between devices: 21.6 us -> 18.1 us
  Pallas kernels: 41.9 us -> 43.1 us
  local copies, waits for them, and re-layouts: 2.69 us -> 1.72 us
    ppermute x8, starting transfers between devices: 14.8 us -> 19.4 us  [moved(): lax.ppermute(x, axis, [(i, (i + by) % length) for i in range(length)])]
    ppermute x8, waiting for transfers between devices: 21.6 us -> 18.1 us  [moved(): lax.ppermute(x, axis, [(i, (i + by) % length) for i in range(length)])]
    pallas_call x1 -> x2, Pallas kernels: 6.5 us -> 7.66 us  [the longest x1 4.19 us: local(): pl.pallas_call(sources_kernel, out_shape=(f32(SLOTS, 128), f32(256, 128),...]
    unnamed x10 -> x6, local copies, waits for them, and re-layouts: 0.99 us -> 0.02 us
  transfers between devices with their start and end apart: 8 -> 8, of which waited for: 5 -> 4; matrix products, arithmetic and copies ran while one was open for 1% -> 1% of each run, Pallas kernels for 18% -> 19%
where the time goes in v5:
time: 85.3 us; the launch traced here: 85.1 us
  Pallas kernels  43.1 us (51%)
  starting transfers between devices  19.4 us (23%)
  waiting for transfers between devices  18.1 us (21%)
  local copies, waits for them, and re-layouts  1.72 us (2%)
  between operations  1.41 us (2%)
  other arithmetic  1.39 us (2%)
    pallas_call x1, Pallas kernels, local(): pl.pallas_call(solve_kernel, out_shape=(f32(MAIN, 128), f32(SENT, 128), f...  26.3 us
    ppermute x8, starting transfers between devices, moved(): lax.ppermute(x, axis, [(i, (i + by) % length) for i in range(length)])  19.4 us
    ppermute x8, waiting for transfers between devices, moved(): lax.ppermute(x, axis, [(i, (i + by) % length) for i in range(length)])  18.1 us
    pallas_call x1, Pallas kernels, local(): pl.pallas_call(sources_kernel, out_shape=(f32(SLOTS, 128), f32(256, 128),...  4.19 us
    pallas_call x1, Pallas kernels, local(): pl.pallas_call(filter_kernel, out_shape=(f32(MAIN, 128), f32(272, 128), f...  3.9 us
    pallas_call x1, Pallas kernels, local(): pl.pallas_call(weights_kernel, out_shape=f32(SLOTS, 128), in_specs=[hbm]...  3.46 us
    pallas_call x1, Pallas kernels, local(): pl.pallas_call(pressure_kernel, out_shape=f32(128, 2048), compiler_params...  3.03 us
    pallas_call x1, Pallas kernels, local(): pl.pallas_call(rims_kernel, out_shape=(f32(512, 128), f32(512, 128), f32(...  1.92 us
  transfers between devices with their start and end apart: 8, of which 4 were waited for; matrix products, arithmetic and copies ran while one was open for 1% of the time, Pallas kernels for 19%

profile of v5, /device:TPU:25, one launch (start us, length us, event | category | flops | bytes accessed | tf_op | source)
XLA Modules:
  0.0 85.1 jit_solution(8390343082807195380)
XLA Ops:
  0.6 1.2 %slice.6 = f32[1536,128]{1,0:T(8,128)S(1)} slice(f32[2048,128]{1,0:T(8,128)} %own_ref.1), slice={[512:2048], [0:128]} | slice | bytes 1572864 | tf_op jit(solution)/shard_map/slice | solution.py:675
  1.8 0.0 copy-start
  1.8 0.0 copy-start.1
  1.8 0.0 copy-start.2
  1.9 1.5 %collective-permute-start.2 = (f32[1536,128]{1,0:T(8,128)S(1)}, f32[1536,128]{1,0:T(8,128)S(1)}, u32[]{:S(2)}, u32[]{:S(2)}) collective-permute-start(f32[1536,128]{1,0:T(8,128)S(1)} %slice.6), channel_id=1, source_target_pairs={{0,1},{1,2},{2,3},{3,4},{4,5},{5,6},{6,7},{7,8},{8,9},{9,10},{10,1... | collective-permute-start | bytes 2359304 | tf_op jit(solution)/shard_map/ppermute | solution.py:651
  3.4 4.2 %sources.1 = (f32[2048,128]{1,0:T(8,128)S(1)}, f32[256,128]{1,0:T(8,128)S(1)}, f32[32,2048]{1,0:T(8,128)}, f32[32,2048]{1,0:T(8,128)}) custom-call(f32[128,2048]{1,0:T(8,128)} %sq_hbm, f32[128,2048]{1,0:T(8,128)} %fw_hbm.1, s32[128,2048]{1,0:T(8,128)} %holes_hbm.1), custom_call_target="tpu_custom_call" | custom-call | flops 2000000 | bytes 5500000 | tf_op jit(solution)/shard_map/sources/pallas_call | solution.py:678
  7.6 4.7 %collective-permute-start = (f32[32,2048]{1,0:T(8,128)}, f32[32,2048]{1,0:T(8,128)S(1)}, u32[]{:S(2)}, u32[]{:S(2)}) collective-permute-start(f32[32,2048]{1,0:T(8,128)} %get-tuple-element.30), channel_id=1, source_target_pairs={{0,120},{8,0},{16,8},{24,16},{32,24},{40,32},{48,40},{56,48},{64,5... | collective-permute-start | bytes 786440 | tf_op jit(solution)/shard_map/ppermute | solution.py:651
  12.3 0.0 collective-permute-start.1
  12.3 0.0 collective-permute-done.2.got_ref
  12.3 0.0 copy-done
  12.3 0.0 copy-done.1
  12.3 0.0 copy-done.2
  12.3 3.9 %filter.1 = (f32[2176,128]{1,0:T(8,128)S(1)}, f32[272,128]{1,0:T(8,128)}, f32[272,128]{1,0:T(8,128)}, f32[128,128]{1,0:T(8,128)S(1)}) custom-call(s32[2048]{0:T(1024)S(1)} %copy-done.2, f32[1536,128]{1,0:T(8,128)S(1)} %collective-permute-done.2.got_ref, f32[2048,128]{1,0:T(8,128)S(1)} %copy-done, f32[5,128,128]{2,1,0:T(8,128)S(1)} %copy-done.1), custom_call_target="tpu_custom_call" | custom-call | flops 1100000000 | bytes 3500000 | tf_op jit(solution)/shard_map/filter/pallas_call | solution.py:695
  16.2 4.8 %collective-permute-start.3 = (f32[272,128]{1,0:T(8,128)}, f32[272,128]{1,0:T(8,128)S(1)}, u32[]{:S(2)}, u32[]{:S(2)}) collective-permute-start(f32[272,128]{1,0:T(8,128)} %get-tuple-element.39), channel_id=1, source_target_pairs={{0,120},{8,0},{16,8},{24,16},{32,24},{40,32},{48,40},{56,48},{64,5... | collective-permute-start | bytes 417800 | tf_op jit(solution)/shard_map/ppermute | solution.py:651
  21.0 0.0 collective-permute-start.4
  21.0 0.1 add_convert_fusion.ok_ref
  21.1 0.0 collective-permute-done.below_ref
  21.1 1.5 %collective-permute-done.1.above_ref = f32[32,2048]{1,0:T(8,128)S(1)} collective-permute-done((f32[32,2048]{1,0:T(8,128)}, f32[32,2048]{1,0:T(8,128)S(1)}, u32[]{:S(2)}, u32[]{:S(2)}) %collective-permute-start.1) | collective-permute-done | bytes 262176 | tf_op jit(solution)/shard_map/ppermute | solution.py:651
  22.6 1.9 %rims.1 = (f32[512,128]{1,0:T(8,128)S(1)}, f32[512,128]{1,0:T(8,128)S(1)}, f32[320,128]{1,0:T(8,128)S(1)}, f32[2176,128]{1,0:T(8,128)S(1)}) custom-call(s32[4]{0:T(128)S(1)} %add_convert_fusion.ok_ref, f32[32,2048]{1,0:T(8,128)S(1)} %collective-permute-done.below_ref, f32[32,2048]{1,0:T(8,128)S(1)} %collective-permute-done.1.above_ref, ...), custom_call_target="tpu_custom_call" | custom-call | flops 500000 | bytes 1200000 | tf_op jit(solution)/shard_map/rims/pallas_call | solution.py:714
  24.6 0.0 collective-permute-done.3.below_ref
  24.6 3.9 %collective-permute-done.4.above_ref = f32[272,128]{1,0:T(8,128)S(1)} collective-permute-done((f32[272,128]{1,0:T(8,128)}, f32[272,128]{1,0:T(8,128)S(1)}, u32[]{:S(2)}, u32[]{:S(2)}) %collective-permute-start.4) | collective-permute-done | bytes 139296 | tf_op jit(solution)/shard_map/ppermute | solution.py:651
  28.5 0.2 corners.1
  28.7 8.3 %collective-permute-start.5 = (f32[488,128]{1,0:T(8,128)S(1)}, f32[488,128]{1,0:T(8,128)S(1)}, u32[]{:S(2)}, u32[]{:S(2)}) collective-permute-start(f32[488,128]{1,0:T(8,128)S(1)} %corners.1), channel_id=1, source_target_pairs={{0,1},{1,2},{2,3},{3,4},{4,5},{5,6},{6,7},{7,0},{8,9},{9,10},{10,1... | collective-permute-start | bytes 749576 | tf_op jit(solution)/shard_map/ppermute | solution.py:651
  37.0 0.0 collective-permute-start.6
  37.0 3.5 %weights.1.fw_ref = f32[2048,128]{1,0:T(8,128)S(1)} custom-call(f32[128,2048]{1,0:T(8,128)} %fw_hbm.1, s32[128,2048]{1,0:T(8,128)} %holes_hbm.1), custom_call_target="tpu_custom_call" | custom-call | flops 1000000 | bytes 3000000 | tf_op jit(solution)/shard_map/weights/pallas_call | solution.py:727
  40.5 0.0 collective-permute-done.5.left_ref
  40.5 3.4 %collective-permute-done.6.right_ref = f32[488,128]{1,0:T(8,128)S(1)} collective-permute-done((f32[488,128]{1,0:T(8,128)S(1)}, f32[488,128]{1,0:T(8,128)S(1)}, u32[]{:S(2)}, u32[]{:S(2)}) %collective-permute-start.6) | collective-permute-done | bytes 249888 | tf_op jit(solution)/shard_map/ppermute | solution.py:651
  43.9 26.3 %solve.1 = (f32[2176,128]{1,0:T(8,128)S(1)}, f32[1536,128]{1,0:T(8,128)S(1)}, f32[2048,128]{1,0:T(8,128)S(1)}) custom-call(s32[4]{0:T(128)S(1)} %add_convert_fusion.ok_ref, s32[2048]{0:T(1024)S(1)} %copy-done.2, f32[2176,128]{1,0:T(8,128)S(1)} %get-tuple-element.38.dens_ref, f32[272,128]{1,0:T(8,128)S(1)} %collective-permute-done.3.below_ref, ...), custom_call_target="tpu_custom_call" | custom-call | flops 1400000000 | bytes 9000000 | tf_op jit(solution)/shard_map/solve/pallas_call | solution.py:744
  70.2 0.1 collective-permute-start.7
  70.3 0.5 slice.7
  71.5 3.0 %pressure.1 = f32[128,2048]{1,0:T(8,128)} custom-call(f32[2176,128]{1,0:T(8,128)S(1)} %get-tuple-element.49.p_ref), custom_call_target="tpu_custom_call" | custom-call | flops 2000000 | bytes 2100000 | tf_op jit(solution)/shard_map/pressure/pallas_call | solution.py:761
  74.5 9.3 %collective-permute-done.7 = f32[1536,128]{1,0:T(8,128)S(1)} collective-permute-done((f32[1536,128]{1,0:T(8,128)S(1)}, f32[1536,128]{1,0:T(8,128)S(1)}, u32[]{:S(2)}, u32[]{:S(2)}) %collective-permute-start.7) | collective-permute-done | bytes 786464 | tf_op jit(solution)/shard_map/ppermute | solution.py:651
  83.8 1.3 %pad_select_fusion = f32[2048,128]{1,0:T(8,128)} fusion(f32[2048,128]{1,0:T(8,128)S(1)} %get-tuple-element.50, f32[1536,128]{1,0:T(8,128)S(1)} %collective-permute-done.7, pred[2048]{0:T(1024)(128)(4,1)S(1)} %iota_compare_fusion), kind=kLoop, calls=%fused_computation | loop fusion | flops 262144 | bytes 2885632 | tf_op jit(solution)/shard_map/jit(_where)/select_n | solution.py:767
  (1 shorter events, 0.0 us)
Async XLA Ops:
  1.8 10.5 %copy-start = (f32[2048,128]{1,0:T(8,128)S(1)}, f32[2048,128]{1,0:T(8,128)}, u32[]{:S(2)}) copy-start(f32[2048,128]{1,0:T(8,128)} %own_ref.1) | copy-start | bytes 3145732
  1.8 10.5 %copy-start.1 = (f32[5,128,128]{2,1,0:T(8,128)S(1)}, f32[5,128,128]{2,1,0:T(8,128)}, u32[]{:S(2)}) copy-start(f32[5,128,128]{2,1,0:T(8,128)} %tiles_ref.3) | copy-start | bytes 983044
  1.8 10.5 %copy-start.2 = (s32[2048]{0:T(1024)S(1)}, s32[2048]{0:T(1024)}, u32[]{:S(2)}) copy-start(s32[2048]{0:T(1024)} %first_ref.3) | copy-start | bytes 24580
  1.9 10.4 %collective-permute-start.2 = (f32[1536,128]{1,0:T(8,128)S(1)}, f32[1536,128]{1,0:T(8,128)S(1)}, u32[]{:S(2)}, u32[]{:S(2)}) collective-permute-start(f32[1536,128]{1,0:T(8,128)S(1)} %slice.6), channel_id=1, source_target_pairs={{0,1},{1,2},{2,3},{3,4},{4,5},{5,6},{6,7},{7,8},{8,9},{9,10},{10,1... | collective-permute-start | bytes 2359304 | tf_op jit(solution)/shard_map/ppermute | solution.py:651
  7.6 13.6 %collective-permute-start = (f32[32,2048]{1,0:T(8,128)}, f32[32,2048]{1,0:T(8,128)S(1)}, u32[]{:S(2)}, u32[]{:S(2)}) collective-permute-start(f32[32,2048]{1,0:T(8,128)} %get-tuple-element.30), channel_id=1, source_target_pairs={{0,120},{8,0},{16,8},{24,16},{32,24},{40,32},{48,40},{56,48},{64,5... | collective-permute-start | bytes 786440 | tf_op jit(solution)/shard_map/ppermute | solution.py:651
  12.3 10.4 %collective-permute-start.1 = (f32[32,2048]{1,0:T(8,128)}, f32[32,2048]{1,0:T(8,128)S(1)}, u32[]{:S(2)}, u32[]{:S(2)}) collective-permute-start(f32[32,2048]{1,0:T(8,128)} %get-tuple-element.31), channel_id=1, source_target_pairs={{0,8},{8,16},{16,24},{24,32},{32,40},{40,48},{48,56},{56,64},{64,7... | collective-permute-start | bytes 786440 | tf_op jit(solution)/shard_map/ppermute | solution.py:651
  16.2 8.4 %collective-permute-start.3 = (f32[272,128]{1,0:T(8,128)}, f32[272,128]{1,0:T(8,128)S(1)}, u32[]{:S(2)}, u32[]{:S(2)}) collective-permute-start(f32[272,128]{1,0:T(8,128)} %get-tuple-element.39), channel_id=1, source_target_pairs={{0,120},{8,0},{16,8},{24,16},{32,24},{40,32},{48,40},{56,48},{64,5... | collective-permute-start | bytes 417800 | tf_op jit(solution)/shard_map/ppermute | solution.py:651
  21.0 7.4 %collective-permute-start.4 = (f32[272,128]{1,0:T(8,128)}, f32[272,128]{1,0:T(8,128)S(1)}, u32[]{:S(2)}, u32[]{:S(2)}) collective-permute-start(f32[272,128]{1,0:T(8,128)} %get-tuple-element.40), channel_id=1, source_target_pairs={{0,8},{8,16},{16,24},{24,32},{32,40},{40,48},{48,56},{56,64},{64,7... | collective-permute-start | bytes 417800 | tf_op jit(solution)/shard_map/ppermute | solution.py:651
  28.7 11.8 %collective-permute-start.5 = (f32[488,128]{1,0:T(8,128)S(1)}, f32[488,128]{1,0:T(8,128)S(1)}, u32[]{:S(2)}, u32[]{:S(2)}) collective-permute-start(f32[488,128]{1,0:T(8,128)S(1)} %corners.1), channel_id=1, source_target_pairs={{0,1},{1,2},{2,3},{3,4},{4,5},{5,6},{6,7},{7,0},{8,9},{9,10},{10,1... | collective-permute-start | bytes 749576 | tf_op jit(solution)/shard_map/ppermute | solution.py:651
  37.0 6.9 %collective-permute-start.6 = (f32[488,128]{1,0:T(8,128)S(1)}, f32[488,128]{1,0:T(8,128)S(1)}, u32[]{:S(2)}, u32[]{:S(2)}) collective-permute-start(f32[488,128]{1,0:T(8,128)S(1)} %corners.1), channel_id=1, source_target_pairs={{0,7},{1,0},{2,1},{3,2},{4,3},{5,4},{6,5},{7,6},{8,15},{9,8},{10,9... | collective-permute-start | bytes 749576 | tf_op jit(solution)/shard_map/ppermute | solution.py:651
  70.2 13.6 %collective-permute-start.7 = (f32[1536,128]{1,0:T(8,128)S(1)}, f32[1536,128]{1,0:T(8,128)S(1)}, u32[]{:S(2)}, u32[]{:S(2)}) collective-permute-start(f32[1536,128]{1,0:T(8,128)S(1)} %get-tuple-element.51), channel_id=1, source_target_pairs={{0,127},{1,0},{2,1},{3,2},{4,3},{5,4},{6,5},{7,6},{8,7},{9,8},{10,... | collective-permute-start | bytes 2359304 | tf_op jit(solution)/shard_map/ppermute | solution.py:651
